TPU v7x, 32 devices: a whole 2x2x4 slice. The times are simulated.
32 devices in a mesh: row: 8 (over z, y), col: 4 (over x, core).
Axes of the slice: x: 2, y: 2, z: 4, core: 2. Of those that a mesh axis runs over, the one named last changes fastest.
Arguments:
- factor_band: float32 [1024, 131072], P('row', 'col'), may hold values from -0.015625 to 0.015625
- normals: float32 [131072, 96], P('col', 'row'), may hold values from -6 to 6
- site_mean: float32 [1024], P('row'), may hold values from 5 to 10
- site_spread: float32 [1024], P('row'), may hold values from 1 to 4
- site_capacity: float32 [1024], P('row'), may hold values from 0.1 to 1
- site_kind: int32 [1024], P('row'), may hold values 0 or 1
- site_plant: int32 [1024], P('row'), may hold values from 0 to 2047
Outputs:
- plant_output: float32 [96, 2048], P('col', 'row')
All inputs are finite; a program needn't handle non-finite values. No bound on the sum of `site_kind` on one device may be relied on, other than what follows from the above.
Results may differ from a plain program's by a relative error of at most 0.000096.
Values sent between devices are 32-bit elements; how exact they have to be, the bound alone decides.
No kernel may reach another device: no remote copies, remote signals or barrier semaphores. Data moves between devices by JAX's collectives and lax.ppermute only.
A program may use at most 128 MiB of HBM per device.

v0:
```python
import math

import jax
import jax.numpy as jnp
from jax import lax
from jax.experimental import pallas as pl
from jax.experimental.pallas import tpu as pltpu
from jax.sharding import PartitionSpec as P


PLANTS = 2048
LANE = 128


def split_bf16(x):
    hi = x.astype(jnp.bfloat16)
    return hi, (x - hi.astype(jnp.float32)).astype(jnp.bfloat16)


def dot_t(a, b):
    return lax.dot_general(a, b, (((1,), (1,)), ((), ())), preferred_element_type=jnp.float32)


def step_width(width):
    tiles = width // LANE
    return LANE * max(d for d in range(1, 29) if tiles % d == 0 and (d < tiles or tiles == 1))


def products(blocks, factor, offset, folds, rows):
    width = blocks[0].shape[1]
    band, cols = factor.shape
    stride = cols // folds
    tk = step_width(width)
    total = sum(b.shape[0] for b in blocks)
    groups = total // (folds * rows)
    steps = width // tk

    def kernel(*refs):
        block_refs, factor_refs = refs[: len(blocks)], refs[len(blocks) : len(blocks) + folds]
        out_ref, acc = refs[-2], refs[-1]
        step = pl.program_id(0)

        @pl.when(step == 0)
        def _():
            acc[...] = jnp.zeros_like(acc)

        hi, lo = split_bf16(jnp.concatenate([r[...] for r in block_refs], axis=0))
        both = jnp.concatenate([hi, lo], axis=0)
        for fold in range(folds):
            f_hi, f_lo = split_bf16(factor_refs[fold][...])
            first = dot_t(both, f_hi)
            acc[fold] += first[:total] + (first[total:] + dot_t(hi, f_lo))

        @pl.when(step == steps - 1)
        def _():
            for g in range(groups):
                base = g * folds * rows
                out_ref[g] = sum(acc[fold, base + fold * rows : base + (fold + 1) * rows] for fold in range(folds))

    def factor_spec(fold):
        start = fold * stride + offset
        return pl.BlockSpec((pl.Element(band), pl.Element(tk)), lambda i: (0, pl.multiple_of(start + i * tk, LANE)))

    return pl.pallas_call(
        kernel,
        grid=(steps,),
        in_specs=[pl.BlockSpec((b.shape[0], tk), lambda i: (0, i)) for b in blocks]
        + [factor_spec(fold) for fold in range(folds)],
        out_specs=pl.BlockSpec((groups, rows, band), lambda i: (0, 0, 0)),
        out_shape=jax.ShapeDtypeStruct((groups, rows, band), jnp.float32),
        scratch_shapes=[pltpu.VMEM((folds, total, band), jnp.float32)],
    )(*blocks, *([factor] * folds))


CHUNKS = 2


def arriving(t, planes):
    if t == 1:
        return [1]
    return sorted({t, planes - t} - {1}) if 2 * t >= planes else []


def plan(planes):
    chunks = [str(c) for c in range(CHUNKS)]
    last = planes - 1
    steps = [("b", "y", 0)]
    for c in chunks:
        steps += [(c, "e", 1), (c, "y", 0)] + [(c, "m", 1)] * (last > 1)
    steps += [("b", "e", 1)] + [("b", "m", 1)] * (last > 1)
    steps += [(c, "mul", (("slot", 0),)) for c in chunks]
    sent = [0]
    for t in range(1, planes):
        new = arriving(t, planes)
        if t == last:
            for j in range(2, planes):
                steps += [("b", "e", j)] + [("b", "m", j + 1)] * (j + 1 < last)
        for c in chunks:
            steps += [(c, "y", j) for j in new]
            if t < last:
                steps += [(c, "m", t + 1)] * (t + 1 < last) + [(c, "e", t + 1)]
            if t == 1 and c == chunks[0] and last > 2:
                steps += [("b", "m", 2)]
            if sent or new:
                steps += [(c, "mul", tuple([("y", j) for j in sent] + [("slot", j) for j in new]))]
        if t == 1:
            steps += [("b", "mul", (("slot", 0), ("slot", 1)))]
        sent = new
    for t in range(2, last):
        if arriving(t, planes):
            steps += [("b", "mul", tuple(("slot", j) for j in arriving(t, planes)))]
    steps += [(c, "mul", tuple(("y", j) for j in sent)) for c in chunks[:-1]]
    if last > 1:
        steps += [("b", "mul", (("slot", last),))]
    steps += [(c, "mul", tuple(("y", j) for j in sent)) for c in chunks[-1:]]
    return steps


def body(factor_band, normals, site_mean, site_spread, site_capacity, site_kind, site_plant):
    row_size, col_size = lax.axis_size("row"), lax.axis_size("col")
    row, col = lax.axis_index("row"), lax.axis_index("col")
    planes = row_size // 2
    z, y = row // 2, row % 2
    cols, rows = normals.shape
    band = factor_band.shape[0]
    folds = 8 // math.gcd(rows, 8)
    stride = cols // folds

    side = [(r, r ^ 1) for r in range(row_size)]

    def line(neighbour):
        return [(r, 2 * neighbour(r // 2) + r % 2) for r in range(row_size)]

    even = line(lambda p: p ^ 1)
    odd = line(lambda p: p if p in (0, planes - 1) else ((p - 1) ^ 1) + 1)
    send = lambda x, pairs: lax.ppermute(x, "row", pairs)
    heading = 1 - 2 * (z % 2)
    reach = jnp.where(heading == 1, planes - 1 - z, z)

    turned = normals.T
    tiles = stride // LANE
    first = max(1, round(tiles * 20 / 128))
    first += (tiles - first) % CHUNKS
    part = (tiles - first) // CHUNKS

    def piece(start, width):
        return jnp.concatenate(
            [turned[:, f * stride + start : f * stride + start + width] for f in range(folds)], axis=0
        )

    have, begin = {}, {"b": 0}
    small = piece(0, first * LANE)
    for c in range(CHUNKS):
        begin[str(c)] = (first + c * part) * LANE
        have[str(c), "slot", 0] = piece(begin[str(c)], part * LANE)

    def slot(stream, j):
        key = stream, "slot", j
        if key not in have:
            e = have[stream, "e", j]
            have[key] = e if j == 1 else jnp.where(j <= reach, e, have[stream, "m", planes - j])
        return have[key]

    parts = [[[], []] for _ in range(planes)]

    def multiply(stream, wanted):
        blocks, places = [], []
        for kind, j in wanted:
            blocks.append(slot(stream, j) if kind == "slot" else have[stream, kind, j])
            places += [(j, 0), (j, 1)] if stream == "b" else [(j, int(kind == "y"))]
        got = products(blocks, factor_band, begin[stream], folds, rows)
        for g, (j, q) in enumerate(places):
            parts[j][q].append(got[g])

    for step in plan(planes):
        stream, move, j = step
        if move == "mul":
            multiply(stream, j)
        elif step == ("b", "y", 0):
            have["b", "slot", 0] = jnp.concatenate([small, send(small, side)], axis=0)
        elif move == "y":
            have[stream, "y", j] = send(slot(stream, j), side)
        else:
            came = have[stream, "m" if move == "e" else "e", j - 1] if j > 1 else slot(stream, 0)
            have[step] = send(came, even if move == "e" else odd)

    sums = [[sum(terms) for terms in pair] for pair in parts]
    share = rows * row_size // col_size
    placed = []
    for plane in range(planes):
        at = jnp.mod(heading * (plane - z), planes)
        mine, other = sums[0]
        for j in range(1, planes):
            mine = jnp.where(at == j, sums[j][0], mine)
            other = jnp.where(at == j, sums[j][1], other)
        placed += [jnp.where(y == 0, mine, other), jnp.where(y == 0, other, mine)]
    total = jnp.concatenate(placed, axis=0).reshape(col_size, share, band)

    samples = lax.dynamic_index_in_dim(total, col, 0, keepdims=False)
    for k in range(1, col_size):
        pairs = [(c, c ^ k) for c in range(col_size)]
        samples = samples + lax.ppermute(lax.dynamic_index_in_dim(total, col ^ k, 0, keepdims=False), "col", pairs)

    speed = site_mean[None, :] + site_spread[None, :] * samples
    positive = jnp.maximum(speed, 0.0)
    wind = jnp.clip((positive * positive * positive - 27.0) / (1728.0 - 27.0), 0.0, 1.0)
    solar = jnp.clip(speed / 12.0, 0.0, 1.0)
    power = jnp.where(site_kind[None, :] == 1, solar, wind) * site_capacity[None, :]

    power = jnp.concatenate([power, site_plant[None, :].astype(jnp.float32)], axis=0)
    pair = jnp.concatenate([power, send(power, side)], axis=1)
    table = jnp.concatenate(
        [pair] + [send(pair, line(lambda p, k=k: p ^ k)) for k in range(1, planes)], axis=1
    )
    plant = table[share].astype(jnp.int32)
    mine = PLANTS // row_size
    onehot = (plant[:, None] == row * mine + jnp.arange(mine, dtype=jnp.int32)[None, :]).astype(jnp.float32)
    return jnp.dot(table[:share], onehot, precision=lax.Precision.HIGHEST, preferred_element_type=jnp.float32)


def solution(mesh):
    in_specs = (P("row", "col"), P("col", "row"), P("row"), P("row"), P("row"), P("row"), P("row"))
    out_specs = P("col", "row")
    return jax.shard_map(body, mesh=mesh, in_specs=in_specs, out_specs=out_specs, check_vma=False)
```

profile of v0, /device:TPU:0, one launch (start us, length us, event | category | flops | bytes accessed | tf_op | source)
XLA Modules:
  0.0 187.4 jit_solution(9423664964580140594)
XLA Ops:
  1.1 3.1 %collective-permute-start.12 = (f32[24,2560]{1,0:T(8,128)S(1)}, f32[24,2560]{1,0:T(8,128)S(1)}, u32[]{:S(2)}, u32[]{:S(2)}) collective-permute-start(f32[24,2560]{1,0:T(8,128)S(1)} %pad_maximum_fusion.3), channel_id=1, source_target_pairs={{0,4},{4,0},{8,12},{12,8},{16,20},{20,16},{24,28},{28,24},{1,5},{5... | collective-permute-start | bytes 737288 | tf_op jit(solution)/shard_map/ppermute | solution.py:136
  4.1 1.5 fusion.16
  5.8 2.1 %collective-permute-start.8 = (f32[24,6912]{1,0:T(8,128)S(1)}, f32[24,6912]{1,0:T(8,128)S(1)}, u32[]{:S(2)}, u32[]{:S(2)}) collective-permute-start(f32[24,6912]{1,0:T(8,128)S(1)} %pad_maximum_fusion.1.refs_0_), channel_id=1, source_target_pairs={{0,8},{4,12},{8,0},{12,4},{16,24},{20,28},{24,16},{28,20},{1,9},{5... | collective-permute-start | bytes 1990664 | tf_op jit(solution)/shard_map/ppermute | solution.py:136
  7.9 3.0 %collective-permute-done.12 = f32[24,2560]{1,0:T(8,128)S(1)} collective-permute-done((f32[24,2560]{1,0:T(8,128)S(1)}, f32[24,2560]{1,0:T(8,128)S(1)}, u32[]{:S(2)}, u32[]{:S(2)}) %collective-permute-start.12) | collective-permute-done | bytes 245792 | tf_op jit(solution)/shard_map/ppermute | solution.py:136
  11.0 1.5 collective-permute-start.16
  12.4 4.2 %collective-permute-start.13 = (f32[48,2560]{1,0:T(8,128)S(1)}, f32[48,2560]{1,0:T(8,128)}, u32[]{:S(2)}, u32[]{:S(2)}) collective-permute-start(f32[48,2560]{1,0:T(8,128)S(1)} %pad_maximum_fusion.2.refs_0_), channel_id=1, source_target_pairs={{0,8},{4,12},{8,0},{12,4},{16,24},{20,28},{24,16},{28,20},{1,9},{5... | collective-permute-start | bytes 1474568 | tf_op jit(solution)/shard_map/ppermute | solution.py:136
  17.5 1.5 collective-permute-start.20
  19.0 6.1 %collective-permute-done.21.refs_0_ = f32[24,6912]{1,0:T(8,128)S(1)} collective-permute-done((f32[24,6912]{1,0:T(8,128)S(1)}, f32[24,6912]{1,0:T(8,128)S(1)}, u32[]{:S(2)}, u32[]{:S(2)}) %collective-permute-start.21) | collective-permute-done | bytes 663584 | tf_op jit(solution)/shard_map/ppermute | solution.py:136
  25.1 2.1 %collective-permute-start.2 = (f32[24,6912]{1,0:T(8,128)}, f32[24,6912]{1,0:T(8,128)S(1)}, u32[]{:S(2)}, u32[]{:S(2)}) collective-permute-start(f32[24,6912]{1,0:T(8,128)} %pad_maximum_fusion.refs_0_), channel_id=1, source_target_pairs={{0,8},{4,12},{8,0},{12,4},{16,24},{20,28},{24,16},{28,20},{1,9},{5... | collective-permute-start | bytes 1990664 | tf_op jit(solution)/shard_map/ppermute | solution.py:136
  27.2 1.5 collective-permute-start.6
  28.8 3.6 %collective-permute-start.19 = (f32[48,2560]{1,0:T(8,128)}, f32[48,2560]{1,0:T(8,128)}, u32[]{:S(2)}, u32[]{:S(2)}) collective-permute-start(f32[48,2560]{1,0:T(8,128)} %collective-permute-done.16), channel_id=1, source_target_pairs={{0,8},{4,12},{8,0},{12,4},{16,24},{20,28},{24,16},{28,20},{1,9},{5... | collective-permute-start | bytes 1474568 | tf_op jit(solution)/shard_map/ppermute | solution.py:136
  32.4 1.9 %collective-permute-done.13.refs_1_ = f32[48,2560]{1,0:T(8,128)} collective-permute-done((f32[48,2560]{1,0:T(8,128)S(1)}, f32[48,2560]{1,0:T(8,128)}, u32[]{:S(2)}, u32[]{:S(2)}) %collective-permute-start.13) | collective-permute-done | bytes 491552 | tf_op jit(solution)/shard_map/ppermute | solution.py:136
  34.3 5.3 %collective-permute-start.14 = (f32[48,2560]{1,0:T(8,128)}, f32[48,2560]{1,0:T(8,128)}, u32[]{:S(2)}, u32[]{:S(2)}) collective-permute-start(f32[48,2560]{1,0:T(8,128)} %collective-permute-done.13.refs_1_), channel_id=1, source_target_pairs={{0,0},{4,4},{8,16},{12,20},{16,8},{20,12},{24,24},{28,28},{1,1},{5... | collective-permute-start | bytes 1474568 | tf_op jit(solution)/shard_map/ppermute | solution.py:136
  39.6 5.4 %shard_map.82 = f32[1,12,128]{2,1,0:T(8,128)} custom-call(f32[24,6912]{1,0:T(8,128)} %pad_maximum_fusion.refs_0_, f32[128,32768]{1,0:T(8,128)} %refs_2_.25, f32[128,32768]{1,0:T(8,128)} %refs_2_.25), custom_call_target="tpu_custom_call" | custom-call | tf_op jit(solution)/shard_map/pallas_call | solution.py:64
  45.0 5.4 %shard_map.83 = f32[1,12,128]{2,1,0:T(8,128)} custom-call(f32[24,6912]{1,0:T(8,128)} %copy-done.4, f32[128,32768]{1,0:T(8,128)} %refs_2_.25, f32[128,32768]{1,0:T(8,128)} %refs_2_.25), custom_call_target="tpu_custom_call" | custom-call | tf_op jit(solution)/shard_map/pallas_call | solution.py:64
  50.4 5.6 %shard_map.80 = f32[2,12,128]{2,1,0:T(8,128)} custom-call(f32[24,6912]{1,0:T(8,128)} %copy-done.10, f32[24,6912]{1,0:T(8,128)} %copy-done.6, f32[128,32768]{1,0:T(8,128)} %refs_2_.25, f32[128,32768]{1,0:T(8,128)} %refs_2_.25), custom_call_target="tpu_custom_call" | custom-call | tf_op jit(solution)/shard_map/pallas_call | solution.py:64
  56.0 1.7 collective-permute-start
  57.7 2.0 %collective-permute-start.18 = (f32[24,6912]{1,0:T(8,128)S(1)}, f32[24,6912]{1,0:T(8,128)S(1)}, u32[]{:S(2)}, u32[]{:S(2)}) collective-permute-start(f32[24,6912]{1,0:T(8,128)S(1)} %copy-done.7), channel_id=1, source_target_pairs={{0,4},{4,0},{8,12},{12,8},{16,20},{20,16},{24,28},{28,24},{1,5},{5... | collective-permute-start | bytes 1990664 | tf_op jit(solution)/shard_map/ppermute | solution.py:136
  59.7 5.5 %shard_map.79 = f32[2,12,128]{2,1,0:T(8,128)} custom-call(f32[24,6912]{1,0:T(8,128)} %collective-permute-done.20.refs_0_, f32[24,6912]{1,0:T(8,128)} %copy-done.8, f32[128,32768]{1,0:T(8,128)} %refs_2_.25, f32[128,32768]{1,0:T(8,128)} %refs_2_.25), custom_call_target="tpu_custom_call" | custom-call | tf_op jit(solution)/shard_map/pallas_call | solution.py:64
  65.2 3.5 %shard_map.81 = f32[4,12,128]{2,1,0:T(8,128)} custom-call(f32[48,2560]{1,0:T(8,128)} %copy-done.5, f32[48,2560]{1,0:T(8,128)} %collective-permute-done.13.refs_1_, f32[128,32768]{1,0:T(8,128)} %refs_2_.25, f32[128,32768]{1,0:T(8,128)} %refs_2_.25), custom_call_target="tpu_custom_call" | custom-call | tf_op jit(solution)/shard_map/pallas_call | solution.py:64
  70.3 3.4 %collective-permute-start.7 = (f32[24,6912]{1,0:T(8,128)}, f32[24,6912]{1,0:T(8,128)}, u32[]{:S(2)}, u32[]{:S(2)}) collective-permute-start(f32[24,6912]{1,0:T(8,128)} %collective-permute-done.6), channel_id=1, source_target_pairs={{0,8},{4,12},{8,0},{12,4},{16,24},{20,28},{24,16},{28,20},{1,9},{5... | collective-permute-start | bytes 1990664 | tf_op jit(solution)/shard_map/ppermute | solution.py:136
  73.7 1.9 broadcast_select_fusion.4.refs_0_
  75.5 3.1 %shard_map.78 = f32[2,12,128]{2,1,0:T(8,128)} custom-call(f32[48,2560]{1,0:T(8,128)} %broadcast_select_fusion.4.refs_0_, f32[128,32768]{1,0:T(8,128)} %refs_2_.25, f32[128,32768]{1,0:T(8,128)} %refs_2_.25), custom_call_target="tpu_custom_call" | custom-call | tf_op jit(solution)/shard_map/pallas_call | solution.py:64
  79.6 9.4 %collective-permute-start.1 = (f32[24,6912]{1,0:T(8,128)S(1)}, f32[24,6912]{1,0:T(8,128)S(1)}, u32[]{:S(2)}, u32[]{:S(2)}) collective-permute-start(f32[24,6912]{1,0:T(8,128)S(1)} %collective-permute-done), channel_id=1, source_target_pairs={{0,8},{4,12},{8,0},{12,4},{16,24},{20,28},{24,16},{28,20},{1,9},{5... | collective-permute-start | bytes 1990664 | tf_op jit(solution)/shard_map/ppermute | solution.py:136
  89.8 1.2 broadcast_select_fusion.2.refs_1_
  92.0 12.7 %collective-permute-done.1 = f32[24,6912]{1,0:T(8,128)S(1)} collective-permute-done((f32[24,6912]{1,0:T(8,128)S(1)}, f32[24,6912]{1,0:T(8,128)S(1)}, u32[]{:S(2)}, u32[]{:S(2)}) %collective-permute-start.1) | collective-permute-done | bytes 663584 | tf_op jit(solution)/shard_map/ppermute | solution.py:136
  104.7 2.0 %collective-permute-start.11 = (f32[24,6912]{1,0:T(8,128)}, f32[24,6912]{1,0:T(8,128)}, u32[]{:S(2)}, u32[]{:S(2)}) collective-permute-start(f32[24,6912]{1,0:T(8,128)} %copy-done.14), channel_id=1, source_target_pairs={{0,8},{4,12},{8,0},{12,4},{16,24},{20,28},{24,16},{28,20},{1,9},{5... | collective-permute-start | bytes 1990664 | tf_op jit(solution)/shard_map/ppermute | solution.py:136
  107.9 5.6 %shard_map.77 = f32[2,12,128]{2,1,0:T(8,128)} custom-call(f32[24,6912]{1,0:T(8,128)} %copy-done.11, f32[24,6912]{1,0:T(8,128)} %copy-done, f32[128,32768]{1,0:T(8,128)} %refs_2_.25, f32[128,32768]{1,0:T(8,128)} %refs_2_.25), custom_call_target="tpu_custom_call" | custom-call | tf_op jit(solution)/shard_map/pallas_call | solution.py:64
  113.6 5.5 %shard_map.76 = f32[2,12,128]{2,1,0:T(8,128)} custom-call(f32[24,6912]{1,0:T(8,128)} %collective-permute-done.17.refs_0_, f32[24,6912]{1,0:T(8,128)} %copy-done.1, f32[128,32768]{1,0:T(8,128)} %refs_2_.25, f32[128,32768]{1,0:T(8,128)} %refs_2_.25), custom_call_target="tpu_custom_call" | custom-call | tf_op jit(solution)/shard_map/pallas_call | solution.py:64
  119.2 10.4 %collective-permute-done.11 = f32[24,6912]{1,0:T(8,128)} collective-permute-done((f32[24,6912]{1,0:T(8,128)}, f32[24,6912]{1,0:T(8,128)}, u32[]{:S(2)}, u32[]{:S(2)}) %collective-permute-start.11) | collective-permute-done | bytes 663584 | tf_op jit(solution)/shard_map/ppermute | solution.py:136
  129.6 1.2 broadcast_select_fusion.refs_1_
  131.8 6.1 %collective-permute-done.5 = f32[24,6912]{1,0:T(8,128)} collective-permute-done((f32[24,6912]{1,0:T(8,128)S(1)}, f32[24,6912]{1,0:T(8,128)}, u32[]{:S(2)}, u32[]{:S(2)}) %collective-permute-start.5) | collective-permute-done | bytes 663584 | tf_op jit(solution)/shard_map/ppermute | solution.py:136
  137.9 1.2 broadcast_select_fusion.1.refs_1_
  139.1 1.5 collective-permute-start.22
  140.6 1.9 %broadcast_select_fusion.5.refs_0_ = f32[48,2560]{1,0:T(8,128)} fusion(f32[48,2560]{1,0:T(8,128)} %collective-permute-done.15, f32[48,2560]{1,0:T(8,128)} %collective-permute-done.16, pred[]{:T(512)S(6)} %ge.5), kind=kLoop, calls=%fused_computation.13 | loop fusion | flops 122880 | bytes 1474561 | tf_op jit(solution)/shard_map/jit(_where)/select_n | solution.py:161
  142.5 3.1 %shard_map.75 = f32[2,12,128]{2,1,0:T(8,128)} custom-call(f32[48,2560]{1,0:T(8,128)} %broadcast_select_fusion.5.refs_0_, f32[128,32768]{1,0:T(8,128)} %refs_2_.25, f32[128,32768]{1,0:T(8,128)} %refs_2_.25), custom_call_target="tpu_custom_call" | custom-call | tf_op jit(solution)/shard_map/pallas_call | solution.py:64
  145.7 5.5 %shard_map.74 = f32[2,12,128]{2,1,0:T(8,128)} custom-call(f32[24,6912]{1,0:T(8,128)} %collective-permute-done.10.refs_0_, f32[24,6912]{1,0:T(8,128)} %copy-done.2, f32[128,32768]{1,0:T(8,128)} %refs_2_.25, f32[128,32768]{1,0:T(8,128)} %refs_2_.25), custom_call_target="tpu_custom_call" | custom-call | tf_op jit(solution)/shard_map/pallas_call | solution.py:64
  151.2 5.5 %shard_map.73 = f32[2,12,128]{2,1,0:T(8,128)} custom-call(f32[24,6912]{1,0:T(8,128)} %collective-permute-done.4.refs_0_, f32[24,6912]{1,0:T(8,128)} %copy-done.3, f32[128,32768]{1,0:T(8,128)} %refs_2_.25, f32[128,32768]{1,0:T(8,128)} %refs_2_.25), custom_call_target="tpu_custom_call" | custom-call | tf_op jit(solution)/shard_map/pallas_call | solution.py:64
  156.7 5.4 %shard_map.85 = f32[1,12,128]{2,1,0:T(8,128)} custom-call(f32[24,6912]{1,0:T(8,128)} %collective-permute-done.23.refs_0_, f32[128,32768]{1,0:T(8,128)} %refs_2_.25, f32[128,32768]{1,0:T(8,128)} %refs_2_.25), custom_call_target="tpu_custom_call" | custom-call | tf_op jit(solution)/shard_map/pallas_call | solution.py:64
  163.1 5.4 %shard_map.84 = f32[1,12,128]{2,1,0:T(8,128)} custom-call(f32[24,6912]{1,0:T(8,128)} %copy-done.17, f32[128,32768]{1,0:T(8,128)} %refs_2_.25, f32[128,32768]{1,0:T(8,128)} %refs_2_.25), custom_call_target="tpu_custom_call" | custom-call | tf_op jit(solution)/shard_map/pallas_call | solution.py:64
  170.0 1.6 collective-permute-start.26
  172.1 1.0 collective-permute-done.26
  173.1 2.1 %collective-permute-done.25 = f32[24,128]{1,0:T(8,128)S(1)} collective-permute-done((f32[24,128]{1,0:T(8,128)S(1)}, f32[24,128]{1,0:T(8,128)S(1)}, u32[]{:S(2)}, u32[]{:S(2)}) %collective-permute-start.25) | collective-permute-done | bytes 12320 | tf_op jit(solution)/shard_map/ppermute | solution.py:202
  175.9 3.2 %collective-permute-done.27 = f32[25,128]{1,0:T(8,128)S(1)} collective-permute-done((f32[25,128]{1,0:T(8,128)S(1)}, f32[25,128]{1,0:T(8,128)S(1)}, u32[]{:S(2)}, u32[]{:S(2)}) %collective-permute-start.27) | collective-permute-done | bytes 12832 | tf_op jit(solution)/shard_map/ppermute | solution.py:136
  179.1 2.3 %collective-permute-start.30 = (f32[25,256]{1,0:T(8,128)S(1)}, f32[25,256]{1,0:T(8,128)S(1)}, u32[]{:S(2)}, u32[]{:S(2)}) collective-permute-start(f32[25,256]{1,0:T(8,128)S(1)} %pad_maximum_fusion.4), channel_id=1, source_target_pairs={{0,24},{4,28},{8,16},{12,20},{16,8},{20,12},{24,0},{28,4},{1,25},{... | collective-permute-start | bytes 76808 | tf_op jit(solution)/shard_map/ppermute | solution.py:136
  181.4 2.1 %collective-permute-start.28 = (f32[25,256]{1,0:T(8,128)S(1)}, f32[25,256]{1,0:T(8,128)S(1)}, u32[]{:S(2)}, u32[]{:S(2)}) collective-permute-start(f32[25,256]{1,0:T(8,128)S(1)} %pad_maximum_fusion.4), channel_id=1, source_target_pairs={{0,8},{4,12},{8,0},{12,4},{16,24},{20,28},{24,16},{28,20},{1,9},{5... | collective-permute-start | bytes 76808 | tf_op jit(solution)/shard_map/ppermute | solution.py:136
  183.5 1.9 %collective-permute-done.28 = f32[25,256]{1,0:T(8,128)S(1)} collective-permute-done((f32[25,256]{1,0:T(8,128)S(1)}, f32[25,256]{1,0:T(8,128)S(1)}, u32[]{:S(2)}, u32[]{:S(2)}) %collective-permute-start.28) | collective-permute-done | bytes 25632 | tf_op jit(solution)/shard_map/ppermute | solution.py:136
  186.3 1.1 fusion
  (127 shorter events, 13.0 us)
Async XLA Ops:
  1.1 9.9 %collective-permute-start.12 = (f32[24,2560]{1,0:T(8,128)S(1)}, f32[24,2560]{1,0:T(8,128)S(1)}, u32[]{:S(2)}, u32[]{:S(2)}) collective-permute-start(f32[24,2560]{1,0:T(8,128)S(1)} %pad_maximum_fusion.3), channel_id=1, source_target_pairs={{0,4},{4,0},{8,12},{12,8},{16,20},{20,16},{24,28},{28,24},{1,5},{5... | collective-permute-start | bytes 737288 | tf_op jit(solution)/shard_map/ppermute | solution.py:136
  5.7 39.2 %copy-start.4 = (f32[24,6912]{1,0:T(8,128)}, f32[24,6912]{1,0:T(8,128)S(1)}, u32[]{:S(2)}) copy-start(f32[24,6912]{1,0:T(8,128)S(1)} %pad_maximum_fusion.1.refs_0_) | copy-start | bytes 1990660
  5.7 19.4 %collective-permute-start.21 = (f32[24,6912]{1,0:T(8,128)S(1)}, f32[24,6912]{1,0:T(8,128)S(1)}, u32[]{:S(2)}, u32[]{:S(2)}) collective-permute-start(f32[24,6912]{1,0:T(8,128)S(1)} %pad_maximum_fusion.1.refs_0_), channel_id=1, source_target_pairs={{0,4},{4,0},{8,12},{12,8},{16,20},{20,16},{24,28},{28,24},{1,5},{5... | collective-permute-start | bytes 1990664 | tf_op jit(solution)/shard_map/ppermute | solution.py:136
  5.8 21.4 %collective-permute-start.8 = (f32[24,6912]{1,0:T(8,128)S(1)}, f32[24,6912]{1,0:T(8,128)S(1)}, u32[]{:S(2)}, u32[]{:S(2)}) collective-permute-start(f32[24,6912]{1,0:T(8,128)S(1)} %pad_maximum_fusion.1.refs_0_), channel_id=1, source_target_pairs={{0,8},{4,12},{8,0},{12,4},{16,24},{20,28},{24,16},{28,20},{1,9},{5... | collective-permute-start | bytes 1990664 | tf_op jit(solution)/shard_map/ppermute | solution.py:136
  11.0 34.0 %copy-start.5 = (f32[48,2560]{1,0:T(8,128)}, f32[48,2560]{1,0:T(8,128)S(1)}, u32[]{:S(2)}) copy-start(f32[48,2560]{1,0:T(8,128)S(1)} %pad_maximum_fusion.2.refs_0_) | copy-start | bytes 1474564
  11.0 17.8 %collective-permute-start.16 = (f32[48,2560]{1,0:T(8,128)S(1)}, f32[48,2560]{1,0:T(8,128)}, u32[]{:S(2)}, u32[]{:S(2)}) collective-permute-start(f32[48,2560]{1,0:T(8,128)S(1)} %pad_maximum_fusion.2.refs_0_), channel_id=1, source_target_pairs={{0,0},{4,4},{8,16},{12,20},{16,8},{20,12},{24,24},{28,28},{1,1},{5... | collective-permute-start | bytes 1474568 | tf_op jit(solution)/shard_map/ppermute | solution.py:136
  12.4 21.8 %collective-permute-start.13 = (f32[48,2560]{1,0:T(8,128)S(1)}, f32[48,2560]{1,0:T(8,128)}, u32[]{:S(2)}, u32[]{:S(2)}) collective-permute-start(f32[48,2560]{1,0:T(8,128)S(1)} %pad_maximum_fusion.2.refs_0_), channel_id=1, source_target_pairs={{0,8},{4,12},{8,0},{12,4},{16,24},{20,28},{24,16},{28,20},{1,9},{5... | collective-permute-start | bytes 1474568 | tf_op jit(solution)/shard_map/ppermute | solution.py:136
  17.5 38.5 %collective-permute-start.20 = (f32[24,6912]{1,0:T(8,128)}, f32[24,6912]{1,0:T(8,128)}, u32[]{:S(2)}, u32[]{:S(2)}) collective-permute-start(f32[24,6912]{1,0:T(8,128)} %pad_maximum_fusion.refs_0_), channel_id=1, source_target_pairs={{0,4},{4,0},{8,12},{12,8},{16,20},{20,16},{24,28},{28,24},{1,5},{5... | collective-permute-start | bytes 1990664 | tf_op jit(solution)/shard_map/ppermute | solution.py:136
  25.1 19.8 %copy-start.10 = (f32[24,6912]{1,0:T(8,128)}, f32[24,6912]{1,0:T(8,128)S(1)}, u32[]{:S(2)}) copy-start(f32[24,6912]{1,0:T(8,128)S(1)} %collective-permute-done.21.refs_0_) | copy-start | bytes 1990660
  25.1 32.6 %collective-permute-start.2 = (f32[24,6912]{1,0:T(8,128)}, f32[24,6912]{1,0:T(8,128)S(1)}, u32[]{:S(2)}, u32[]{:S(2)}) collective-permute-start(f32[24,6912]{1,0:T(8,128)} %pad_maximum_fusion.refs_0_), channel_id=1, source_target_pairs={{0,8},{4,12},{8,0},{12,4},{16,24},{20,28},{24,16},{28,20},{1,9},{5... | collective-permute-start | bytes 1990664 | tf_op jit(solution)/shard_map/ppermute | solution.py:136
  27.2 17.7 %copy-start.6 = (f32[24,6912]{1,0:T(8,128)}, f32[24,6912]{1,0:T(8,128)S(1)}, u32[]{:S(2)}) copy-start(f32[24,6912]{1,0:T(8,128)S(1)} %collective-permute-done.8.refs_1_) | copy-start | bytes 1990660
  27.2 41.5 %collective-permute-start.6 = (f32[24,6912]{1,0:T(8,128)S(1)}, f32[24,6912]{1,0:T(8,128)}, u32[]{:S(2)}, u32[]{:S(2)}) collective-permute-start(f32[24,6912]{1,0:T(8,128)S(1)} %pad_maximum_fusion.1.refs_0_), channel_id=1, source_target_pairs={{0,0},{4,4},{8,16},{12,20},{16,8},{20,12},{24,24},{28,28},{1,1},{5... | collective-permute-start | bytes 1990664 | tf_op jit(solution)/shard_map/ppermute | solution.py:136
  28.8 40.7 %collective-permute-start.19 = (f32[48,2560]{1,0:T(8,128)}, f32[48,2560]{1,0:T(8,128)}, u32[]{:S(2)}, u32[]{:S(2)}) collective-permute-start(f32[48,2560]{1,0:T(8,128)} %collective-permute-done.16), channel_id=1, source_target_pairs={{0,8},{4,12},{8,0},{12,4},{16,24},{20,28},{24,16},{28,20},{1,9},{5... | collective-permute-start | bytes 1474568 | tf_op jit(solution)/shard_map/ppermute | solution.py:136
  34.3 36.0 %collective-permute-start.14 = (f32[48,2560]{1,0:T(8,128)}, f32[48,2560]{1,0:T(8,128)}, u32[]{:S(2)}, u32[]{:S(2)}) collective-permute-start(f32[48,2560]{1,0:T(8,128)} %collective-permute-done.13.refs_1_), channel_id=1, source_target_pairs={{0,0},{4,4},{8,16},{12,20},{16,8},{20,12},{24,24},{28,28},{1,1},{5... | collective-permute-start | bytes 1474568 | tf_op jit(solution)/shard_map/ppermute | solution.py:136
  50.4 7.3 %copy-start.7 = (f32[24,6912]{1,0:T(8,128)S(1)}, f32[24,6912]{1,0:T(8,128)}, u32[]{:S(2)}) copy-start(f32[24,6912]{1,0:T(8,128)} %copy-done.6) | copy-start | bytes 1990660
  56.0 22.7 %collective-permute-start = (f32[24,6912]{1,0:T(8,128)}, f32[24,6912]{1,0:T(8,128)S(1)}, u32[]{:S(2)}, u32[]{:S(2)}) collective-permute-start(f32[24,6912]{1,0:T(8,128)} %pad_maximum_fusion.refs_0_), channel_id=1, source_target_pairs={{0,0},{4,4},{8,16},{12,20},{16,8},{20,12},{24,24},{28,28},{1,1},{5... | collective-permute-start | bytes 1990664 | tf_op jit(solution)/shard_map/ppermute | solution.py:136
  57.7 49.2 %collective-permute-start.18 = (f32[24,6912]{1,0:T(8,128)S(1)}, f32[24,6912]{1,0:T(8,128)S(1)}, u32[]{:S(2)}, u32[]{:S(2)}) collective-permute-start(f32[24,6912]{1,0:T(8,128)S(1)} %copy-done.7), channel_id=1, source_target_pairs={{0,4},{4,0},{8,12},{12,8},{16,20},{20,16},{24,28},{28,24},{1,5},{5... | collective-permute-start | bytes 1990664 | tf_op jit(solution)/shard_map/ppermute | solution.py:136
  68.7 10.8 %collective-permute-start.9 = (f32[24,6912]{1,0:T(8,128)S(1)}, f32[24,6912]{1,0:T(8,128)S(1)}, u32[]{:S(2)}, u32[]{:S(2)}) collective-permute-start(f32[24,6912]{1,0:T(8,128)S(1)} %copy-done.7), channel_id=1, source_target_pairs={{0,0},{4,4},{8,16},{12,20},{16,8},{20,12},{24,24},{28,28},{1,1},{5... | collective-permute-start | bytes 1990664 | tf_op jit(solution)/shard_map/ppermute | solution.py:136
  69.4 44.1 %collective-permute-start.17 = (f32[24,6912]{1,0:T(8,128)S(1)}, f32[24,6912]{1,0:T(8,128)}, u32[]{:S(2)}, u32[]{:S(2)}) collective-permute-start(f32[24,6912]{1,0:T(8,128)S(1)} %copy-done.9), channel_id=1, source_target_pairs={{0,4},{4,0},{8,12},{12,8},{16,20},{20,16},{24,28},{28,24},{1,5},{5... | collective-permute-start | bytes 1990664 | tf_op jit(solution)/shard_map/ppermute | solution.py:136
  70.3 18.7 %collective-permute-start.7 = (f32[24,6912]{1,0:T(8,128)}, f32[24,6912]{1,0:T(8,128)}, u32[]{:S(2)}, u32[]{:S(2)}) collective-permute-start(f32[24,6912]{1,0:T(8,128)} %collective-permute-done.6), channel_id=1, source_target_pairs={{0,8},{4,12},{8,0},{12,4},{16,24},{20,28},{24,16},{28,20},{1,9},{5... | collective-permute-start | bytes 1990664 | tf_op jit(solution)/shard_map/ppermute | solution.py:136
  78.7 26.1 %copy-start.12 = (f32[24,6912]{1,0:T(8,128)}, f32[24,6912]{1,0:T(8,128)S(1)}, u32[]{:S(2)}) copy-start(f32[24,6912]{1,0:T(8,128)S(1)} %collective-permute-done) | copy-start | bytes 1990660
  78.7 12.4 %collective-permute-start.3 = (f32[24,6912]{1,0:T(8,128)S(1)}, f32[24,6912]{1,0:T(8,128)S(1)}, u32[]{:S(2)}, u32[]{:S(2)}) collective-permute-start(f32[24,6912]{1,0:T(8,128)S(1)} %copy-done.9), channel_id=1, source_target_pairs={{0,0},{4,4},{8,16},{12,20},{16,8},{20,12},{24,24},{28,28},{1,1},{5... | collective-permute-start | bytes 1990664 | tf_op jit(solution)/shard_map/ppermute | solution.py:136
  79.6 9.4 %copy-start.14 = (f32[24,6912]{1,0:T(8,128)}, f32[24,6912]{1,0:T(8,128)S(1)}, u32[]{:S(2)}) copy-start(f32[24,6912]{1,0:T(8,128)S(1)} %collective-permute-done.9) | copy-start | bytes 1990660
  79.6 25.2 %collective-permute-start.1 = (f32[24,6912]{1,0:T(8,128)S(1)}, f32[24,6912]{1,0:T(8,128)S(1)}, u32[]{:S(2)}, u32[]{:S(2)}) collective-permute-start(f32[24,6912]{1,0:T(8,128)S(1)} %collective-permute-done), channel_id=1, source_target_pairs={{0,8},{4,12},{8,0},{12,4},{16,24},{20,28},{24,16},{28,20},{1,9},{5... | collective-permute-start | bytes 1990664 | tf_op jit(solution)/shard_map/ppermute | solution.py:136
  89.0 51.6 %collective-permute-start.15 = (f32[48,2560]{1,0:T(8,128)}, f32[48,2560]{1,0:T(8,128)}, u32[]{:S(2)}, u32[]{:S(2)}) collective-permute-start(f32[48,2560]{1,0:T(8,128)} %collective-permute-done.14), channel_id=1, source_target_pairs={{0,8},{4,12},{8,0},{12,4},{16,24},{20,28},{24,16},{28,20},{1,9},{5... | collective-permute-start | bytes 1474568 | tf_op jit(solution)/shard_map/ppermute | solution.py:136
  91.0 16.9 %copy-start = (f32[24,6912]{1,0:T(8,128)}, f32[24,6912]{1,0:T(8,128)S(1)}, u32[]{:S(2)}) copy-start(f32[24,6912]{1,0:T(8,128)S(1)} %broadcast_select_fusion.2.refs_1_) | copy-start | bytes 1990660
  91.0 15.9 %copy-start.15 = (f32[24,6912]{1,0:T(8,128)}, f32[24,6912]{1,0:T(8,128)S(1)}, u32[]{:S(2)}) copy-start(f32[24,6912]{1,0:T(8,128)S(1)} %collective-permute-done.3) | copy-start | bytes 1990660
  91.0 54.6 %collective-permute-start.10 = (f32[24,6912]{1,0:T(8,128)S(1)}, f32[24,6912]{1,0:T(8,128)}, u32[]{:S(2)}, u32[]{:S(2)}) collective-permute-start(f32[24,6912]{1,0:T(8,128)S(1)} %broadcast_select_fusion.2.refs_1_), channel_id=1, source_target_pairs={{0,4},{4,0},{8,12},{12,8},{16,20},{20,16},{24,28},{28,24},{1,5},{5... | collective-permute-start | bytes 1990664 | tf_op jit(solution)/shard_map/ppermute | solution.py:136
  104.7 24.9 %collective-permute-start.11 = (f32[24,6912]{1,0:T(8,128)}, f32[24,6912]{1,0:T(8,128)}, u32[]{:S(2)}, u32[]{:S(2)}) collective-permute-start(f32[24,6912]{1,0:T(8,128)} %copy-done.14), channel_id=1, source_target_pairs={{0,8},{4,12},{8,0},{12,4},{16,24},{20,28},{24,16},{28,20},{1,9},{5... | collective-permute-start | bytes 1990664 | tf_op jit(solution)/shard_map/ppermute | solution.py:136
  106.9 6.6 %copy-start.1 = (f32[24,6912]{1,0:T(8,128)}, f32[24,6912]{1,0:T(8,128)S(1)}, u32[]{:S(2)}) copy-start(f32[24,6912]{1,0:T(8,128)S(1)} %broadcast_select_fusion.3.refs_1_) | copy-start | bytes 1990660
  106.9 44.3 %collective-permute-start.4 = (f32[24,6912]{1,0:T(8,128)S(1)}, f32[24,6912]{1,0:T(8,128)}, u32[]{:S(2)}, u32[]{:S(2)}) collective-permute-start(f32[24,6912]{1,0:T(8,128)S(1)} %broadcast_select_fusion.3.refs_1_), channel_id=1, source_target_pairs={{0,4},{4,0},{8,12},{12,8},{16,20},{20,16},{24,28},{28,24},{1,5},{5... | collective-permute-start | bytes 1990664 | tf_op jit(solution)/shard_map/ppermute | solution.py:136
  113.5 24.3 %collective-permute-start.5 = (f32[24,6912]{1,0:T(8,128)S(1)}, f32[24,6912]{1,0:T(8,128)}, u32[]{:S(2)}, u32[]{:S(2)}) collective-permute-start(f32[24,6912]{1,0:T(8,128)S(1)} %copy-done.16), channel_id=1, source_target_pairs={{0,8},{4,12},{8,0},{12,4},{16,24},{20,28},{24,16},{28,20},{1,9},{5... | collective-permute-start | bytes 1990664 | tf_op jit(solution)/shard_map/ppermute | solution.py:136
  119.2 18.7 %copy-start.13 = (f32[24,6912]{1,0:T(8,128)S(1)}, f32[24,6912]{1,0:T(8,128)}, u32[]{:S(2)}) copy-start(f32[24,6912]{1,0:T(8,128)} %copy-done.12) | copy-start | bytes 1990660
  130.8 14.9 %copy-start.2 = (f32[24,6912]{1,0:T(8,128)}, f32[24,6912]{1,0:T(8,128)S(1)}, u32[]{:S(2)}) copy-start(f32[24,6912]{1,0:T(8,128)S(1)} %broadcast_select_fusion.refs_1_) | copy-start | bytes 1990660
  130.8 26.0 %collective-permute-start.23 = (f32[24,6912]{1,0:T(8,128)S(1)}, f32[24,6912]{1,0:T(8,128)}, u32[]{:S(2)}, u32[]{:S(2)}) collective-permute-start(f32[24,6912]{1,0:T(8,128)S(1)} %broadcast_select_fusion.refs_1_), channel_id=1, source_target_pairs={{0,4},{4,0},{8,12},{12,8},{16,20},{20,16},{24,28},{28,24},{1,5},{5... | collective-permute-start | bytes 1990664 | tf_op jit(solution)/shard_map/ppermute | solution.py:136
  139.1 6.6 %copy-start.3 = (f32[24,6912]{1,0:T(8,128)}, f32[24,6912]{1,0:T(8,128)S(1)}, u32[]{:S(2)}) copy-start(f32[24,6912]{1,0:T(8,128)S(1)} %broadcast_select_fusion.1.refs_1_) | copy-start | bytes 1990660
  139.1 23.2 %collective-permute-start.22 = (f32[24,6912]{1,0:T(8,128)S(1)}, f32[24,6912]{1,0:T(8,128)S(1)}, u32[]{:S(2)}, u32[]{:S(2)}) collective-permute-start(f32[24,6912]{1,0:T(8,128)S(1)} %broadcast_select_fusion.1.refs_1_), channel_id=1, source_target_pairs={{0,4},{4,0},{8,12},{12,8},{16,20},{20,16},{24,28},{28,24},{1,5},{5... | collective-permute-start | bytes 1990664 | tf_op jit(solution)/shard_map/ppermute | solution.py:136
  162.2 9.9 %copy-start.34 = (s32[128]{0:T(128)S(1)}, s32[128]{0:T(128)}, u32[]{:S(2)}) copy-start(s32[128]{0:T(128)} %param.12) | copy-start | bytes 1540
  162.2 13.0 %copy-start.30 = (f32[128]{0:T(128)S(1)}, f32[128]{0:T(128)}, u32[]{:S(2)}) copy-start(f32[128]{0:T(128)} %param.11) | copy-start | bytes 1540
  162.2 13.0 %copy-start.31 = (f32[128]{0:T(128)S(1)}, f32[128]{0:T(128)}, u32[]{:S(2)}) copy-start(f32[128]{0:T(128)} %param.10) | copy-start | bytes 1540
  162.2 13.0 %copy-start.32 = (f32[128]{0:T(128)S(1)}, f32[128]{0:T(128)}, u32[]{:S(2)}) copy-start(f32[128]{0:T(128)} %param.9) | copy-start | bytes 1540
  169.9 2.2 %collective-permute-start.24 = (f32[24,128]{1,0:T(8,128)S(1)}, f32[24,128]{1,0:T(8,128)S(1)}, u32[]{:S(2)}, u32[]{:S(2)}) collective-permute-start(f32[24,128]{1,0:T(8,128)S(1)} %get-tuple-element.37), channel_id=1, source_target_pairs={{0,1},{1,0},{2,3},{3,2},{4,5},{5,4},{6,7},{7,6},{8,9},{9,8},{10,11... | collective-permute-start | bytes 36872 | tf_op jit(solution)/shard_map/ppermute | solution.py:202
  170.0 3.2 %collective-permute-start.26 = (f32[24,128]{1,0:T(8,128)S(1)}, f32[24,128]{1,0:T(8,128)S(1)}, u32[]{:S(2)}, u32[]{:S(2)}) collective-permute-start(f32[24,128]{1,0:T(8,128)S(1)} %get-tuple-element.38), channel_id=1, source_target_pairs={{0,3},{1,2},{2,1},{3,0},{4,7},{5,6},{6,5},{7,4},{8,11},{9,10},{10,... | collective-permute-start | bytes 36872 | tf_op jit(solution)/shard_map/ppermute | solution.py:202
  171.6 3.7 %collective-permute-start.25 = (f32[24,128]{1,0:T(8,128)S(1)}, f32[24,128]{1,0:T(8,128)S(1)}, u32[]{:S(2)}, u32[]{:S(2)}) collective-permute-start(f32[24,128]{1,0:T(8,128)S(1)} %get-tuple-element.39), channel_id=1, source_target_pairs={{0,2},{1,3},{2,0},{3,1},{4,6},{5,7},{6,4},{7,5},{8,10},{9,11},{10,... | collective-permute-start | bytes 36872 | tf_op jit(solution)/shard_map/ppermute | solution.py:202
  175.3 3.8 %collective-permute-start.27 = (f32[25,128]{1,0:T(8,128)S(1)}, f32[25,128]{1,0:T(8,128)S(1)}, u32[]{:S(2)}, u32[]{:S(2)}) collective-permute-start(f32[25,128]{1,0:T(8,128)S(1)} %get-tuple-element.40), channel_id=1, source_target_pairs={{0,4},{4,0},{8,12},{12,8},{16,20},{20,16},{24,28},{28,24},{1,5},{5... | collective-permute-start | bytes 38408 | tf_op jit(solution)/shard_map/ppermute | solution.py:136
  179.1 7.1 %collective-permute-start.30 = (f32[25,256]{1,0:T(8,128)S(1)}, f32[25,256]{1,0:T(8,128)S(1)}, u32[]{:S(2)}, u32[]{:S(2)}) collective-permute-start(f32[25,256]{1,0:T(8,128)S(1)} %pad_maximum_fusion.4), channel_id=1, source_target_pairs={{0,24},{4,28},{8,16},{12,20},{16,8},{20,12},{24,0},{28,4},{1,25},{... | collective-permute-start | bytes 76808 | tf_op jit(solution)/shard_map/ppermute | solution.py:136
  181.4 4.8 %collective-permute-start.29 = (f32[25,256]{1,0:T(8,128)S(1)}, f32[25,256]{1,0:T(8,128)S(1)}, u32[]{:S(2)}, u32[]{:S(2)}) collective-permute-start(f32[25,256]{1,0:T(8,128)S(1)} %pad_maximum_fusion.4), channel_id=1, source_target_pairs={{0,16},{4,20},{8,24},{12,28},{16,0},{20,4},{24,8},{28,12},{1,17},{... | collective-permute-start | bytes 76808 | tf_op jit(solution)/shard_map/ppermute | solution.py:136
  181.4 4.0 %collective-permute-start.28 = (f32[25,256]{1,0:T(8,128)S(1)}, f32[25,256]{1,0:T(8,128)S(1)}, u32[]{:S(2)}, u32[]{:S(2)}) collective-permute-start(f32[25,256]{1,0:T(8,128)S(1)} %pad_maximum_fusion.4), channel_id=1, source_target_pairs={{0,8},{4,12},{8,0},{12,4},{16,24},{20,28},{24,16},{28,20},{1,9},{5... | collective-permute-start | bytes 76808 | tf_op jit(solution)/shard_map/ppermute | solution.py:136
  (18 other events, 95.9 us)
where the time goes:
time: 188 us; the launch traced here: 187 us
  Pallas kernels  64.5 us (34%)
  starting transfers between devices  58.5 us (31%)
  waiting for transfers between devices  49.4 us (26%)
  other arithmetic  9.25 us (5%)
  local copies, waits for them, and re-layouts  4.05 us (2%)
    pallas_call x13, Pallas kernels, products(): pl.pallas_call(kernel, grid=(steps,), in_specs=[pl.BlockSpec((b.shape[0],...  64.5 us
    ppermute x28, starting transfers between devices, body(): send = lambda x, pairs: lax.ppermute(x, 'row', pairs)  56.3 us
    ppermute x28, waiting for transfers between devices, body(): send = lambda x, pairs: lax.ppermute(x, 'row', pairs)  46.3 us
    select_n x6, other arithmetic, slot(): jnp.where(j <= reach, e, have[stream, 'm', planes - j])  7.42 us
  transfers between devices with their start and end apart: 31, of which 11 were waited for; matrix products, arithmetic and copies ran while one was open for 5% of the time, Pallas kernels for 32%

commit v1 on v0

--- a/solution.py
+++ b/solution.py
@@ -26,10 +26,10 @@
     return LANE * max(d for d in range(1, 29) if tiles % d == 0 and (d < tiles or tiles == 1))
 
 
-def products(blocks, factor, offset, folds, rows):
+def products(blocks, factors, starts, rows):
+    folds = len(factors)
     width = blocks[0].shape[1]
-    band, cols = factor.shape
-    stride = cols // folds
+    band = factors[0].shape[0]
     tk = step_width(width)
     total = sum(b.shape[0] for b in blocks)
     groups = total // (folds * rows)
@@ -58,7 +58,7 @@
                 out_ref[g] = sum(acc[fold, base + fold * rows : base + (fold + 1) * rows] for fold in range(folds))
 
     def factor_spec(fold):
-        start = fold * stride + offset
+        start = starts[fold]
         return pl.BlockSpec((pl.Element(band), pl.Element(tk)), lambda i: (0, pl.multiple_of(start + i * tk, LANE)))
 
     return pl.pallas_call(
@@ -69,10 +69,34 @@
         out_specs=pl.BlockSpec((groups, rows, band), lambda i: (0, 0, 0)),
         out_shape=jax.ShapeDtypeStruct((groups, rows, band), jnp.float32),
         scratch_shapes=[pltpu.VMEM((folds, total, band), jnp.float32)],
-    )(*blocks, *([factor] * folds))
+    )(*blocks, *factors)
 
 
 CHUNKS = 2
+
+
+def choose(flag, a, b):
+    def kernel(flag_ref, a_ref, b_ref, out_ref, sem):
+        @pl.when(flag_ref[0] == 1)
+        def _():
+            copy = pltpu.make_async_copy(a_ref, out_ref, sem)
+            copy.start()
+            copy.wait()
+
+        @pl.when(flag_ref[0] != 1)
+        def _():
+            copy = pltpu.make_async_copy(b_ref, out_ref, sem)
+            copy.start()
+            copy.wait()
+
+    anywhere = pl.BlockSpec(memory_space=pl.ANY)
+    return pl.pallas_call(
+        kernel,
+        in_specs=[pl.BlockSpec(memory_space=pltpu.SMEM), anywhere, anywhere],
+        out_specs=anywhere,
+        out_shape=jax.ShapeDtypeStruct(a.shape, a.dtype),
+        scratch_shapes=[pltpu.SemaphoreType.DMA],
+    )(flag.astype(jnp.int32).reshape(1), a, b)
 
 
 def arriving(t, planes):
@@ -81,37 +105,61 @@
     return sorted({t, planes - t} - {1}) if 2 * t >= planes else []
 
 
+def exports(planes):
+    return planes == 4
+
+
 def plan(planes):
+    slots = lambda *js: tuple(("slot", j) for j in js)
+    if exports(planes):
+        return (
+            [("b", "y", 0), ("0", "e", 1), ("0", "m", 1), ("x", "y", 0), ("1", "e", 1), ("0", "y", 0), ("1", "m", 1)]
+            + [("1", "y", 0), ("b", "e", 1), ("x", "e", 1), ("x", "f", 0), ("x", "f", 1)]
+            + [("0", "mul", slots(0))]
+            + [("0", "y", 1), ("0", "m", 2), ("0", "e", 2), ("1", "mul", slots(0))]
+            + [("1", "y", 1), ("1", "m", 2), ("1", "e", 2), ("b", "m", 1), ("x", "m", 1)]
+            + [("0", "mul", (("y", 0), ("slot", 1))), ("b", "m", 2), ("1", "mul", (("y", 0), ("slot", 1)))]
+            + [("0", "sel", 2), ("0", "y", 2), ("0", "e", 3), ("x", "m", 2), ("b", "mul", slots(0, 1))]
+            + [("1", "sel", 2), ("1", "y", 2), ("1", "e", 3), ("b", "e", 2)]
+            + [("0", "mul", (("y", 1), ("slot", 2)))]
+            + [("0", "sel", 3), ("0", "y", 3), ("1", "mul", (("y", 1), ("slot", 2)))]
+            + [("1", "sel", 3), ("1", "y", 3), ("b", "e", 3)]
+            + [("0", "mul", (("y", 2), ("slot", 3))), ("1", "mul", (("y", 2), ("slot", 3)))]
+            + [("x", "mul", "own"), ("x", "mul", "far"), ("x", "back", 0)]
+            + [("b", "sel", 2), ("b", "mul", slots(2)), ("0", "mul", (("y", 3),))]
+            + [("b", "sel", 3), ("b", "mul", slots(3)), ("1", "mul", (("y", 3),))]
+        )
     chunks = [str(c) for c in range(CHUNKS)]
     last = planes - 1
     steps = [("b", "y", 0)]
     for c in chunks:
         steps += [(c, "e", 1), (c, "y", 0)] + [(c, "m", 1)] * (last > 1)
     steps += [("b", "e", 1)] + [("b", "m", 1)] * (last > 1)
-    steps += [(c, "mul", (("slot", 0),)) for c in chunks]
+    steps += [(c, "mul", slots(0)) for c in chunks]
     sent = [0]
     for t in range(1, planes):
         new = arriving(t, planes)
         if t == last:
             for j in range(2, planes):
-                steps += [("b", "e", j)] + [("b", "m", j + 1)] * (j + 1 < last)
+                steps += [("b", "e", j)] + [("b", "m", j + 1)] * (1 < j < last - 1)
         for c in chunks:
-            steps += [(c, "y", j) for j in new]
+            for j in new:
+                steps += [(c, "sel", j)] * (j > 1) + [(c, "y", j)]
             if t < last:
                 steps += [(c, "m", t + 1)] * (t + 1 < last) + [(c, "e", t + 1)]
-            if t == 1 and c == chunks[0] and last > 2:
+            if t == 1 and c == chunks[-1] and last > 2:
                 steps += [("b", "m", 2)]
             if sent or new:
-                steps += [(c, "mul", tuple([("y", j) for j in sent] + [("slot", j) for j in new]))]
+                steps += [(c, "mul", tuple(("y", j) for j in sent) + slots(*new))]
         if t == 1:
-            steps += [("b", "mul", (("slot", 0), ("slot", 1)))]
+            steps += [("b", "mul", slots(0, 1))]
         sent = new
     for t in range(2, last):
         if arriving(t, planes):
-            steps += [("b", "mul", tuple(("slot", j) for j in arriving(t, planes)))]
+            steps += [("b", "sel", j) for j in arriving(t, planes)] + [("b", "mul", slots(*arriving(t, planes)))]
     steps += [(c, "mul", tuple(("y", j) for j in sent)) for c in chunks[:-1]]
     if last > 1:
-        steps += [("b", "mul", (("slot", last),))]
+        steps += [("b", "sel", last), ("b", "mul", slots(last))]
     steps += [(c, "mul", tuple(("y", j) for j in sent)) for c in chunks[-1:]]
     return steps
 
@@ -137,64 +185,101 @@
     heading = 1 - 2 * (z % 2)
     reach = jnp.where(heading == 1, planes - 1 - z, z)
 
+    outer = (z == 0) | (z == planes - 1)
+
+    def between(pairs, take):
+        return [(a, b) for a, b in pairs if take(a // 2 in (0, planes - 1))]
+
+    inward = between(even, lambda is_outer: is_outer)
+    outward = between(even, lambda is_outer: not is_outer)
+
     turned = normals.T
     tiles = stride // LANE
-    first = max(1, round(tiles * 20 / 128))
-    first += (tiles - first) % CHUNKS
-    part = (tiles - first) // CHUNKS
-
-    def piece(start, width):
+    pairs_of = lambda share: 2 * round(tiles * share / 2)
+    sizes = {"x": pairs_of(18 / 128), "b": pairs_of(22 / 128)} if exports(planes) else {"b": pairs_of(20 / 128)}
+    rest = tiles - sum(sizes.values())
+    sizes["1"] = 2 * (rest * 5 // 22)
+    sizes["0"] = rest - sizes["1"]
+    begin, at = {}, 0
+    for stream in sizes:
+        begin[stream], at = at * LANE, at + sizes[stream]
+
+    def piece(stream):
+        start, width = begin[stream], sizes[stream] * LANE
         return jnp.concatenate(
             [turned[:, f * stride + start : f * stride + start + width] for f in range(folds)], axis=0
         )
 
-    have, begin = {}, {"b": 0}
-    small = piece(0, first * LANE)
-    for c in range(CHUNKS):
-        begin[str(c)] = (first + c * part) * LANE
-        have[str(c), "slot", 0] = piece(begin[str(c)], part * LANE)
-
-    def slot(stream, j):
-        key = stream, "slot", j
-        if key not in have:
-            e = have[stream, "e", j]
-            have[key] = e if j == 1 else jnp.where(j <= reach, e, have[stream, "m", planes - j])
-        return have[key]
-
+    own = {stream: piece(stream) for stream in ("b", "0", "x", "1") if stream in sizes}
+    have = {(stream, "slot", 0): own[stream] for stream in ("0", "1")}
     parts = [[[], []] for _ in range(planes)]
+    far = [[None, None] for _ in range(planes)]
+
+    def starts_of(stream):
+        return [f * stride + begin[stream] for f in range(folds)]
 
     def multiply(stream, wanted):
         blocks, places = [], []
         for kind, j in wanted:
-            blocks.append(slot(stream, j) if kind == "slot" else have[stream, kind, j])
+            blocks.append(have[stream, kind, j])
             places += [(j, 0), (j, 1)] if stream == "b" else [(j, int(kind == "y"))]
-        got = products(blocks, factor_band, begin[stream], folds, rows)
+        got = products(blocks, [factor_band] * folds, starts_of(stream), rows)
         for g, (j, q) in enumerate(places):
             parts[j][q].append(got[g])
+
+    def multiply_exported(whose):
+        blocks = [have["x", "slot", 0], have["x", "e", 1], have["x", "m", 1], have["x", "m", 2]]
+        places = [(j % planes, q) for j in (0, 1, -1, -2) for q in (0, 1)]
+        if whose == "own":
+            got = products(blocks, [factor_band] * folds, starts_of("x"), rows)
+            for g, (j, q) in enumerate(places):
+                parts[j][q].append(jnp.where(outer, 0.0, got[g]))
+        else:
+            got = products(blocks, [have["x", "f", f] for f in range(folds)], [0] * folds, rows)
+            for g, (j, q) in enumerate(places):
+                far[j][q] = got[g]
+
+    def place(sums):
+        placed = []
+        for plane in range(planes):
+            at = jnp.mod(heading * (plane - z), planes)
+            mine, other = sums[0]
+            for j in range(1, planes):
+                mine = jnp.where(at == j, sums[j][0], mine)
+                other = jnp.where(at == j, sums[j][1], other)
+            placed += [jnp.where(y == 0, mine, other), jnp.where(y == 0, other, mine)]
+        return jnp.concatenate(placed, axis=0)
 
     for step in plan(planes):
         stream, move, j = step
         if move == "mul":
-            multiply(stream, j)
-        elif step == ("b", "y", 0):
-            have["b", "slot", 0] = jnp.concatenate([small, send(small, side)], axis=0)
+            multiply_exported(j) if stream == "x" else multiply(stream, j)
+        elif move == "back":
+            back = send(place(far), outward)
+        elif move == "f":
+            if j < folds:
+                start = starts_of("x")[j]
+                have[step] = send(factor_band[:, start : start + sizes["x"] * LANE], inward)
+        elif move == "sel":
+            have[stream, "slot", j] = choose(j <= reach, have[stream, "e", j], have[stream, "m", planes - j])
+        elif move == "y" and stream in ("b", "x"):
+            have[stream, "slot", 0] = jnp.concatenate([own[stream], send(own[stream], side)], axis=0)
         elif move == "y":
-            have[stream, "y", j] = send(slot(stream, j), side)
+            have[step] = send(have[stream, "slot", j], side)
         else:
-            came = have[stream, "m" if move == "e" else "e", j - 1] if j > 1 else slot(stream, 0)
-            have[step] = send(came, even if move == "e" else odd)
-
-    sums = [[sum(terms) for terms in pair] for pair in parts]
+            came = have[stream, "m" if move == "e" else "e", j - 1] if j > 1 else have[stream, "slot", 0]
+            pairs = odd if move == "m" else inward if stream == "x" else even
+            if exports(planes) and move == "e" and j > 1:
+                pairs = outward
+            have[step] = send(came, pairs)
+            if move == "e" and j == 1:
+                have[stream, "slot", 1] = have[step]
+
+    total = place([[sum(terms) for terms in pair] for pair in parts])
+    if exports(planes):
+        total = total + jnp.where(outer, back, 0.0)
     share = rows * row_size // col_size
-    placed = []
-    for plane in range(planes):
-        at = jnp.mod(heading * (plane - z), planes)
-        mine, other = sums[0]
-        for j in range(1, planes):
-            mine = jnp.where(at == j, sums[j][0], mine)
-            other = jnp.where(at == j, sums[j][1], other)
-        placed += [jnp.where(y == 0, mine, other), jnp.where(y == 0, other, mine)]
-    total = jnp.concatenate(placed, axis=0).reshape(col_size, share, band)
+    total = total.reshape(col_size, share, band)
 
     samples = lax.dynamic_index_in_dim(total, col, 0, keepdims=False)
     for k in range(1, col_size):

time: 188 us -> 298 us (1.59)
  Pallas kernels: 64.5 us -> 171 us
  starting transfers between devices: 58.5 us -> 73.1 us
  waiting for transfers between devices: 49.4 us -> 39.1 us
  other arithmetic: 9.25 us -> 3.64 us
  local copies, waits for them, and re-layouts: 4.05 us -> 8.12 us
    pallas_call x0 -> x6, Pallas kernels: none -> 105 us  [choose(): pl.pallas_call(kernel, in_specs=[pl.BlockSpec(memory_space=pltpu.SMEM), a...]
    ppermute x28 -> x35, starting transfers between devices: 56.3 us -> 70.9 us  [body(): send = lambda x, pairs: lax.ppermute(x, 'row', pairs)]
    ppermute x28 -> x35, waiting for transfers between devices: 46.3 us -> 35.9 us  [body(): send = lambda x, pairs: lax.ppermute(x, 'row', pairs)]
    select_n x10, other arithmetic: 8.17 us -> 3.31 us  [place(): placed += [jnp.where(y == 0, mine, other), jnp.where(y == 0, other, mine)]]
    slice x0 -> x1, local copies, waits for them, and re-layouts: none -> 3.19 us  [body(): have[step] = send(factor_band[:, start:start + sizes['x'] * LANE], inward)]
    pallas_call x13 -> x15, Pallas kernels: 64.5 us -> 66.1 us  [products(): pl.pallas_call(kernel, grid=(steps,), in_specs=[pl.BlockSpec((b.shape[0],...]
  transfers between devices with their start and end apart: 31 -> 38, of which waited for: 11 -> 10; matrix products, arithmetic and copies ran while one was open for 5% -> 3% of each run, Pallas kernels for 32% -> 58%
where the time goes in v1:
time: 298 us; the launch traced here: 297 us
  Pallas kernels  171 us (57%)
  starting transfers between devices  73.1 us (25%)
  waiting for transfers between devices  39.1 us (13%)
  local copies, waits for them, and re-layouts  8.12 us (3%)
  other arithmetic  3.64 us (1%)
    pallas_call x6, Pallas kernels, choose(): pl.pallas_call(kernel, in_specs=[pl.BlockSpec(memory_space=pltpu.SMEM), a...  105 us
    ppermute x35, starting transfers between devices, body(): send = lambda x, pairs: lax.ppermute(x, 'row', pairs)  70.9 us
    pallas_call x15, Pallas kernels, products(): pl.pallas_call(kernel, grid=(steps,), in_specs=[pl.BlockSpec((b.shape[0],...  66.1 us
    ppermute x35, waiting for transfers between devices, body(): send = lambda x, pairs: lax.ppermute(x, 'row', pairs)  35.9 us
  transfers between devices with their start and end apart: 38, of which 10 were waited for; matrix products, arithmetic and copies ran while one was open for 3% of the time, Pallas kernels for 58%

profile of v1, /device:TPU:0, one launch (start us, length us, event | category | flops | bytes accessed | tf_op | source)
XLA Modules:
  0.0 297.0 jit_solution(13298292573726387876)
XLA Ops:
  1.4 3.1 %collective-permute-start.25 = (f32[24,5120]{1,0:T(8,128)S(1)}, f32[24,5120]{1,0:T(8,128)S(1)}, u32[]{:S(2)}, u32[]{:S(2)}) collective-permute-start(f32[24,5120]{1,0:T(8,128)S(1)} %pad_maximum_fusion.2.refs_0_), channel_id=1, source_target_pairs={{0,4},{4,0},{8,12},{12,8},{16,20},{20,16},{24,28},{28,24},{1,5},{5... | collective-permute-start | bytes 1474568 | tf_op jit(solution)/shard_map/ppermute | solution.py:184
  4.4 1.6 collective-permute-start.8
  7.4 1.6 collective-permute-start.16
  9.1 12.1 %collective-permute-done.12 = f32[24,2304]{1,0:T(8,128)S(1)} collective-permute-done((f32[24,2304]{1,0:T(8,128)S(1)}, f32[24,2304]{1,0:T(8,128)S(1)}, u32[]{:S(2)}, u32[]{:S(2)}) %collective-permute-start.12) | collective-permute-done | bytes 221216 | tf_op jit(solution)/shard_map/ppermute | solution.py:184
  21.2 2.0 collective-permute-start.24
  23.2 3.8 %collective-permute-done.16 = f32[24,2816]{1,0:T(8,128)S(1)} collective-permute-done((f32[24,2816]{1,0:T(8,128)S(1)}, f32[24,2816]{1,0:T(8,128)S(1)}, u32[]{:S(2)}, u32[]{:S(2)}) %collective-permute-start.16) | collective-permute-done | bytes 270368 | tf_op jit(solution)/shard_map/ppermute | solution.py:184
  27.0 2.1 collective-permute-start.2
  30.7 7.5 %collective-permute-start.13 = (f32[48,2304]{1,0:T(8,128)S(1)}, f32[48,2304]{1,0:T(8,128)S(1)}, u32[]{:S(2)}, u32[]{:S(2)}) collective-permute-start(f32[48,2304]{1,0:T(8,128)S(1)} %pad_maximum_fusion.3.refs_0_), channel_id=1, source_target_pairs={{0,8},{4,12},{24,16},{28,20},{1,9},{5,13},{25,17},{29,21},{2,10},{... | collective-permute-start | bytes 1327112 | tf_op jit(solution)/shard_map/ppermute | solution.py:184
  38.8 1.8 collective-permute-start.17
  40.6 2.2 collective-permute-done.2.refs_1_
  42.8 1.5 collective-permute-start.22
  44.3 3.2 %fusion.28 = (f32[128,2304]{1,0:T(8,128)}, f32[128,2304]{1,0:T(8,128)}) fusion(f32[128,32768]{1,0:T(8,128)} %refs_2_.25), kind=kLoop, calls=%fused_computation.100 | loop fusion | bytes 4718592 | tf_op jit(solution)/shard_map/slice | solution.py:262
  47.6 5.5 %collective-permute-start.29 = (f32[128,2304]{1,0:T(8,128)}, f32[128,2304]{1,0:T(8,128)}, u32[]{:S(2)}, u32[]{:S(2)}) collective-permute-start(f32[128,2304]{1,0:T(8,128)} %get-tuple-element.37), channel_id=1, source_target_pairs={{0,8},{4,12},{24,16},{28,20},{1,9},{5,13},{25,17},{29,21},{2,10},{... | collective-permute-start | bytes 3538952 | tf_op jit(solution)/shard_map/ppermute | solution.py:184
  53.1 4.7 %collective-permute-start.28 = (f32[128,2304]{1,0:T(8,128)}, f32[128,2304]{1,0:T(8,128)}, u32[]{:S(2)}, u32[]{:S(2)}) collective-permute-start(f32[128,2304]{1,0:T(8,128)} %get-tuple-element.38), channel_id=1, source_target_pairs={{0,8},{4,12},{24,16},{28,20},{1,9},{5,13},{25,17},{29,21},{2,10},{... | collective-permute-start | bytes 3538952 | tf_op jit(solution)/shard_map/ppermute | solution.py:184
  59.2 4.7 %collective-permute-done.17.refs_1_ = f32[48,2816]{1,0:T(8,128)S(1)} collective-permute-done((f32[48,2816]{1,0:T(8,128)S(1)}, f32[48,2816]{1,0:T(8,128)S(1)}, u32[]{:S(2)}, u32[]{:S(2)}) %collective-permute-start.17) | collective-permute-done | bytes 540704 | tf_op jit(solution)/shard_map/ppermute | solution.py:184
  65.9 6.0 %collective-permute-start.3 = (f32[24,6144]{1,0:T(8,128)}, f32[24,6144]{1,0:T(8,128)}, u32[]{:S(2)}, u32[]{:S(2)}) collective-permute-start(f32[24,6144]{1,0:T(8,128)} %collective-permute-done.2.refs_1_), channel_id=1, source_target_pairs={{0,0},{4,4},{8,16},{12,20},{16,8},{20,12},{24,24},{28,28},{1,1},{5... | collective-permute-start | bytes 1769480 | tf_op jit(solution)/shard_map/ppermute | solution.py:184
  71.8 5.4 %collective-permute-done.7.a_ref = f32[24,5120]{1,0:T(8,128)S(1)} collective-permute-done((f32[24,5120]{1,0:T(8,128)S(1)}, f32[24,5120]{1,0:T(8,128)S(1)}, u32[]{:S(2)}, u32[]{:S(2)}) %collective-permute-start.7) | collective-permute-done | bytes 491552 | tf_op jit(solution)/shard_map/ppermute | solution.py:184
  78.6 1.5 collective-permute-start.20
  80.2 4.4 %shard_map.90 = f32[1,12,128]{2,1,0:T(8,128)} custom-call(f32[24,5120]{1,0:T(8,128)} %copy-done.4, f32[128,32768]{1,0:T(8,128)} %refs_2_.25, f32[128,32768]{1,0:T(8,128)} %refs_2_.25), custom_call_target="tpu_custom_call" | custom-call | tf_op jit(solution)/shard_map/pallas_call | solution.py:64
  84.7 4.9 %shard_map.89 = f32[1,12,128]{2,1,0:T(8,128)} custom-call(f32[24,6144]{1,0:T(8,128)} %copy-done.1, f32[128,32768]{1,0:T(8,128)} %refs_2_.25, f32[128,32768]{1,0:T(8,128)} %refs_2_.25), custom_call_target="tpu_custom_call" | custom-call | tf_op jit(solution)/shard_map/pallas_call | solution.py:64
  89.6 4.6 %shard_map.87 = f32[2,12,128]{2,1,0:T(8,128)} custom-call(f32[24,5120]{1,0:T(8,128)} %copy-done.21, f32[24,5120]{1,0:T(8,128)} %copy-done.22, f32[128,32768]{1,0:T(8,128)} %refs_2_.25, f32[128,32768]{1,0:T(8,128)} %refs_2_.25), custom_call_target="tpu_custom_call" | custom-call | tf_op jit(solution)/shard_map/pallas_call | solution.py:64
  94.2 5.1 %shard_map.86 = f32[2,12,128]{2,1,0:T(8,128)} custom-call(f32[24,6144]{1,0:T(8,128)} %copy-done.12, f32[24,6144]{1,0:T(8,128)} %collective-permute-done.2.refs_1_, f32[128,32768]{1,0:T(8,128)} %refs_2_.25, f32[128,32768]{1,0:T(8,128)} %refs_2_.25), custom_call_target="tpu_custom_call" | custom-call | tf_op jit(solution)/shard_map/pallas_call | solution.py:64
  99.2 3.5 %shard_map.88 = f32[4,12,128]{2,1,0:T(8,128)} custom-call(f32[48,2816]{1,0:T(8,128)} %copy-done.2, f32[48,2816]{1,0:T(8,128)} %copy-done.17, f32[128,32768]{1,0:T(8,128)} %refs_2_.25, f32[128,32768]{1,0:T(8,128)} %refs_2_.25), custom_call_target="tpu_custom_call" | custom-call | tf_op jit(solution)/shard_map/pallas_call | solution.py:64
  102.8 16.0 %shard_map.76.refs_1_ = f32[24,5120]{1,0:T(8,128)} custom-call(s32[1]{0:T(128)} %bitcast.flag_ref, f32[24,5120]{1,0:T(8,128)} %copy-done.20, f32[24,5120]{1,0:T(8,128)} %collective-permute-done.9.b_ref), custom_call_target="tpu_custom_call" | custom-call | tf_op jit(solution)/shard_map/pallas_call | solution.py:93
  118.8 4.6 %shard_map.83 = f32[2,12,128]{2,1,0:T(8,128)} custom-call(f32[24,5120]{1,0:T(8,128)} %copy-done.23, f32[24,5120]{1,0:T(8,128)} %shard_map.76.refs_1_, f32[128,32768]{1,0:T(8,128)} %refs_2_.25, f32[128,32768]{1,0:T(8,128)} %refs_2_.25), custom_call_target="tpu_custom_call" | custom-call | tf_op jit(solution)/shard_map/pallas_call | solution.py:64
  123.4 4.1 %shard_map.79 = f32[8,12,128]{2,1,0:T(8,128)} custom-call(f32[48,2304]{1,0:T(8,128)} %copy-done, f32[48,2304]{1,0:T(8,128)} %copy-done.7, f32[48,2304]{1,0:T(8,128)} %copy-done.6, f32[48,2304]{1,0:T(8,128)} %copy-done.8, f32[128,32768]{1,0:T(8,128)} %refs_2_.25, f32[128,32768]{1,0:T(8,128)} %refs_2_.25), custom_call_target="tpu_custom_call" | custom-call | tf_op jit(solution)/shard_map/pallas_call | solution.py:64
  127.5 1.6 collective-permute-start.21
  131.9 4.1 %shard_map.93 = f32[8,12,128]{2,1,0:T(8,128)} custom-call(f32[48,2304]{1,0:T(8,128)} %copy-done, f32[48,2304]{1,0:T(8,128)} %copy-done.7, f32[48,2304]{1,0:T(8,128)} %copy-done.6, f32[48,2304]{1,0:T(8,128)} %copy-done.8, f32[128,2304]{1,0:T(8,128)} %collective-permute-done.28.refs_4_, f32[128,2304]{1,0:T(8,128)} %collective-permute-done.29.refs_5_), custom_call_target="tpu_custom_call" | custom-call | tf_op jit(solution)/shard_map/pallas_call | solution.py:64
  139.4 19.0 %shard_map.73.refs_1_ = f32[24,6144]{1,0:T(8,128)} custom-call(s32[1]{0:T(128)} %bitcast.flag_ref, f32[24,6144]{1,0:T(8,128)} %collective-permute-done.1.a_ref, f32[24,6144]{1,0:T(8,128)} %collective-permute-done.3.b_ref), custom_call_target="tpu_custom_call" | custom-call | tf_op jit(solution)/shard_map/pallas_call | solution.py:93
  160.7 16.0 %shard_map.77.refs_1_ = f32[24,5120]{1,0:T(8,128)} custom-call(s32[1]{0:T(128)} %bitcast.2.flag_ref, f32[24,5120]{1,0:T(8,128)} %collective-permute-done.11.a_ref, f32[24,5120]{1,0:T(8,128)} %copy-done.19), custom_call_target="tpu_custom_call" | custom-call | tf_op jit(solution)/shard_map/pallas_call | solution.py:93
  176.7 1.6 collective-permute-start.4
  179.7 19.0 %shard_map.74.refs_1_ = f32[24,6144]{1,0:T(8,128)} custom-call(s32[1]{0:T(128)} %bitcast.2.flag_ref, f32[24,6144]{1,0:T(8,128)} %copy-done.11, f32[24,6144]{1,0:T(8,128)} %copy-done.10), custom_call_target="tpu_custom_call" | custom-call | tf_op jit(solution)/shard_map/pallas_call | solution.py:93
  199.3 1.5 collective-permute-start.26
  201.4 5.1 %shard_map.82 = f32[2,12,128]{2,1,0:T(8,128)} custom-call(f32[24,6144]{1,0:T(8,128)} %copy-done.13, f32[24,6144]{1,0:T(8,128)} %shard_map.73.refs_1_, f32[128,32768]{1,0:T(8,128)} %refs_2_.25, f32[128,32768]{1,0:T(8,128)} %refs_2_.25), custom_call_target="tpu_custom_call" | custom-call | tf_op jit(solution)/shard_map/pallas_call | solution.py:64
  206.4 17.5 %shard_map.84.refs_0_ = f32[48,2816]{1,0:T(8,128)} custom-call(s32[1]{0:T(128)} %bitcast.flag_ref, f32[48,2816]{1,0:T(8,128)} %collective-permute-done.23.a_ref, f32[48,2816]{1,0:T(8,128)} %collective-permute-done.18.b_ref), custom_call_target="tpu_custom_call" | custom-call | tf_op jit(solution)/shard_map/pallas_call | solution.py:93
  223.9 3.4 %shard_map.85 = f32[2,12,128]{2,1,0:T(8,128)} custom-call(f32[48,2816]{1,0:T(8,128)} %shard_map.84.refs_0_, f32[128,32768]{1,0:T(8,128)} %refs_2_.25, f32[128,32768]{1,0:T(8,128)} %refs_2_.25), custom_call_target="tpu_custom_call" | custom-call | tf_op jit(solution)/shard_map/pallas_call | solution.py:64
  228.6 4.6 %shard_map.78 = f32[2,12,128]{2,1,0:T(8,128)} custom-call(f32[24,5120]{1,0:T(8,128)} %copy-done.24, f32[24,5120]{1,0:T(8,128)} %shard_map.77.refs_1_, f32[128,32768]{1,0:T(8,128)} %refs_2_.25, f32[128,32768]{1,0:T(8,128)} %refs_2_.25), custom_call_target="tpu_custom_call" | custom-call | tf_op jit(solution)/shard_map/pallas_call | solution.py:64
  234.0 5.1 %shard_map.75 = f32[2,12,128]{2,1,0:T(8,128)} custom-call(f32[24,6144]{1,0:T(8,128)} %copy-done.14, f32[24,6144]{1,0:T(8,128)} %shard_map.74.refs_1_, f32[128,32768]{1,0:T(8,128)} %refs_2_.25, f32[128,32768]{1,0:T(8,128)} %refs_2_.25), custom_call_target="tpu_custom_call" | custom-call | tf_op jit(solution)/shard_map/pallas_call | solution.py:64
  239.9 17.5 %shard_map.80.refs_0_ = f32[48,2816]{1,0:T(8,128)} custom-call(s32[1]{0:T(128)} %bitcast.2.flag_ref, f32[48,2816]{1,0:T(8,128)} %copy-done.16, f32[48,2816]{1,0:T(8,128)} %collective-permute-done.20.b_ref), custom_call_target="tpu_custom_call" | custom-call | tf_op jit(solution)/shard_map/pallas_call | solution.py:93
  257.4 3.4 %shard_map.81 = f32[2,12,128]{2,1,0:T(8,128)} custom-call(f32[48,2816]{1,0:T(8,128)} %shard_map.80.refs_0_, f32[128,32768]{1,0:T(8,128)} %refs_2_.25, f32[128,32768]{1,0:T(8,128)} %refs_2_.25), custom_call_target="tpu_custom_call" | custom-call | tf_op jit(solution)/shard_map/pallas_call | solution.py:64
  260.8 4.4 %shard_map.92 = f32[1,12,128]{2,1,0:T(8,128)} custom-call(f32[24,5120]{1,0:T(8,128)} %collective-permute-done.27.refs_0_, f32[128,32768]{1,0:T(8,128)} %refs_2_.25, f32[128,32768]{1,0:T(8,128)} %refs_2_.25), custom_call_target="tpu_custom_call" | custom-call | tf_op jit(solution)/shard_map/pallas_call | solution.py:64
  266.1 4.9 %shard_map.91 = f32[1,12,128]{2,1,0:T(8,128)} custom-call(f32[24,6144]{1,0:T(8,128)} %copy-done.15, f32[128,32768]{1,0:T(8,128)} %refs_2_.25, f32[128,32768]{1,0:T(8,128)} %refs_2_.25), custom_call_target="tpu_custom_call" | custom-call | tf_op jit(solution)/shard_map/pallas_call | solution.py:64
  272.5 1.6 collective-permute-start.33
  275.7 2.1 collective-permute-done.32
  278.5 3.2 %collective-permute-done.34 = f32[25,128]{1,0:T(8,128)S(1)} collective-permute-done((f32[25,128]{1,0:T(8,128)S(1)}, f32[25,128]{1,0:T(8,128)S(1)}, u32[]{:S(2)}, u32[]{:S(2)}) %collective-permute-start.34) | collective-permute-done | bytes 12832 | tf_op jit(solution)/shard_map/ppermute | solution.py:184
  281.7 2.5 collective-permute-start.37
  284.2 7.8 %collective-permute-start.36 = (f32[25,256]{1,0:T(8,128)S(1)}, f32[25,256]{1,0:T(8,128)S(1)}, u32[]{:S(2)}, u32[]{:S(2)}) collective-permute-start(f32[25,256]{1,0:T(8,128)S(1)} %pad_maximum_fusion.6), channel_id=1, source_target_pairs={{0,16},{4,20},{8,24},{12,28},{16,0},{20,4},{24,8},{28,12},{1,17},{... | collective-permute-start | bytes 76808 | tf_op jit(solution)/shard_map/ppermute | solution.py:184
  292.1 3.8 %collective-permute-done.35 = f32[25,256]{1,0:T(8,128)S(1)} collective-permute-done((f32[25,256]{1,0:T(8,128)S(1)}, f32[25,256]{1,0:T(8,128)S(1)}, u32[]{:S(2)}, u32[]{:S(2)}) %collective-permute-start.35) | collective-permute-done | bytes 25632 | tf_op jit(solution)/shard_map/ppermute | solution.py:184
  (172 shorter events, 29.2 us)
Async XLA Ops:
  1.4 27.9 %collective-permute-start.25 = (f32[24,5120]{1,0:T(8,128)S(1)}, f32[24,5120]{1,0:T(8,128)S(1)}, u32[]{:S(2)}, u32[]{:S(2)}) collective-permute-start(f32[24,5120]{1,0:T(8,128)S(1)} %pad_maximum_fusion.2.refs_0_), channel_id=1, source_target_pairs={{0,4},{4,0},{8,12},{12,8},{16,20},{20,16},{24,28},{28,24},{1,5},{5... | collective-permute-start | bytes 1474568 | tf_op jit(solution)/shard_map/ppermute | solution.py:184
  4.4 25.5 %collective-permute-start.8 = (f32[24,5120]{1,0:T(8,128)S(1)}, f32[24,5120]{1,0:T(8,128)S(1)}, u32[]{:S(2)}, u32[]{:S(2)}) collective-permute-start(f32[24,5120]{1,0:T(8,128)S(1)} %pad_maximum_fusion.2.refs_0_), channel_id=1, source_target_pairs={{0,8},{4,12},{8,0},{12,4},{16,24},{20,28},{24,16},{28,20},{1,9},{5... | collective-permute-start | bytes 1474568 | tf_op jit(solution)/shard_map/ppermute | solution.py:184
  6.0 24.7 %collective-permute-start.6 = (f32[24,5120]{1,0:T(8,128)S(1)}, f32[24,5120]{1,0:T(8,128)S(1)}, u32[]{:S(2)}, u32[]{:S(2)}) collective-permute-start(f32[24,5120]{1,0:T(8,128)S(1)} %pad_maximum_fusion.2.refs_0_), channel_id=1, source_target_pairs={{0,0},{4,4},{8,16},{12,20},{16,8},{20,12},{24,24},{28,28},{1,1},{5... | collective-permute-start | bytes 1474568 | tf_op jit(solution)/shard_map/ppermute | solution.py:184
  6.7 14.5 %collective-permute-start.12 = (f32[24,2304]{1,0:T(8,128)S(1)}, f32[24,2304]{1,0:T(8,128)S(1)}, u32[]{:S(2)}, u32[]{:S(2)}) collective-permute-start(f32[24,2304]{1,0:T(8,128)S(1)} %pad_maximum_fusion.5), channel_id=1, source_target_pairs={{0,4},{4,0},{8,12},{12,8},{16,20},{20,16},{24,28},{28,24},{1,5},{5... | collective-permute-start | bytes 663560 | tf_op jit(solution)/shard_map/ppermute | solution.py:184
  7.4 19.6 %collective-permute-start.16 = (f32[24,2816]{1,0:T(8,128)S(1)}, f32[24,2816]{1,0:T(8,128)S(1)}, u32[]{:S(2)}, u32[]{:S(2)}) collective-permute-start(f32[24,2816]{1,0:T(8,128)S(1)} %pad_maximum_fusion.4), channel_id=1, source_target_pairs={{0,4},{4,0},{8,12},{12,8},{16,20},{20,16},{24,28},{28,24},{1,5},{5... | collective-permute-start | bytes 811016 | tf_op jit(solution)/shard_map/ppermute | solution.py:184
  9.1 38.4 %copy-start.1 = (f32[24,6144]{1,0:T(8,128)}, f32[24,6144]{1,0:T(8,128)S(1)}, u32[]{:S(2)}) copy-start(f32[24,6144]{1,0:T(8,128)S(1)} %pad_maximum_fusion.refs_0_) | copy-start | bytes 1769476
  21.2 17.6 %collective-permute-start.24 = (f32[24,6144]{1,0:T(8,128)S(1)}, f32[24,6144]{1,0:T(8,128)S(1)}, u32[]{:S(2)}, u32[]{:S(2)}) collective-permute-start(f32[24,6144]{1,0:T(8,128)S(1)} %pad_maximum_fusion.refs_0_), channel_id=1, source_target_pairs={{0,4},{4,0},{8,12},{12,8},{16,20},{20,16},{24,28},{28,24},{1,5},{5... | collective-permute-start | bytes 1769480 | tf_op jit(solution)/shard_map/ppermute | solution.py:184
  27.0 15.8 %collective-permute-start.2 = (f32[24,6144]{1,0:T(8,128)S(1)}, f32[24,6144]{1,0:T(8,128)}, u32[]{:S(2)}, u32[]{:S(2)}) collective-permute-start(f32[24,6144]{1,0:T(8,128)S(1)} %pad_maximum_fusion.refs_0_), channel_id=1, source_target_pairs={{0,8},{4,12},{8,0},{12,4},{16,24},{20,28},{24,16},{28,20},{1,9},{5... | collective-permute-start | bytes 1769480 | tf_op jit(solution)/shard_map/ppermute | solution.py:184
  29.1 18.4 %copy-start = (f32[48,2304]{1,0:T(8,128)}, f32[48,2304]{1,0:T(8,128)S(1)}, u32[]{:S(2)}) copy-start(f32[48,2304]{1,0:T(8,128)S(1)} %pad_maximum_fusion.3.refs_0_) | copy-start | bytes 1327108
  29.2 49.4 %copy-start.2 = (f32[48,2816]{1,0:T(8,128)}, f32[48,2816]{1,0:T(8,128)S(1)}, u32[]{:S(2)}) copy-start(f32[48,2816]{1,0:T(8,128)S(1)} %pad_maximum_fusion.1.refs_0_) | copy-start | bytes 1622020
  29.2 18.3 %collective-permute-start = (f32[24,6144]{1,0:T(8,128)S(1)}, f32[24,6144]{1,0:T(8,128)S(1)}, u32[]{:S(2)}, u32[]{:S(2)}) collective-permute-start(f32[24,6144]{1,0:T(8,128)S(1)} %pad_maximum_fusion.refs_0_), channel_id=1, source_target_pairs={{0,0},{4,4},{8,16},{12,20},{16,8},{20,12},{24,24},{28,28},{1,1},{5... | collective-permute-start | bytes 1769480 | tf_op jit(solution)/shard_map/ppermute | solution.py:184
  29.9 50.1 %copy-start.22 = (f32[24,5120]{1,0:T(8,128)}, f32[24,5120]{1,0:T(8,128)S(1)}, u32[]{:S(2)}) copy-start(f32[24,5120]{1,0:T(8,128)S(1)} %collective-permute-done.8.refs_1_) | copy-start | bytes 1474564
  30.0 23.1 %collective-permute-start.14 = (f32[48,2304]{1,0:T(8,128)S(1)}, f32[48,2304]{1,0:T(8,128)S(1)}, u32[]{:S(2)}, u32[]{:S(2)}) collective-permute-start(f32[48,2304]{1,0:T(8,128)S(1)} %pad_maximum_fusion.3.refs_0_), channel_id=1, source_target_pairs={{0,0},{4,4},{8,16},{12,20},{16,8},{20,12},{24,24},{28,28},{1,1},{5... | collective-permute-start | bytes 1327112 | tf_op jit(solution)/shard_map/ppermute | solution.py:184
  30.7 49.4 %copy-start.19 = (f32[24,5120]{1,0:T(8,128)}, f32[24,5120]{1,0:T(8,128)S(1)}, u32[]{:S(2)}) copy-start(f32[24,5120]{1,0:T(8,128)S(1)} %collective-permute-done.6.b_ref) | copy-start | bytes 1474564
  30.7 27.1 %collective-permute-start.13 = (f32[48,2304]{1,0:T(8,128)S(1)}, f32[48,2304]{1,0:T(8,128)S(1)}, u32[]{:S(2)}, u32[]{:S(2)}) collective-permute-start(f32[48,2304]{1,0:T(8,128)S(1)} %pad_maximum_fusion.3.refs_0_), channel_id=1, source_target_pairs={{0,8},{4,12},{24,16},{28,20},{1,9},{5,13},{25,17},{29,21},{2,10},{... | collective-permute-start | bytes 1327112 | tf_op jit(solution)/shard_map/ppermute | solution.py:184
  38.8 25.1 %collective-permute-start.17 = (f32[48,2816]{1,0:T(8,128)S(1)}, f32[48,2816]{1,0:T(8,128)S(1)}, u32[]{:S(2)}, u32[]{:S(2)}) collective-permute-start(f32[48,2816]{1,0:T(8,128)S(1)} %pad_maximum_fusion.1.refs_0_), channel_id=1, source_target_pairs={{0,8},{4,12},{8,0},{12,4},{16,24},{20,28},{24,16},{28,20},{1,9},{5... | collective-permute-start | bytes 1622024 | tf_op jit(solution)/shard_map/ppermute | solution.py:184
  42.8 22.4 %collective-permute-start.22 = (f32[24,5120]{1,0:T(8,128)S(1)}, f32[24,5120]{1,0:T(8,128)S(1)}, u32[]{:S(2)}, u32[]{:S(2)}) collective-permute-start(f32[24,5120]{1,0:T(8,128)S(1)} %collective-permute-done.8.refs_1_), channel_id=1, source_target_pairs={{0,4},{4,0},{8,12},{12,8},{16,20},{20,16},{24,28},{28,24},{1,5},{5... | collective-permute-start | bytes 1474568 | tf_op jit(solution)/shard_map/ppermute | solution.py:184
  47.5 37.1 %copy-start.10 = (f32[24,6144]{1,0:T(8,128)}, f32[24,6144]{1,0:T(8,128)S(1)}, u32[]{:S(2)}) copy-start(f32[24,6144]{1,0:T(8,128)S(1)} %collective-permute-done.b_ref) | copy-start | bytes 1769476
  47.6 81.6 %collective-permute-start.29 = (f32[128,2304]{1,0:T(8,128)}, f32[128,2304]{1,0:T(8,128)}, u32[]{:S(2)}, u32[]{:S(2)}) collective-permute-start(f32[128,2304]{1,0:T(8,128)} %get-tuple-element.37), channel_id=1, source_target_pairs={{0,8},{4,12},{24,16},{28,20},{1,9},{5,13},{25,17},{29,21},{2,10},{... | collective-permute-start | bytes 3538952 | tf_op jit(solution)/shard_map/ppermute | solution.py:184
  53.1 31.5 %copy-start.6 = (f32[48,2304]{1,0:T(8,128)}, f32[48,2304]{1,0:T(8,128)S(1)}, u32[]{:S(2)}) copy-start(f32[48,2304]{1,0:T(8,128)S(1)} %collective-permute-done.14.refs_2_) | copy-start | bytes 1327108
  53.1 77.5 %collective-permute-start.28 = (f32[128,2304]{1,0:T(8,128)}, f32[128,2304]{1,0:T(8,128)}, u32[]{:S(2)}, u32[]{:S(2)}) collective-permute-start(f32[128,2304]{1,0:T(8,128)} %get-tuple-element.38), channel_id=1, source_target_pairs={{0,8},{4,12},{24,16},{28,20},{1,9},{5,13},{25,17},{29,21},{2,10},{... | collective-permute-start | bytes 3538952 | tf_op jit(solution)/shard_map/ppermute | solution.py:184
  57.7 26.9 %copy-start.7 = (f32[48,2304]{1,0:T(8,128)}, f32[48,2304]{1,0:T(8,128)S(1)}, u32[]{:S(2)}) copy-start(f32[48,2304]{1,0:T(8,128)S(1)} %collective-permute-done.13.refs_1_) | copy-start | bytes 1327108
  57.7 8.1 %collective-permute-start.9 = (f32[24,5120]{1,0:T(8,128)S(1)}, f32[24,5120]{1,0:T(8,128)}, u32[]{:S(2)}, u32[]{:S(2)}) collective-permute-start(f32[24,5120]{1,0:T(8,128)S(1)} %collective-permute-done.8.refs_1_), channel_id=1, source_target_pairs={{0,0},{4,4},{8,16},{12,20},{16,8},{20,12},{24,24},{28,28},{1,1},{5... | collective-permute-start | bytes 1474568 | tf_op jit(solution)/shard_map/ppermute | solution.py:184
  63.9 13.4 %collective-permute-start.7 = (f32[24,5120]{1,0:T(8,128)S(1)}, f32[24,5120]{1,0:T(8,128)S(1)}, u32[]{:S(2)}, u32[]{:S(2)}) collective-permute-start(f32[24,5120]{1,0:T(8,128)S(1)} %collective-permute-done.6.b_ref), channel_id=1, source_target_pairs={{8,0},{12,4},{16,24},{20,28},{9,1},{13,5},{17,25},{21,29},{10,2},{... | collective-permute-start | bytes 1474568 | tf_op jit(solution)/shard_map/ppermute | solution.py:184
  65.2 13.4 %collective-permute-start.15 = (f32[48,2304]{1,0:T(8,128)S(1)}, f32[48,2304]{1,0:T(8,128)S(1)}, u32[]{:S(2)}, u32[]{:S(2)}) collective-permute-start(f32[48,2304]{1,0:T(8,128)S(1)} %collective-permute-done.13.refs_1_), channel_id=1, source_target_pairs={{0,0},{4,4},{8,16},{12,20},{16,8},{20,12},{24,24},{28,28},{1,1},{5... | collective-permute-start | bytes 1327112 | tf_op jit(solution)/shard_map/ppermute | solution.py:184
  65.9 70.1 %collective-permute-start.3 = (f32[24,6144]{1,0:T(8,128)}, f32[24,6144]{1,0:T(8,128)}, u32[]{:S(2)}, u32[]{:S(2)}) collective-permute-start(f32[24,6144]{1,0:T(8,128)} %collective-permute-done.2.refs_1_), channel_id=1, source_target_pairs={{0,0},{4,4},{8,16},{12,20},{16,8},{20,12},{24,24},{28,28},{1,1},{5... | collective-permute-start | bytes 1769480 | tf_op jit(solution)/shard_map/ppermute | solution.py:184
  77.3 60.0 %collective-permute-start.1 = (f32[24,6144]{1,0:T(8,128)S(1)}, f32[24,6144]{1,0:T(8,128)}, u32[]{:S(2)}, u32[]{:S(2)}) collective-permute-start(f32[24,6144]{1,0:T(8,128)S(1)} %collective-permute-done.b_ref), channel_id=1, source_target_pairs={{8,0},{12,4},{16,24},{20,28},{9,1},{13,5},{17,25},{21,29},{10,2},{... | collective-permute-start | bytes 1769480 | tf_op jit(solution)/shard_map/ppermute | solution.py:184
  78.6 48.9 %collective-permute-start.20 = (f32[48,2816]{1,0:T(8,128)S(1)}, f32[48,2816]{1,0:T(8,128)}, u32[]{:S(2)}, u32[]{:S(2)}) collective-permute-start(f32[48,2816]{1,0:T(8,128)S(1)} %pad_maximum_fusion.1.refs_0_), channel_id=1, source_target_pairs={{0,0},{4,4},{8,16},{12,20},{16,8},{20,12},{24,24},{28,28},{1,1},{5... | collective-permute-start | bytes 1622024 | tf_op jit(solution)/shard_map/ppermute | solution.py:184
  127.5 32.6 %copy-start.5 = (f32[24,5120]{1,0:T(8,128)S(1)}, f32[24,5120]{1,0:T(8,128)}, u32[]{:S(2)}) copy-start(f32[24,5120]{1,0:T(8,128)} %shard_map.76.refs_1_) | copy-start | bytes 1474564
  127.5 71.2 %collective-permute-start.21 = (f32[24,6144]{1,0:T(8,128)}, f32[24,6144]{1,0:T(8,128)S(1)}, u32[]{:S(2)}, u32[]{:S(2)}) collective-permute-start(f32[24,6144]{1,0:T(8,128)} %collective-permute-done.2.refs_1_), channel_id=1, source_target_pairs={{0,4},{4,0},{8,12},{12,8},{16,20},{20,16},{24,28},{28,24},{1,5},{5... | collective-permute-start | bytes 1769480 | tf_op jit(solution)/shard_map/ppermute | solution.py:184
  129.1 47.5 %collective-permute-start.18 = (f32[48,2816]{1,0:T(8,128)S(1)}, f32[48,2816]{1,0:T(8,128)}, u32[]{:S(2)}, u32[]{:S(2)}) collective-permute-start(f32[48,2816]{1,0:T(8,128)S(1)} %copy-done.18), channel_id=1, source_target_pairs={{0,0},{4,4},{8,16},{12,20},{16,8},{20,12},{24,24},{28,28},{1,1},{5... | collective-permute-start | bytes 1622024 | tf_op jit(solution)/shard_map/ppermute | solution.py:184
  130.6 68.7 %collective-permute-start.23 = (f32[48,2816]{1,0:T(8,128)}, f32[48,2816]{1,0:T(8,128)}, u32[]{:S(2)}, u32[]{:S(2)}) collective-permute-start(f32[48,2816]{1,0:T(8,128)} %collective-permute-done.20.b_ref), channel_id=1, source_target_pairs={{8,0},{12,4},{16,24},{20,28},{9,1},{13,5},{17,25},{21,29},{10,2},{... | collective-permute-start | bytes 1622024 | tf_op jit(solution)/shard_map/ppermute | solution.py:184
  136.0 24.1 %collective-permute-start.11 = (f32[24,5120]{1,0:T(8,128)}, f32[24,5120]{1,0:T(8,128)}, u32[]{:S(2)}, u32[]{:S(2)}) collective-permute-start(f32[24,5120]{1,0:T(8,128)} %collective-permute-done.9.b_ref), channel_id=1, source_target_pairs={{8,0},{12,4},{16,24},{20,28},{9,1},{13,5},{17,25},{21,29},{10,2},{... | collective-permute-start | bytes 1474568 | tf_op jit(solution)/shard_map/ppermute | solution.py:184
  137.3 41.0 %collective-permute-start.5 = (f32[24,6144]{1,0:T(8,128)}, f32[24,6144]{1,0:T(8,128)S(1)}, u32[]{:S(2)}, u32[]{:S(2)}) collective-permute-start(f32[24,6144]{1,0:T(8,128)} %collective-permute-done.3.b_ref), channel_id=1, source_target_pairs={{8,0},{12,4},{16,24},{20,28},{9,1},{13,5},{17,25},{21,29},{10,2},{... | collective-permute-start | bytes 1769480 | tf_op jit(solution)/shard_map/ppermute | solution.py:184
  158.4 42.5 %copy-start.9 = (f32[8,12,128]{2,1,0:T(8,128)S(1)}, f32[8,12,128]{2,1,0:T(8,128)}, u32[]{:S(2)}) copy-start(f32[8,12,128]{2,1,0:T(8,128)} %shard_map.93) | copy-start | bytes 147460
  160.1 67.2 %collective-permute-start.10 = (f32[24,5120]{1,0:T(8,128)S(1)}, f32[24,5120]{1,0:T(8,128)S(1)}, u32[]{:S(2)}, u32[]{:S(2)}) collective-permute-start(f32[24,5120]{1,0:T(8,128)S(1)} %copy-done.5), channel_id=1, source_target_pairs={{0,4},{4,0},{8,12},{12,8},{16,20},{20,16},{24,28},{28,24},{1,5},{5... | collective-permute-start | bytes 1474568 | tf_op jit(solution)/shard_map/ppermute | solution.py:184
  176.7 56.5 %collective-permute-start.4 = (f32[24,6144]{1,0:T(8,128)}, f32[24,6144]{1,0:T(8,128)S(1)}, u32[]{:S(2)}, u32[]{:S(2)}) collective-permute-start(f32[24,6144]{1,0:T(8,128)} %shard_map.73.refs_1_), channel_id=1, source_target_pairs={{0,4},{4,0},{8,12},{12,8},{16,20},{20,16},{24,28},{28,24},{1,5},{5... | collective-permute-start | bytes 1769480 | tf_op jit(solution)/shard_map/ppermute | solution.py:184
  178.3 60.8 %collective-permute-start.19 = (f32[48,2816]{1,0:T(8,128)}, f32[48,2816]{1,0:T(8,128)S(1)}, u32[]{:S(2)}, u32[]{:S(2)}) collective-permute-start(f32[48,2816]{1,0:T(8,128)} %collective-permute-done.18.b_ref), channel_id=1, source_target_pairs={{8,0},{12,4},{16,24},{20,28},{9,1},{13,5},{17,25},{21,29},{10,2},{... | collective-permute-start | bytes 1622024 | tf_op jit(solution)/shard_map/ppermute | solution.py:184
  198.7 62.0 %collective-permute-start.27 = (f32[24,5120]{1,0:T(8,128)}, f32[24,5120]{1,0:T(8,128)}, u32[]{:S(2)}, u32[]{:S(2)}) collective-permute-start(f32[24,5120]{1,0:T(8,128)} %shard_map.77.refs_1_), channel_id=1, source_target_pairs={{0,4},{4,0},{8,12},{12,8},{16,20},{20,16},{24,28},{28,24},{1,5},{5... | collective-permute-start | bytes 1474568 | tf_op jit(solution)/shard_map/ppermute | solution.py:184
  199.3 66.0 %collective-permute-start.26 = (f32[24,6144]{1,0:T(8,128)}, f32[24,6144]{1,0:T(8,128)S(1)}, u32[]{:S(2)}, u32[]{:S(2)}) collective-permute-start(f32[24,6144]{1,0:T(8,128)} %shard_map.74.refs_1_), channel_id=1, source_target_pairs={{0,4},{4,0},{8,12},{12,8},{16,20},{20,16},{24,28},{28,24},{1,5},{5... | collective-permute-start | bytes 1769480 | tf_op jit(solution)/shard_map/ppermute | solution.py:184
  227.3 45.1 %collective-permute-start.30 = (f32[96,128]{1,0:T(8,128)S(1)}, f32[96,128]{1,0:T(8,128)S(1)}, u32[]{:S(2)}, u32[]{:S(2)}) collective-permute-start(f32[96,128]{1,0:T(8,128)S(1)} %concatenate.43), channel_id=1, source_target_pairs={{8,0},{12,4},{16,24},{20,28},{9,1},{13,5},{17,25},{21,29},{10,2},{... | collective-permute-start | bytes 147464 | tf_op jit(solution)/shard_map/ppermute | solution.py:184
  272.5 2.2 collective-permute-start.31
  272.5 3.2 %collective-permute-start.33 = (f32[24,128]{1,0:T(8,128)S(1)}, f32[24,128]{1,0:T(8,128)S(1)}, u32[]{:S(2)}, u32[]{:S(2)}) collective-permute-start(f32[24,128]{1,0:T(8,128)S(1)} %get-tuple-element.54), channel_id=1, source_target_pairs={{0,3},{1,2},{2,1},{3,0},{4,7},{5,6},{6,5},{7,4},{8,11},{9,10},{10,... | collective-permute-start | bytes 36872 | tf_op jit(solution)/shard_map/ppermute | solution.py:287
  274.1 3.7 %collective-permute-start.32 = (f32[24,128]{1,0:T(8,128)S(1)}, f32[24,128]{1,0:T(8,128)S(1)}, u32[]{:S(2)}, u32[]{:S(2)}) collective-permute-start(f32[24,128]{1,0:T(8,128)S(1)} %get-tuple-element.55), channel_id=1, source_target_pairs={{0,2},{1,3},{2,0},{3,1},{4,6},{5,7},{6,4},{7,5},{8,10},{9,11},{10,... | collective-permute-start | bytes 36872 | tf_op jit(solution)/shard_map/ppermute | solution.py:287
  277.9 3.8 %collective-permute-start.34 = (f32[25,128]{1,0:T(8,128)S(1)}, f32[25,128]{1,0:T(8,128)S(1)}, u32[]{:S(2)}, u32[]{:S(2)}) collective-permute-start(f32[25,128]{1,0:T(8,128)S(1)} %get-tuple-element.56), channel_id=1, source_target_pairs={{0,4},{4,0},{8,12},{12,8},{16,20},{20,16},{24,28},{28,24},{1,5},{5... | collective-permute-start | bytes 38408 | tf_op jit(solution)/shard_map/ppermute | solution.py:184
  281.7 14.2 %collective-permute-start.37 = (f32[25,256]{1,0:T(8,128)S(1)}, f32[25,256]{1,0:T(8,128)S(1)}, u32[]{:S(2)}, u32[]{:S(2)}) collective-permute-start(f32[25,256]{1,0:T(8,128)S(1)} %pad_maximum_fusion.6), channel_id=1, source_target_pairs={{0,24},{4,28},{8,16},{12,20},{16,8},{20,12},{24,0},{28,4},{1,25},{... | collective-permute-start | bytes 76808 | tf_op jit(solution)/shard_map/ppermute | solution.py:184
  284.2 11.7 %collective-permute-start.36 = (f32[25,256]{1,0:T(8,128)S(1)}, f32[25,256]{1,0:T(8,128)S(1)}, u32[]{:S(2)}, u32[]{:S(2)}) collective-permute-start(f32[25,256]{1,0:T(8,128)S(1)} %pad_maximum_fusion.6), channel_id=1, source_target_pairs={{0,16},{4,20},{8,24},{12,28},{16,0},{20,4},{24,8},{28,12},{1,17},{... | collective-permute-start | bytes 76808 | tf_op jit(solution)/shard_map/ppermute | solution.py:184
  292.0 3.9 %collective-permute-start.35 = (f32[25,256]{1,0:T(8,128)S(1)}, f32[25,256]{1,0:T(8,128)S(1)}, u32[]{:S(2)}, u32[]{:S(2)}) collective-permute-start(f32[25,256]{1,0:T(8,128)S(1)} %pad_maximum_fusion.6), channel_id=1, source_target_pairs={{0,8},{4,12},{8,0},{12,4},{16,24},{20,28},{24,16},{28,20},{1,9},{5... | collective-permute-start | bytes 76808 | tf_op jit(solution)/shard_map/ppermute | solution.py:184
  (33 other events, 218.6 us)

commit v2 on v1

--- a/solution.py
+++ b/solution.py
@@ -26,25 +26,56 @@
     return LANE * max(d for d in range(1, 29) if tiles % d == 0 and (d < tiles or tiles == 1))
 
 
-def products(blocks, factors, starts, rows):
+def products(blocks, factors, starts, rows, band, order=None):
     folds = len(factors)
-    width = blocks[0].shape[1]
-    band = factors[0].shape[0]
+    arrays, specs, flags, places = [], [], [], []
+    width = (blocks[0][1] if isinstance(blocks[0], tuple) else blocks[0]).shape[1]
     tk = step_width(width)
-    total = sum(b.shape[0] for b in blocks)
+    steps = width // tk
+    total = 0
+    for block in blocks:
+        if isinstance(block, tuple):
+            flag, a, b = block
+            k = len(flags)
+            flags.append(flag)
+            places.append((len(arrays), k))
+            arrays += [a, b]
+            specs.append(pl.BlockSpec((a.shape[0], tk), lambda i, s, k=k: (0, i * s[k])))
+            specs.append(pl.BlockSpec((a.shape[0], tk), lambda i, s, k=k: (0, i * (1 - s[k]))))
+        else:
+            a = block
+            places.append((len(arrays), None))
+            arrays.append(a)
+            specs.append(pl.BlockSpec((a.shape[0], tk), lambda i, s: (0, i)))
+        total += a.shape[0]
     groups = total // (folds * rows)
-    steps = width // tk
-
-    def kernel(*refs):
-        block_refs, factor_refs = refs[: len(blocks)], refs[len(blocks) : len(blocks) + folds]
+    if order is None:
+        order = range(groups)
+    scalars = jnp.stack([jnp.asarray(s, jnp.int32) for s in flags + list(order)])
+
+    for fold in range(folds):
+        top, left = starts[fold]
+        specs.append(
+            pl.BlockSpec(
+                (pl.Element(band), pl.Element(tk)),
+                lambda i, s, top=top, left=left: (top, pl.multiple_of(left + i * tk, LANE)),
+            )
+        )
+
+    def kernel(scalar_ref, *refs):
         out_ref, acc = refs[-2], refs[-1]
+        factor_refs = refs[len(arrays) : len(arrays) + folds]
         step = pl.program_id(0)
 
         @pl.when(step == 0)
         def _():
             acc[...] = jnp.zeros_like(acc)
 
-        hi, lo = split_bf16(jnp.concatenate([r[...] for r in block_refs], axis=0))
+        taken = [
+            refs[i][...] if k is None else jnp.where(scalar_ref[k] == 1, refs[i][...], refs[i + 1][...])
+            for i, k in places
+        ]
+        hi, lo = split_bf16(jnp.concatenate(taken, axis=0))
         both = jnp.concatenate([hi, lo], axis=0)
         for fold in range(folds):
             f_hi, f_lo = split_bf16(factor_refs[fold][...])
@@ -55,47 +86,51 @@
         def _():
             for g in range(groups):
                 base = g * folds * rows
-                out_ref[g] = sum(acc[fold, base + fold * rows : base + (fold + 1) * rows] for fold in range(folds))
-
-    def factor_spec(fold):
-        start = starts[fold]
-        return pl.BlockSpec((pl.Element(band), pl.Element(tk)), lambda i: (0, pl.multiple_of(start + i * tk, LANE)))
+                out_ref[scalar_ref[len(flags) + g]] = sum(
+                    acc[fold, base + fold * rows : base + (fold + 1) * rows] for fold in range(folds)
+                )
 
     return pl.pallas_call(
         kernel,
-        grid=(steps,),
-        in_specs=[pl.BlockSpec((b.shape[0], tk), lambda i: (0, i)) for b in blocks]
-        + [factor_spec(fold) for fold in range(folds)],
-        out_specs=pl.BlockSpec((groups, rows, band), lambda i: (0, 0, 0)),
+        grid_spec=pltpu.PrefetchScalarGridSpec(
+            num_scalar_prefetch=1,
+            grid=(steps,),
+            in_specs=specs,
+            out_specs=pl.BlockSpec((groups, rows, band), lambda i, s: (0, 0, 0)),
+            scratch_shapes=[pltpu.VMEM((folds, total, band), jnp.float32)],
+        ),
         out_shape=jax.ShapeDtypeStruct((groups, rows, band), jnp.float32),
-        scratch_shapes=[pltpu.VMEM((folds, total, band), jnp.float32)],
-    )(*blocks, *factors)
+    )(scalars, *arrays, *factors)
 
 
 CHUNKS = 2
 
 
 def choose(flag, a, b):
-    def kernel(flag_ref, a_ref, b_ref, out_ref, sem):
+    height, width = a.shape
+    tk = step_width(width)
+
+    def kernel(flag_ref, a_ref, b_ref, out_ref):
         @pl.when(flag_ref[0] == 1)
         def _():
-            copy = pltpu.make_async_copy(a_ref, out_ref, sem)
-            copy.start()
-            copy.wait()
+            out_ref[...] = a_ref[...]
 
         @pl.when(flag_ref[0] != 1)
         def _():
-            copy = pltpu.make_async_copy(b_ref, out_ref, sem)
-            copy.start()
-            copy.wait()
-
-    anywhere = pl.BlockSpec(memory_space=pl.ANY)
+            out_ref[...] = b_ref[...]
+
     return pl.pallas_call(
         kernel,
-        in_specs=[pl.BlockSpec(memory_space=pltpu.SMEM), anywhere, anywhere],
-        out_specs=anywhere,
+        grid_spec=pltpu.PrefetchScalarGridSpec(
+            num_scalar_prefetch=1,
+            grid=(width // tk,),
+            in_specs=[
+                pl.BlockSpec((height, tk), lambda i, flag: (0, i * flag[0])),
+                pl.BlockSpec((height, tk), lambda i, flag: (0, i * (1 - flag[0]))),
+            ],
+            out_specs=pl.BlockSpec((height, tk), lambda i, flag: (0, i)),
+        ),
         out_shape=jax.ShapeDtypeStruct(a.shape, a.dtype),
-        scratch_shapes=[pltpu.SemaphoreType.DMA],
     )(flag.astype(jnp.int32).reshape(1), a, b)
 
 
@@ -112,26 +147,24 @@
 def plan(planes):
     slots = lambda *js: tuple(("slot", j) for j in js)
     if exports(planes):
+        near = slots(0) + (("y", 0),) + slots(1)
+        inner = (("y", 1),) + slots(2) + (("y", 2),) + slots(3)
         return (
-            [("b", "y", 0), ("0", "e", 1), ("0", "m", 1), ("x", "y", 0), ("1", "e", 1), ("0", "y", 0), ("1", "m", 1)]
-            + [("1", "y", 0), ("b", "e", 1), ("x", "e", 1), ("x", "f", 0), ("x", "f", 1)]
-            + [("0", "mul", slots(0))]
-            + [("0", "y", 1), ("0", "m", 2), ("0", "e", 2), ("1", "mul", slots(0))]
-            + [("1", "y", 1), ("1", "m", 2), ("1", "e", 2), ("b", "m", 1), ("x", "m", 1)]
-            + [("0", "mul", (("y", 0), ("slot", 1))), ("b", "m", 2), ("1", "mul", (("y", 0), ("slot", 1)))]
-            + [("0", "sel", 2), ("0", "y", 2), ("0", "e", 3), ("x", "m", 2), ("b", "mul", slots(0, 1))]
-            + [("1", "sel", 2), ("1", "y", 2), ("1", "e", 3), ("b", "e", 2)]
-            + [("0", "mul", (("y", 1), ("slot", 2)))]
-            + [("0", "sel", 3), ("0", "y", 3), ("1", "mul", (("y", 1), ("slot", 2)))]
+            [("bx", "y", 0), ("0", "e", 1), ("0", "m", 1), ("1", "e", 1), ("0", "y", 0), ("1", "m", 1), ("1", "y", 0)]
+            + [("b", "e", 1), ("x", "e", 1), ("x", "f", 0)]
+            + [("0", "y", 1), ("0", "m", 2), ("0", "e", 2), ("0", "mul", near)]
+            + [("1", "y", 1), ("1", "m", 2), ("1", "e", 2), ("bx", "m", 1)]
+            + [("b", "m", 2), ("1", "mul", near)]
+            + [("0", "sel", 2), ("0", "y", 2), ("0", "e", 3), ("x", "m", 2)]
+            + [("1", "sel", 2), ("1", "y", 2), ("1", "e", 3), ("b", "e", 2), ("b", "mul", slots(0, 1))]
+            + [("0", "sel", 3), ("0", "y", 3)]
             + [("1", "sel", 3), ("1", "y", 3), ("b", "e", 3)]
-            + [("0", "mul", (("y", 2), ("slot", 3))), ("1", "mul", (("y", 2), ("slot", 3)))]
-            + [("x", "mul", "own"), ("x", "mul", "far"), ("x", "back", 0)]
-            + [("b", "sel", 2), ("b", "mul", slots(2)), ("0", "mul", (("y", 3),))]
-            + [("b", "sel", 3), ("b", "mul", slots(3)), ("1", "mul", (("y", 3),))]
+            + [("x", "mul", "own"), ("0", "mul", inner), ("x", "mul", "far"), ("x", "back", 0)]
+            + [("1", "mul", inner), ("0", "mul", (("y", 3),)), ("b", "mul", slots(2, 3)), ("1", "mul", (("y", 3),))]
         )
     chunks = [str(c) for c in range(CHUNKS)]
     last = planes - 1
-    steps = [("b", "y", 0)]
+    steps = [("bx", "y", 0)]
     for c in chunks:
         steps += [(c, "e", 1), (c, "y", 0)] + [(c, "m", 1)] * (last > 1)
     steps += [("b", "e", 1)] + [("b", "m", 1)] * (last > 1)
@@ -156,10 +189,10 @@
         sent = new
     for t in range(2, last):
         if arriving(t, planes):
-            steps += [("b", "sel", j) for j in arriving(t, planes)] + [("b", "mul", slots(*arriving(t, planes)))]
+            steps += [("b", "mul", slots(*arriving(t, planes)))]
     steps += [(c, "mul", tuple(("y", j) for j in sent)) for c in chunks[:-1]]
     if last > 1:
-        steps += [("b", "sel", last), ("b", "mul", slots(last))]
+        steps += [("b", "mul", slots(last))]
     steps += [(c, "mul", tuple(("y", j) for j in sent)) for c in chunks[-1:]]
     return steps
 
@@ -204,26 +237,33 @@
     for stream in sizes:
         begin[stream], at = at * LANE, at + sizes[stream]
 
+    begin["bx"], sizes["bx"] = 0, sizes["b"] + sizes.get("x", 0)
+
     def piece(stream):
         start, width = begin[stream], sizes[stream] * LANE
         return jnp.concatenate(
             [turned[:, f * stride + start : f * stride + start + width] for f in range(folds)], axis=0
         )
 
-    own = {stream: piece(stream) for stream in ("b", "0", "x", "1") if stream in sizes}
+    own = {stream: piece(stream) for stream in ("bx", "0", "1")}
     have = {(stream, "slot", 0): own[stream] for stream in ("0", "1")}
     parts = [[[], []] for _ in range(planes)]
-    far = [[None, None] for _ in range(planes)]
 
     def starts_of(stream):
-        return [f * stride + begin[stream] for f in range(folds)]
+        return [(0, f * stride + begin[stream]) for f in range(folds)]
+
+    def cut(stream, block):
+        return block[:, begin[stream] : begin[stream] + sizes[stream] * LANE]
 
     def multiply(stream, wanted):
         blocks, places = [], []
         for kind, j in wanted:
-            blocks.append(have[stream, kind, j])
+            if stream == "b" and j > 1:
+                blocks.append((j <= reach, have["b", "e", j], have["b", "m", planes - j]))
+            else:
+                blocks.append(have[stream, kind, j])
             places += [(j, 0), (j, 1)] if stream == "b" else [(j, int(kind == "y"))]
-        got = products(blocks, [factor_band] * folds, starts_of(stream), rows)
+        got = products(blocks, [factor_band] * folds, starts_of(stream), rows, band)
         for g, (j, q) in enumerate(places):
             parts[j][q].append(got[g])
 
@@ -231,13 +271,16 @@
         blocks = [have["x", "slot", 0], have["x", "e", 1], have["x", "m", 1], have["x", "m", 2]]
         places = [(j % planes, q) for j in (0, 1, -1, -2) for q in (0, 1)]
         if whose == "own":
-            got = products(blocks, [factor_band] * folds, starts_of("x"), rows)
+            got = products(blocks, [factor_band] * folds, starts_of("x"), rows, band)
             for g, (j, q) in enumerate(places):
                 parts[j][q].append(jnp.where(outer, 0.0, got[g]))
         else:
-            got = products(blocks, [have["x", "f", f] for f in range(folds)], [0] * folds, rows)
-            for g, (j, q) in enumerate(places):
-                far[j][q] = got[g]
+            order = [
+                2 * jnp.mod(z + heading * j, planes) + (y if q == 0 else 1 - y) for j, q in places
+            ]
+            have["x", "far", 0] = products(
+                blocks, [have["x", "f", 0]] * folds, [(f * band, 0) for f in range(folds)], rows, band, order
+            ).reshape(row_size * rows, band)
 
     def place(sums):
         placed = []
@@ -255,15 +298,17 @@
         if move == "mul":
             multiply_exported(j) if stream == "x" else multiply(stream, j)
         elif move == "back":
-            back = send(place(far), outward)
+            back = send(have["x", "far", 0], outward)
         elif move == "f":
-            if j < folds:
-                start = starts_of("x")[j]
-                have[step] = send(factor_band[:, start : start + sizes["x"] * LANE], inward)
+            strips = [factor_band[:, left : left + sizes["x"] * LANE] for _, left in starts_of("x")]
+            have[step] = send(jnp.concatenate(strips, axis=0), inward)
         elif move == "sel":
             have[stream, "slot", j] = choose(j <= reach, have[stream, "e", j], have[stream, "m", planes - j])
-        elif move == "y" and stream in ("b", "x"):
-            have[stream, "slot", 0] = jnp.concatenate([own[stream], send(own[stream], side)], axis=0)
+        elif step == ("bx", "y", 0):
+            have["bx", "slot", 0] = jnp.concatenate([own["bx"], send(own["bx"], side)], axis=0)
+            for part in ("b", "x"):
+                if part in sizes:
+                    have[part, "slot", 0] = cut(part, have["bx", "slot", 0])
         elif move == "y":
             have[step] = send(have[stream, "slot", j], side)
         else:
@@ -272,6 +317,9 @@
             if exports(planes) and move == "e" and j > 1:
                 pairs = outward
             have[step] = send(came, pairs)
+            if stream == "bx":
+                for part in ("b", "x"):
+                    have[part, move, j] = cut(part, have[step])
             if move == "e" and j == 1:
                 have[stream, "slot", 1] = have[step]
 

time: 298 us -> 263 us (0.88)
  Pallas kernels: 171 us -> 58.1 us
  waiting for transfers between devices: 39.1 us -> 108 us
  local copies, waits for them, and re-layouts: 8.12 us -> 17.7 us
    pallas_call x21 -> x14, Pallas kernels: 171 us -> 58.1 us  [the longest x10 50.4 us: products(): pl.pallas_call(kernel, grid_spec=pltpu.PrefetchScalarGridSpec(num_scalar_...]
    ppermute x35 -> x32, waiting for transfers between devices: 35.9 us -> 105 us  [body(): send = lambda x, pairs: lax.ppermute(x, 'row', pairs)]
    another operation x0 -> x7, local copies, waits for them, and re-layouts: none -> 4.14 us
    ppermute x35 -> x32, starting transfers between devices: 70.9 us -> 70.7 us  [body(): send = lambda x, pairs: lax.ppermute(x, 'row', pairs)]
  transfers between devices with their start and end apart: 38 -> 35, of which waited for: 10 -> 10; matrix products, arithmetic and copies ran while one was open for 3% -> 5% of each run, Pallas kernels for 58% -> 22%
where the time goes in v2:
time: 263 us; the launch traced here: 261 us
  waiting for transfers between devices  108 us (41%)
  starting transfers between devices  72.9 us (28%)
  Pallas kernels  58.1 us (22%)
  local copies, waits for them, and re-layouts  17.7 us (7%)
  other arithmetic  2.66 us (1%)
    ppermute x32, waiting for transfers between devices, body(): send = lambda x, pairs: lax.ppermute(x, 'row', pairs)  105 us
    ppermute x32, starting transfers between devices, body(): send = lambda x, pairs: lax.ppermute(x, 'row', pairs)  70.7 us
    pallas_call x10, Pallas kernels, products(): pl.pallas_call(kernel, grid_spec=pltpu.PrefetchScalarGridSpec(num_scalar_...  50.4 us
    pallas_call x4, Pallas kernels, choose(): pl.pallas_call(kernel, grid_spec=pltpu.PrefetchScalarGridSpec(num_scalar_...  7.73 us
  transfers between devices with their start and end apart: 35, of which 10 were waited for; matrix products, arithmetic and copies ran while one was open for 5% of the time, Pallas kernels for 22%

profile of v2, /device:TPU:0, one launch (start us, length us, event | category | flops | bytes accessed | tf_op | source)
XLA Modules:
  0.0 260.9 jit_solution(10905929231347199711)
XLA Ops:
  0.0 1.3 fusion.25
  1.4 3.1 %collective-permute-start.22 = (f32[24,6144]{1,0:T(8,128)S(1)}, f32[24,6144]{1,0:T(8,128)S(1)}, u32[]{:S(2)}, u32[]{:S(2)}) collective-permute-start(f32[24,6144]{1,0:T(8,128)S(1)} %pad_maximum_fusion.2.refs_0_), channel_id=1, source_target_pairs={{0,4},{4,0},{8,12},{12,8},{16,20},{20,16},{24,28},{28,24},{1,5},{5... | collective-permute-start | bytes 1769480 | tf_op jit(solution)/shard_map/ppermute | solution.py:217
  4.5 1.5 collective-permute-start.6
  6.0 3.6 %collective-permute-start.4 = (f32[24,6144]{1,0:T(8,128)S(1)}, f32[24,6144]{1,0:T(8,128)}, u32[]{:S(2)}, u32[]{:S(2)}) collective-permute-start(f32[24,6144]{1,0:T(8,128)S(1)} %pad_maximum_fusion.2.refs_0_), channel_id=1, source_target_pairs={{0,8},{4,12},{8,0},{12,4},{16,24},{20,28},{24,16},{28,20},{1,9},{5... | collective-permute-start | bytes 1769480 | tf_op jit(solution)/shard_map/ppermute | solution.py:217
  10.4 1.6 collective-permute-start.23
  12.0 1.8 fusion.24
  13.7 15.4 %collective-permute-done = f32[24,5120]{1,0:T(8,128)S(1)} collective-permute-done((f32[24,5120]{1,0:T(8,128)S(1)}, f32[24,5120]{1,0:T(8,128)S(1)}, u32[]{:S(2)}, u32[]{:S(2)}) %collective-permute-start) | collective-permute-done | bytes 491552 | tf_op jit(solution)/shard_map/ppermute | solution.py:217
  29.9 9.0 %collective-permute-done.23.refs_1_ = f32[24,5120]{1,0:T(8,128)S(1)} collective-permute-done((f32[24,5120]{1,0:T(8,128)S(1)}, f32[24,5120]{1,0:T(8,128)S(1)}, u32[]{:S(2)}, u32[]{:S(2)}) %collective-permute-start.23) | collective-permute-done | bytes 491552 | tf_op jit(solution)/shard_map/ppermute | solution.py:217
  38.9 1.8 collective-permute-start.11
  40.8 5.2 %collective-permute-start.1 = (f32[48,2304]{1,0:T(8,128)S(1)}, f32[48,2304]{1,0:T(8,128)S(1)}, u32[]{:S(2)}, u32[]{:S(2)}) collective-permute-start(f32[48,2304]{1,0:T(8,128)S(1)} %slice.178.refs_0_), channel_id=1, source_target_pairs={{0,8},{4,12},{24,16},{28,20},{1,9},{5,13},{25,17},{29,21},{2,10},{... | collective-permute-start | bytes 1327112 | tf_op jit(solution)/shard_map/ppermute | solution.py:217
  46.0 6.2 %collective-permute-done.11.refs_2_ = f32[24,5120]{1,0:T(8,128)S(1)} collective-permute-done((f32[24,5120]{1,0:T(8,128)S(1)}, f32[24,5120]{1,0:T(8,128)S(1)}, u32[]{:S(2)}, u32[]{:S(2)}) %collective-permute-start.11) | collective-permute-done | bytes 491552 | tf_op jit(solution)/shard_map/ppermute | solution.py:217
  52.3 1.4 collective-permute-start.15
  53.7 1.5 collective-permute-start.12
  55.2 1.3 collective-permute-start.14
  56.5 1.6 pad_maximum_fusion
  58.1 6.7 %collective-permute-start.26 = (f32[256,2304]{1,0:T(8,128)}, f32[256,2304]{1,0:T(8,128)S(1)}, u32[]{:S(2)}, u32[]{:S(2)}) collective-permute-start(f32[256,2304]{1,0:T(8,128)} %pad_maximum_fusion), channel_id=1, source_target_pairs={{0,8},{4,12},{24,16},{28,20},{1,9},{5,13},{25,17},{29,21},{2,10},{... | collective-permute-start | bytes 7077896 | tf_op jit(solution)/shard_map/ppermute | solution.py:217
  65.6 6.0 %collective-permute-start.8 = (f32[24,6144]{1,0:T(8,128)}, f32[24,6144]{1,0:T(8,128)}, u32[]{:S(2)}, u32[]{:S(2)}) collective-permute-start(f32[24,6144]{1,0:T(8,128)} %collective-permute-done.4.refs_2_), channel_id=1, source_target_pairs={{0,0},{4,4},{8,16},{12,20},{16,8},{20,12},{24,24},{28,28},{1,1},{5... | collective-permute-start | bytes 1769480 | tf_op jit(solution)/shard_map/ppermute | solution.py:217
  76.2 3.4 %collective-permute-start.19 = (f32[48,2816]{1,0:T(8,128)}, f32[48,2816]{1,0:T(8,128)}, u32[]{:S(2)}, u32[]{:S(2)}) collective-permute-start(f32[48,2816]{1,0:T(8,128)} %slice.188.refs_0_), channel_id=1, source_target_pairs={{0,8},{4,12},{8,0},{12,4},{16,24},{20,28},{24,16},{28,20},{1,9},{5... | collective-permute-start | bytes 1622024 | tf_op jit(solution)/shard_map/ppermute | solution.py:217
  80.9 1.9 shard_map.77.refs_1_
  82.8 40.0 %collective-permute-done.19.refs_1_ = f32[48,2816]{1,0:T(8,128)} collective-permute-done((f32[48,2816]{1,0:T(8,128)}, f32[48,2816]{1,0:T(8,128)}, u32[]{:S(2)}, u32[]{:S(2)}) %collective-permute-start.19) | collective-permute-done | bytes 540704 | tf_op jit(solution)/shard_map/ppermute | solution.py:217
  123.8 1.6 collective-permute-start.2
  125.5 5.0 %collective-permute-start.3 = (f32[48,2304]{1,0:T(8,128)}, f32[48,2304]{1,0:T(8,128)}, u32[]{:S(2)}, u32[]{:S(2)}) collective-permute-start(f32[48,2304]{1,0:T(8,128)} %copy-done.6), channel_id=1, source_target_pairs={{0,0},{4,4},{8,16},{12,20},{16,8},{20,12},{24,24},{28,28},{1,1},{5... | collective-permute-start | bytes 1327112 | tf_op jit(solution)/shard_map/ppermute | solution.py:217
  130.5 1.9 shard_map.74.refs_1_
  133.8 5.8 %collective-permute-start.20 = (f32[48,2816]{1,0:T(8,128)}, f32[48,2816]{1,0:T(8,128)}, u32[]{:S(2)}, u32[]{:S(2)}) collective-permute-start(f32[48,2816]{1,0:T(8,128)} %collective-permute-done.19.refs_1_), channel_id=1, source_target_pairs={{0,0},{4,4},{8,16},{12,20},{16,8},{20,12},{24,24},{28,28},{1,1},{5... | collective-permute-start | bytes 1622024 | tf_op jit(solution)/shard_map/ppermute | solution.py:217
  141.0 1.9 shard_map.75.refs_3_
  142.9 1.4 collective-permute-start.24
  145.4 26.6 %collective-permute-done.17.a_ref = f32[24,5120]{1,0:T(8,128)} collective-permute-done((f32[24,5120]{1,0:T(8,128)}, f32[24,5120]{1,0:T(8,128)}, u32[]{:S(2)}, u32[]{:S(2)}) %collective-permute-start.17) | collective-permute-done | bytes 491552 | tf_op jit(solution)/shard_map/ppermute | solution.py:217
  173.3 1.5 collective-permute-start.21
  174.8 2.0 shard_map.78.refs_3_
  176.7 1.4 collective-permute-start.25
  180.0 5.3 %shard_map.82 = f32[3,12,128]{2,1,0:T(8,128)} custom-call(s32[3]{0:T(128)} %iota.24.scalar_ref, f32[24,5120]{1,0:T(8,128)} %copy-done.5, f32[24,5120]{1,0:T(8,128)} %copy-done.11, f32[24,5120]{1,0:T(8,128)} %copy-done.12, f32[128,32768]{1,0:T(8,128)} %refs_2_.5, f32[128,32768]{1,0:T(8,128)} %refs_2_.5), custom_call_target="tpu_custom_call" | custom-call | tf_op jit(solution)/shard_map/pallas_call | solution.py:93
  185.8 5.8 %shard_map.81 = f32[3,12,128]{2,1,0:T(8,128)} custom-call(s32[3]{0:T(128)} %iota.23.scalar_ref, f32[24,6144]{1,0:T(8,128)} %copy-done.2, f32[24,6144]{1,0:T(8,128)} %copy-done.7, f32[24,6144]{1,0:T(8,128)} %collective-permute-done.4.refs_2_, f32[128,32768]{1,0:T(8,128)} %refs_2_.5, f32[128,32768]{1,0:T(8,128)} %refs_2_.5), custom_call_target="tpu_custom_call" | custom-call | tf_op jit(solution)/shard_map/pallas_call | solution.py:93
  192.2 4.2 %shard_map.83 = f32[4,12,128]{2,1,0:T(8,128)} custom-call(s32[4]{0:T(128)} %iota.25.scalar_ref, f32[48,2816]{1,0:T(8,128)} %slice.188.refs_0_, f32[48,2816]{1,0:T(8,128)} %collective-permute-done.19.refs_1_, f32[128,32768]{1,0:T(8,128)} %refs_2_.5, f32[128,32768]{1,0:T(8,128)} %refs_2_.5), custom_call_target="tpu_custom_call" | custom-call | tf_op jit(solution)/shard_map/pallas_call | solution.py:93
  196.4 1.8 slice.179.refs_2_
  198.8 5.7 %shard_map.79 = f32[4,12,128]{2,1,0:T(8,128)} custom-call(s32[4]{0:T(128)} %iota.22.scalar_ref, f32[24,5120]{1,0:T(8,128)} %copy-done.13, f32[24,5120]{1,0:T(8,128)} %shard_map.77.refs_1_, f32[24,5120]{1,0:T(8,128)} %collective-permute-done.16.refs_2_, f32[24,5120]{1,0:T(8,128)} %shard_map.78.refs_3_, f32[128,32768]{1,0:T(8,128)} %refs_2_.5, ...), custom_call_target="tpu_custom_call" | custom-call | tf_op jit(solution)/shard_map/pallas_call | solution.py:93
  205.0 4.8 %shard_map.73 = f32[8,12,128]{2,1,0:T(8,128)} custom-call(s32[8]{0:T(128)} %iota.20.scalar_ref, f32[48,2304]{1,0:T(8,128)} %copy-done.1, f32[48,2304]{1,0:T(8,128)} %copy-done.6, f32[48,2304]{1,0:T(8,128)} %slice.179.refs_2_, f32[48,2304]{1,0:T(8,128)} %collective-permute-done.3.refs_3_, f32[128,32768]{1,0:T(8,128)} %refs_2_.5, f32[128,32768]{1,0:T(8,128)} %refs_2_.5), custom_call_target="tpu_custom_call" | custom-call | tf_op jit(solution)/shard_map/pallas_call | solution.py:93
  210.4 6.2 %shard_map.76 = f32[4,12,128]{2,1,0:T(8,128)} custom-call(s32[4]{0:T(128)} %iota.21.scalar_ref, f32[24,6144]{1,0:T(8,128)} %collective-permute-done.5.refs_0_, f32[24,6144]{1,0:T(8,128)} %shard_map.74.refs_1_, f32[24,6144]{1,0:T(8,128)} %collective-permute-done.9.refs_2_, f32[24,6144]{1,0:T(8,128)} %shard_map.75.refs_3_, f32[128,32768]{1,0:T(8,128)} %refs_2_.5, ...), custom_call_target="tpu_custom_call" | custom-call | tf_op jit(solution)/shard_map/pallas_call | solution.py:93
  216.6 4.4 %shard_map.85 = f32[1,12,128]{2,1,0:T(8,128)} custom-call(s32[1]{0:T(128)} %constant.114.clone.1.scalar_ref, f32[24,5120]{1,0:T(8,128)} %collective-permute-done.25.refs_0_, f32[128,32768]{1,0:T(8,128)} %refs_2_.5, f32[128,32768]{1,0:T(8,128)} %refs_2_.5), custom_call_target="tpu_custom_call" | custom-call | tf_op jit(solution)/shard_map/pallas_call | solution.py:93
  220.9 4.5 %shard_map.80 = f32[4,12,128]{2,1,0:T(8,128)} custom-call(s32[6]{0:T(128)} %stack.32.scalar_ref, f32[48,2816]{1,0:T(8,128)} %collective-permute-done.18.refs_0_, f32[48,2816]{1,0:T(8,128)} %collective-permute-done.20.refs_1_, f32[48,2816]{1,0:T(8,128)} %collective-permute-done.21.refs_2_, f32[48,2816]{1,0:T(8,128)} %copy-done.3, f32[128,32768]{1,0:T(8,128)} %refs_2_.5, ...), custom_call_target="tpu_custom_call" | custom-call | tf_op jit(solution)/shard_map/pallas_call | solution.py:93
  225.4 1.4 copy-done
  226.8 4.8 %shard_map.86 = f32[8,12,128]{2,1,0:T(8,128)} custom-call(s32[8]{0:T(128)} %stack.41.scalar_ref, f32[48,2304]{1,0:T(8,128)} %copy-done.1, f32[48,2304]{1,0:T(8,128)} %copy-done.6, f32[48,2304]{1,0:T(8,128)} %slice.179.refs_2_, f32[48,2304]{1,0:T(8,128)} %collective-permute-done.3.refs_3_, f32[256,2304]{1,0:T(8,128)} %copy-done, f32[256,2304]{1,0:T(8,128)} %copy-done), custom_call_target="tpu_custom_call" | custom-call | tf_op jit(solution)/shard_map/pallas_call | solution.py:93
  232.5 1.4 collective-permute-start.27
  234.8 4.9 %shard_map.84 = f32[1,12,128]{2,1,0:T(8,128)} custom-call(s32[1]{0:T(128)} %constant.114.clone.1.scalar_ref, f32[24,6144]{1,0:T(8,128)} %copy-done.8, f32[128,32768]{1,0:T(8,128)} %refs_2_.5, f32[128,32768]{1,0:T(8,128)} %refs_2_.5), custom_call_target="tpu_custom_call" | custom-call | tf_op jit(solution)/shard_map/pallas_call | solution.py:93
  241.2 1.6 collective-permute-start.30
  244.3 2.1 collective-permute-done.29
  247.2 3.1 %collective-permute-done.31 = f32[25,128]{1,0:T(8,128)S(1)} collective-permute-done((f32[25,128]{1,0:T(8,128)S(1)}, f32[25,128]{1,0:T(8,128)S(1)}, u32[]{:S(2)}, u32[]{:S(2)}) %collective-permute-start.31) | collective-permute-done | bytes 12832 | tf_op jit(solution)/shard_map/ppermute | solution.py:217
  251.5 4.3 %collective-permute-start.33 = (f32[25,256]{1,0:T(8,128)S(1)}, f32[25,256]{1,0:T(8,128)S(1)}, u32[]{:S(2)}, u32[]{:S(2)}) collective-permute-start(f32[25,256]{1,0:T(8,128)S(1)} %pad_maximum_fusion.5), channel_id=1, source_target_pairs={{0,16},{4,20},{8,24},{12,28},{16,0},{20,4},{24,8},{28,12},{1,17},{... | collective-permute-start | bytes 76808 | tf_op jit(solution)/shard_map/ppermute | solution.py:217
  255.8 3.9 %collective-permute-done.32 = f32[25,256]{1,0:T(8,128)S(1)} collective-permute-done((f32[25,256]{1,0:T(8,128)S(1)}, f32[25,256]{1,0:T(8,128)S(1)}, u32[]{:S(2)}, u32[]{:S(2)}) %collective-permute-start.32) | collective-permute-done | bytes 25632 | tf_op jit(solution)/shard_map/ppermute | solution.py:217
  (130 shorter events, 26.9 us)
Async XLA Ops:
  0.0 9.6 %copy-start.4 = (f32[32768,12]{0,1:T(8,128)S(1)}, f32[32768,12]{0,1:T(8,128)}, u32[]{:S(2)}) copy-start(f32[32768,12]{0,1:T(8,128)} %param.8) | copy-start | bytes 4718596
  1.4 9.0 %copy-start.2 = (f32[24,6144]{1,0:T(8,128)}, f32[24,6144]{1,0:T(8,128)S(1)}, u32[]{:S(2)}) copy-start(f32[24,6144]{1,0:T(8,128)S(1)} %pad_maximum_fusion.2.refs_0_) | copy-start | bytes 1769476
  1.4 52.3 %collective-permute-start.22 = (f32[24,6144]{1,0:T(8,128)S(1)}, f32[24,6144]{1,0:T(8,128)S(1)}, u32[]{:S(2)}, u32[]{:S(2)}) collective-permute-start(f32[24,6144]{1,0:T(8,128)S(1)} %pad_maximum_fusion.2.refs_0_), channel_id=1, source_target_pairs={{0,4},{4,0},{8,12},{12,8},{16,20},{20,16},{24,28},{28,24},{1,5},{5... | collective-permute-start | bytes 1769480 | tf_op jit(solution)/shard_map/ppermute | solution.py:217
  4.5 50.8 %collective-permute-start.6 = (f32[24,6144]{1,0:T(8,128)S(1)}, f32[24,6144]{1,0:T(8,128)}, u32[]{:S(2)}, u32[]{:S(2)}) collective-permute-start(f32[24,6144]{1,0:T(8,128)S(1)} %pad_maximum_fusion.2.refs_0_), channel_id=1, source_target_pairs={{0,0},{4,4},{8,16},{12,20},{16,8},{20,12},{24,24},{28,28},{1,1},{5... | collective-permute-start | bytes 1769480 | tf_op jit(solution)/shard_map/ppermute | solution.py:217
  6.0 52.1 %collective-permute-start.4 = (f32[24,6144]{1,0:T(8,128)S(1)}, f32[24,6144]{1,0:T(8,128)}, u32[]{:S(2)}, u32[]{:S(2)}) collective-permute-start(f32[24,6144]{1,0:T(8,128)S(1)} %pad_maximum_fusion.2.refs_0_), channel_id=1, source_target_pairs={{0,8},{4,12},{8,0},{12,4},{16,24},{20,28},{24,16},{28,20},{1,9},{5... | collective-permute-start | bytes 1769480 | tf_op jit(solution)/shard_map/ppermute | solution.py:217
  9.7 19.4 %collective-permute-start = (f32[24,5120]{1,0:T(8,128)S(1)}, f32[24,5120]{1,0:T(8,128)S(1)}, u32[]{:S(2)}, u32[]{:S(2)}) collective-permute-start(f32[24,5120]{1,0:T(8,128)S(1)} %pad_maximum_fusion.3), channel_id=1, source_target_pairs={{0,4},{4,0},{8,12},{12,8},{16,20},{20,16},{24,28},{28,24},{1,5},{5... | collective-permute-start | bytes 1474568 | tf_op jit(solution)/shard_map/ppermute | solution.py:217
  10.4 28.5 %copy-start.5 = (f32[24,5120]{1,0:T(8,128)}, f32[24,5120]{1,0:T(8,128)S(1)}, u32[]{:S(2)}) copy-start(f32[24,5120]{1,0:T(8,128)S(1)} %pad_maximum_fusion.4.refs_0_) | copy-start | bytes 1474564
  10.4 28.5 %collective-permute-start.23 = (f32[24,5120]{1,0:T(8,128)S(1)}, f32[24,5120]{1,0:T(8,128)S(1)}, u32[]{:S(2)}, u32[]{:S(2)}) collective-permute-start(f32[24,5120]{1,0:T(8,128)S(1)} %pad_maximum_fusion.4.refs_0_), channel_id=1, source_target_pairs={{0,4},{4,0},{8,12},{12,8},{16,20},{20,16},{24,28},{28,24},{1,5},{5... | collective-permute-start | bytes 1474568 | tf_op jit(solution)/shard_map/ppermute | solution.py:217
  29.2 11.6 %collective-permute-start.13 = (f32[24,5120]{1,0:T(8,128)S(1)}, f32[24,5120]{1,0:T(8,128)S(1)}, u32[]{:S(2)}, u32[]{:S(2)}) collective-permute-start(f32[24,5120]{1,0:T(8,128)S(1)} %pad_maximum_fusion.4.refs_0_), channel_id=1, source_target_pairs={{0,0},{4,4},{8,16},{12,20},{16,8},{20,12},{24,24},{28,28},{1,1},{5... | collective-permute-start | bytes 1474568 | tf_op jit(solution)/shard_map/ppermute | solution.py:217
  38.9 17.7 %copy-start.11 = (f32[24,5120]{1,0:T(8,128)}, f32[24,5120]{1,0:T(8,128)S(1)}, u32[]{:S(2)}) copy-start(f32[24,5120]{1,0:T(8,128)S(1)} %collective-permute-done.23.refs_1_) | copy-start | bytes 1474564
  38.9 13.4 %collective-permute-start.11 = (f32[24,5120]{1,0:T(8,128)S(1)}, f32[24,5120]{1,0:T(8,128)S(1)}, u32[]{:S(2)}, u32[]{:S(2)}) collective-permute-start(f32[24,5120]{1,0:T(8,128)S(1)} %pad_maximum_fusion.4.refs_0_), channel_id=1, source_target_pairs={{0,8},{4,12},{8,0},{12,4},{16,24},{20,28},{24,16},{28,20},{1,9},{5... | collective-permute-start | bytes 1474568 | tf_op jit(solution)/shard_map/ppermute | solution.py:217
  40.8 17.3 %copy-start.1 = (f32[48,2304]{1,0:T(8,128)}, f32[48,2304]{1,0:T(8,128)S(1)}, u32[]{:S(2)}) copy-start(f32[48,2304]{1,0:T(8,128)S(1)} %slice.178.refs_0_) | copy-start | bytes 1327108
  40.8 30.8 %copy-start.9 = (f32[24,5120]{1,0:T(8,128)}, f32[24,5120]{1,0:T(8,128)S(1)}, u32[]{:S(2)}) copy-start(f32[24,5120]{1,0:T(8,128)S(1)} %collective-permute-done.13.b_ref) | copy-start | bytes 1474564
  40.8 24.0 %collective-permute-start.1 = (f32[48,2304]{1,0:T(8,128)S(1)}, f32[48,2304]{1,0:T(8,128)S(1)}, u32[]{:S(2)}, u32[]{:S(2)}) collective-permute-start(f32[48,2304]{1,0:T(8,128)S(1)} %slice.178.refs_0_), channel_id=1, source_target_pairs={{0,8},{4,12},{24,16},{28,20},{1,9},{5,13},{25,17},{29,21},{2,10},{... | collective-permute-start | bytes 1327112 | tf_op jit(solution)/shard_map/ppermute | solution.py:217
  52.3 21.4 %copy-start.12 = (f32[24,5120]{1,0:T(8,128)}, f32[24,5120]{1,0:T(8,128)S(1)}, u32[]{:S(2)}) copy-start(f32[24,5120]{1,0:T(8,128)S(1)} %collective-permute-done.11.refs_2_) | copy-start | bytes 1474564
  52.3 21.4 %collective-permute-start.15 = (f32[24,5120]{1,0:T(8,128)S(1)}, f32[24,5120]{1,0:T(8,128)}, u32[]{:S(2)}, u32[]{:S(2)}) collective-permute-start(f32[24,5120]{1,0:T(8,128)S(1)} %collective-permute-done.11.refs_2_), channel_id=1, source_target_pairs={{0,0},{4,4},{8,16},{12,20},{16,8},{20,12},{24,24},{28,28},{1,1},{5... | collective-permute-start | bytes 1474568 | tf_op jit(solution)/shard_map/ppermute | solution.py:217
  53.7 21.7 %collective-permute-start.12 = (f32[24,5120]{1,0:T(8,128)S(1)}, f32[24,5120]{1,0:T(8,128)S(1)}, u32[]{:S(2)}, u32[]{:S(2)}) collective-permute-start(f32[24,5120]{1,0:T(8,128)S(1)} %collective-permute-done.11.refs_2_), channel_id=1, source_target_pairs={{0,4},{4,0},{8,12},{12,8},{16,20},{20,16},{24,28},{28,24},{1,5},{5... | collective-permute-start | bytes 1474568 | tf_op jit(solution)/shard_map/ppermute | solution.py:217
  55.2 16.3 %collective-permute-start.14 = (f32[24,5120]{1,0:T(8,128)S(1)}, f32[24,5120]{1,0:T(8,128)S(1)}, u32[]{:S(2)}, u32[]{:S(2)}) collective-permute-start(f32[24,5120]{1,0:T(8,128)S(1)} %collective-permute-done.13.b_ref), channel_id=1, source_target_pairs={{8,0},{12,4},{16,24},{20,28},{9,1},{13,5},{17,25},{21,29},{10,2},{... | collective-permute-start | bytes 1474568 | tf_op jit(solution)/shard_map/ppermute | solution.py:217
  58.1 167.3 %collective-permute-start.26 = (f32[256,2304]{1,0:T(8,128)}, f32[256,2304]{1,0:T(8,128)S(1)}, u32[]{:S(2)}, u32[]{:S(2)}) collective-permute-start(f32[256,2304]{1,0:T(8,128)} %pad_maximum_fusion), channel_id=1, source_target_pairs={{0,8},{4,12},{24,16},{28,20},{1,9},{5,13},{25,17},{29,21},{2,10},{... | collective-permute-start | bytes 7077896 | tf_op jit(solution)/shard_map/ppermute | solution.py:217
  65.6 14.0 %collective-permute-start.8 = (f32[24,6144]{1,0:T(8,128)}, f32[24,6144]{1,0:T(8,128)}, u32[]{:S(2)}, u32[]{:S(2)}) collective-permute-start(f32[24,6144]{1,0:T(8,128)} %collective-permute-done.4.refs_2_), channel_id=1, source_target_pairs={{0,0},{4,4},{8,16},{12,20},{16,8},{20,12},{24,24},{28,28},{1,1},{5... | collective-permute-start | bytes 1769480 | tf_op jit(solution)/shard_map/ppermute | solution.py:217
  72.4 51.5 %collective-permute-start.7 = (f32[24,6144]{1,0:T(8,128)}, f32[24,6144]{1,0:T(8,128)}, u32[]{:S(2)}, u32[]{:S(2)}) collective-permute-start(f32[24,6144]{1,0:T(8,128)} %collective-permute-done.6.b_ref), channel_id=1, source_target_pairs={{8,0},{12,4},{16,24},{20,28},{9,1},{13,5},{17,25},{21,29},{10,2},{... | collective-permute-start | bytes 1769480 | tf_op jit(solution)/shard_map/ppermute | solution.py:217
  73.7 51.8 %collective-permute-start.5 = (f32[24,6144]{1,0:T(8,128)}, f32[24,6144]{1,0:T(8,128)}, u32[]{:S(2)}, u32[]{:S(2)}) collective-permute-start(f32[24,6144]{1,0:T(8,128)} %collective-permute-done.4.refs_2_), channel_id=1, source_target_pairs={{0,4},{4,0},{8,12},{12,8},{16,20},{20,16},{24,28},{28,24},{1,5},{5... | collective-permute-start | bytes 1769480 | tf_op jit(solution)/shard_map/ppermute | solution.py:217
  76.2 46.6 %collective-permute-start.19 = (f32[48,2816]{1,0:T(8,128)}, f32[48,2816]{1,0:T(8,128)}, u32[]{:S(2)}, u32[]{:S(2)}) collective-permute-start(f32[48,2816]{1,0:T(8,128)} %slice.188.refs_0_), channel_id=1, source_target_pairs={{0,8},{4,12},{8,0},{12,4},{16,24},{20,28},{24,16},{28,20},{1,9},{5... | collective-permute-start | bytes 1622024 | tf_op jit(solution)/shard_map/ppermute | solution.py:217
  79.6 60.1 %collective-permute-start.10 = (f32[24,6144]{1,0:T(8,128)}, f32[24,6144]{1,0:T(8,128)}, u32[]{:S(2)}, u32[]{:S(2)}) collective-permute-start(f32[24,6144]{1,0:T(8,128)} %collective-permute-done.8.b_ref), channel_id=1, source_target_pairs={{8,0},{12,4},{16,24},{20,28},{9,1},{13,5},{17,25},{21,29},{10,2},{... | collective-permute-start | bytes 1769480 | tf_op jit(solution)/shard_map/ppermute | solution.py:217
  122.8 11.1 %collective-permute-start.16 = (f32[24,5120]{1,0:T(8,128)}, f32[24,5120]{1,0:T(8,128)}, u32[]{:S(2)}, u32[]{:S(2)}) collective-permute-start(f32[24,5120]{1,0:T(8,128)} %shard_map.77.refs_1_), channel_id=1, source_target_pairs={{0,4},{4,0},{8,12},{12,8},{16,20},{20,16},{24,28},{28,24},{1,5},{5... | collective-permute-start | bytes 1474568 | tf_op jit(solution)/shard_map/ppermute | solution.py:217
  123.8 19.0 %collective-permute-start.2 = (f32[48,5120]{1,0:T(8,128)S(1)}, f32[48,5120]{1,0:T(8,128)}, u32[]{:S(2)}, u32[]{:S(2)}) collective-permute-start(f32[48,5120]{1,0:T(8,128)S(1)} %pad_maximum_fusion.1), channel_id=1, source_target_pairs={{0,0},{4,4},{8,16},{12,20},{16,8},{20,12},{24,24},{28,28},{1,1},{5... | collective-permute-start | bytes 2949128 | tf_op jit(solution)/shard_map/ppermute | solution.py:217
  125.5 6.9 %collective-permute-start.3 = (f32[48,2304]{1,0:T(8,128)}, f32[48,2304]{1,0:T(8,128)}, u32[]{:S(2)}, u32[]{:S(2)}) collective-permute-start(f32[48,2304]{1,0:T(8,128)} %copy-done.6), channel_id=1, source_target_pairs={{0,0},{4,4},{8,16},{12,20},{16,8},{20,12},{24,24},{28,28},{1,1},{5... | collective-permute-start | bytes 1327112 | tf_op jit(solution)/shard_map/ppermute | solution.py:217
  132.4 44.3 %collective-permute-start.9 = (f32[24,6144]{1,0:T(8,128)}, f32[24,6144]{1,0:T(8,128)}, u32[]{:S(2)}, u32[]{:S(2)}) collective-permute-start(f32[24,6144]{1,0:T(8,128)} %shard_map.74.refs_1_), channel_id=1, source_target_pairs={{0,4},{4,0},{8,12},{12,8},{16,20},{20,16},{24,28},{28,24},{1,5},{5... | collective-permute-start | bytes 1769480 | tf_op jit(solution)/shard_map/ppermute | solution.py:217
  133.8 39.4 %collective-permute-start.20 = (f32[48,2816]{1,0:T(8,128)}, f32[48,2816]{1,0:T(8,128)}, u32[]{:S(2)}, u32[]{:S(2)}) collective-permute-start(f32[48,2816]{1,0:T(8,128)} %collective-permute-done.19.refs_1_), channel_id=1, source_target_pairs={{0,0},{4,4},{8,16},{12,20},{16,8},{20,12},{24,24},{28,28},{1,1},{5... | collective-permute-start | bytes 1622024 | tf_op jit(solution)/shard_map/ppermute | solution.py:217
  139.7 32.3 %collective-permute-start.17 = (f32[24,5120]{1,0:T(8,128)}, f32[24,5120]{1,0:T(8,128)}, u32[]{:S(2)}, u32[]{:S(2)}) collective-permute-start(f32[24,5120]{1,0:T(8,128)} %collective-permute-done.15.b_ref), channel_id=1, source_target_pairs={{8,0},{12,4},{16,24},{20,28},{9,1},{13,5},{17,25},{21,29},{10,2},{... | collective-permute-start | bytes 1474568 | tf_op jit(solution)/shard_map/ppermute | solution.py:217
  140.9 38.4 %copy-start.25 = (s32[128]{0:T(128)S(1)}, s32[128]{0:T(128)}, u32[]{:S(2)}) copy-start(s32[128]{0:T(128)} %param.13) | copy-start | bytes 1540
  142.9 91.1 %collective-permute-start.24 = (f32[24,6144]{1,0:T(8,128)}, f32[24,6144]{1,0:T(8,128)S(1)}, u32[]{:S(2)}, u32[]{:S(2)}) collective-permute-start(f32[24,6144]{1,0:T(8,128)} %shard_map.75.refs_3_), channel_id=1, source_target_pairs={{0,4},{4,0},{8,12},{12,8},{16,20},{20,16},{24,28},{28,24},{1,5},{5... | collective-permute-start | bytes 1769480 | tf_op jit(solution)/shard_map/ppermute | solution.py:217
  145.4 39.9 %copy-start.3 = (f32[48,2816]{1,0:T(8,128)}, f32[48,2816]{1,0:T(8,128)S(1)}, u32[]{:S(2)}) copy-start(f32[48,2816]{1,0:T(8,128)S(1)} %slice.187.refs_3_) | copy-start | bytes 1622020
  172.0 48.9 %collective-permute-start.18 = (f32[48,2816]{1,0:T(8,128)S(1)}, f32[48,2816]{1,0:T(8,128)}, u32[]{:S(2)}, u32[]{:S(2)}) collective-permute-start(f32[48,2816]{1,0:T(8,128)S(1)} %slice.187.refs_3_), channel_id=1, source_target_pairs={{8,0},{12,4},{16,24},{20,28},{9,1},{13,5},{17,25},{21,29},{10,2},{... | collective-permute-start | bytes 1622024 | tf_op jit(solution)/shard_map/ppermute | solution.py:217
  173.3 47.7 %collective-permute-start.21 = (f32[48,2816]{1,0:T(8,128)}, f32[48,2816]{1,0:T(8,128)}, u32[]{:S(2)}, u32[]{:S(2)}) collective-permute-start(f32[48,2816]{1,0:T(8,128)} %collective-permute-done.20.refs_1_), channel_id=1, source_target_pairs={{8,0},{12,4},{16,24},{20,28},{9,1},{13,5},{17,25},{21,29},{10,2},{... | collective-permute-start | bytes 1622024 | tf_op jit(solution)/shard_map/ppermute | solution.py:217
  176.7 39.8 %collective-permute-start.25 = (f32[24,5120]{1,0:T(8,128)}, f32[24,5120]{1,0:T(8,128)}, u32[]{:S(2)}, u32[]{:S(2)}) collective-permute-start(f32[24,5120]{1,0:T(8,128)} %shard_map.78.refs_3_), channel_id=1, source_target_pairs={{0,4},{4,0},{8,12},{12,8},{16,20},{20,16},{24,28},{28,24},{1,5},{5... | collective-permute-start | bytes 1474568 | tf_op jit(solution)/shard_map/ppermute | solution.py:217
  232.5 10.8 %copy-start.26 = (s32[128]{0:T(128)S(1)}, s32[128]{0:T(128)}, u32[]{:S(2)}) copy-start(s32[128]{0:T(128)} %param.12) | copy-start | bytes 1540
  232.5 14.0 %copy-start.22 = (f32[128]{0:T(128)S(1)}, f32[128]{0:T(128)}, u32[]{:S(2)}) copy-start(f32[128]{0:T(128)} %param.11) | copy-start | bytes 1540
  232.5 13.9 %copy-start.23 = (f32[128]{0:T(128)S(1)}, f32[128]{0:T(128)}, u32[]{:S(2)}) copy-start(f32[128]{0:T(128)} %param.10) | copy-start | bytes 1540
  232.5 13.9 %copy-start.24 = (f32[128]{0:T(128)S(1)}, f32[128]{0:T(128)}, u32[]{:S(2)}) copy-start(f32[128]{0:T(128)} %param.9) | copy-start | bytes 1540
  232.5 8.5 %collective-permute-start.27 = (f32[96,128]{1,0:T(8,128)S(1)}, f32[96,128]{1,0:T(8,128)S(1)}, u32[]{:S(2)}, u32[]{:S(2)}) collective-permute-start(f32[96,128]{1,0:T(8,128)S(1)} %reshape.95), channel_id=1, source_target_pairs={{8,0},{12,4},{16,24},{20,28},{9,1},{13,5},{17,25},{21,29},{10,2},{... | collective-permute-start | bytes 147464 | tf_op jit(solution)/shard_map/ppermute | solution.py:217
  241.1 2.2 collective-permute-start.28
  241.2 3.2 %collective-permute-start.30 = (f32[24,128]{1,0:T(8,128)S(1)}, f32[24,128]{1,0:T(8,128)S(1)}, u32[]{:S(2)}, u32[]{:S(2)}) collective-permute-start(f32[24,128]{1,0:T(8,128)S(1)} %get-tuple-element.40), channel_id=1, source_target_pairs={{0,3},{1,2},{2,1},{3,0},{4,7},{5,6},{6,5},{7,4},{8,11},{9,10},{10,... | collective-permute-start | bytes 36872 | tf_op jit(solution)/shard_map/ppermute | solution.py:335
  242.7 3.7 %collective-permute-start.29 = (f32[24,128]{1,0:T(8,128)S(1)}, f32[24,128]{1,0:T(8,128)S(1)}, u32[]{:S(2)}, u32[]{:S(2)}) collective-permute-start(f32[24,128]{1,0:T(8,128)S(1)} %get-tuple-element.41), channel_id=1, source_target_pairs={{0,2},{1,3},{2,0},{3,1},{4,6},{5,7},{6,4},{7,5},{8,10},{9,11},{10,... | collective-permute-start | bytes 36872 | tf_op jit(solution)/shard_map/ppermute | solution.py:335
  246.5 3.8 %collective-permute-start.31 = (f32[25,128]{1,0:T(8,128)S(1)}, f32[25,128]{1,0:T(8,128)S(1)}, u32[]{:S(2)}, u32[]{:S(2)}) collective-permute-start(f32[25,128]{1,0:T(8,128)S(1)} %get-tuple-element.42), channel_id=1, source_target_pairs={{0,4},{4,0},{8,12},{12,8},{16,20},{20,16},{24,28},{28,24},{1,5},{5... | collective-permute-start | bytes 38408 | tf_op jit(solution)/shard_map/ppermute | solution.py:217
  250.3 9.5 %collective-permute-start.34 = (f32[25,256]{1,0:T(8,128)S(1)}, f32[25,256]{1,0:T(8,128)S(1)}, u32[]{:S(2)}, u32[]{:S(2)}) collective-permute-start(f32[25,256]{1,0:T(8,128)S(1)} %pad_maximum_fusion.5), channel_id=1, source_target_pairs={{0,24},{4,28},{8,16},{12,20},{16,8},{20,12},{24,0},{28,4},{1,25},{... | collective-permute-start | bytes 76808 | tf_op jit(solution)/shard_map/ppermute | solution.py:217
  251.5 8.2 %collective-permute-start.33 = (f32[25,256]{1,0:T(8,128)S(1)}, f32[25,256]{1,0:T(8,128)S(1)}, u32[]{:S(2)}, u32[]{:S(2)}) collective-permute-start(f32[25,256]{1,0:T(8,128)S(1)} %pad_maximum_fusion.5), channel_id=1, source_target_pairs={{0,16},{4,20},{8,24},{12,28},{16,0},{20,4},{24,8},{28,12},{1,17},{... | collective-permute-start | bytes 76808 | tf_op jit(solution)/shard_map/ppermute | solution.py:217
  255.8 3.9 %collective-permute-start.32 = (f32[25,256]{1,0:T(8,128)S(1)}, f32[25,256]{1,0:T(8,128)S(1)}, u32[]{:S(2)}, u32[]{:S(2)}) collective-permute-start(f32[25,256]{1,0:T(8,128)S(1)} %pad_maximum_fusion.5), channel_id=1, source_target_pairs={{0,8},{4,12},{8,0},{12,4},{16,24},{20,28},{24,16},{28,20},{1,9},{5... | collective-permute-start | bytes 76808 | tf_op jit(solution)/shard_map/ppermute | solution.py:217
  (14 other events, 64.5 us)

commit v3 on v2

--- a/solution.py
+++ b/solution.py
@@ -40,29 +40,32 @@
             flags.append(flag)
             places.append((len(arrays), k))
             arrays += [a, b]
-            specs.append(pl.BlockSpec((a.shape[0], tk), lambda i, s, k=k: (0, i * s[k])))
-            specs.append(pl.BlockSpec((a.shape[0], tk), lambda i, s, k=k: (0, i * (1 - s[k]))))
+            specs.append(pl.BlockSpec((a.shape[0], tk), lambda i, *s, k=k: (0, i * s[k][0])))
+            specs.append(pl.BlockSpec((a.shape[0], tk), lambda i, *s, k=k: (0, i * (1 - s[k][0]))))
         else:
             a = block
             places.append((len(arrays), None))
             arrays.append(a)
-            specs.append(pl.BlockSpec((a.shape[0], tk), lambda i, s: (0, i)))
+            specs.append(pl.BlockSpec((a.shape[0], tk), lambda i, *s: (0, i)))
         total += a.shape[0]
     groups = total // (folds * rows)
-    if order is None:
-        order = range(groups)
-    scalars = jnp.stack([jnp.asarray(s, jnp.int32) for s in flags + list(order)])
+    scalars = flags + ([] if order is None else [order])
 
     for fold in range(folds):
         top, left = starts[fold]
         specs.append(
             pl.BlockSpec(
                 (pl.Element(band), pl.Element(tk)),
-                lambda i, s, top=top, left=left: (top, pl.multiple_of(left + i * tk, LANE)),
+                lambda i, *s, top=top, left=left: (top, pl.multiple_of(left + i * tk, LANE)),
             )
         )
 
-    def kernel(scalar_ref, *refs):
+    lows = [fold * rows // 8 * 8 for fold in range(folds)]
+    tall = max(-(-(fold + 1) * rows // 8) * 8 - lows[fold] for fold in range(folds))
+    lows = [min(low, folds * rows - tall) for low in lows]
+
+    def kernel(*refs):
+        scalar_refs, refs = refs[: len(scalars)], refs[len(scalars) :]
         out_ref, acc = refs[-2], refs[-1]
         factor_refs = refs[len(arrays) : len(arrays) + folds]
         step = pl.program_id(0)
@@ -71,36 +74,37 @@
         def _():
             acc[...] = jnp.zeros_like(acc)
 
-        taken = [
-            refs[i][...] if k is None else jnp.where(scalar_ref[k] == 1, refs[i][...], refs[i + 1][...])
-            for i, k in places
-        ]
-        hi, lo = split_bf16(jnp.concatenate(taken, axis=0))
-        both = jnp.concatenate([hi, lo], axis=0)
+        taken = []
+        for i, k in places:
+            block = refs[i][...]
+            if k is not None:
+                block = jnp.where(scalar_refs[k][0] == 1, block, refs[i + 1][...])
+            taken += [block[top : top + folds * rows] for top in range(0, block.shape[0], folds * rows)]
         for fold in range(folds):
+            hi, lo = split_bf16(jnp.concatenate([t[lows[fold] : lows[fold] + tall] for t in taken], axis=0))
             f_hi, f_lo = split_bf16(factor_refs[fold][...])
-            first = dot_t(both, f_hi)
-            acc[fold] += first[:total] + (first[total:] + dot_t(hi, f_lo))
+            first = dot_t(jnp.concatenate([hi, lo], axis=0), f_hi)
+            acc[fold] += first[: groups * tall] + (first[groups * tall :] + dot_t(hi, f_lo))
 
         @pl.when(step == steps - 1)
         def _():
             for g in range(groups):
-                base = g * folds * rows
-                out_ref[scalar_ref[len(flags) + g]] = sum(
-                    acc[fold, base + fold * rows : base + (fold + 1) * rows] for fold in range(folds)
+                base = [g * tall + fold * rows - lows[fold] for fold in range(folds)]
+                out_ref[g if order is None else scalar_refs[-1][g]] = sum(
+                    acc[fold, base[fold] : base[fold] + rows] for fold in range(folds)
                 )
 
     return pl.pallas_call(
         kernel,
         grid_spec=pltpu.PrefetchScalarGridSpec(
-            num_scalar_prefetch=1,
+            num_scalar_prefetch=len(scalars),
             grid=(steps,),
             in_specs=specs,
-            out_specs=pl.BlockSpec((groups, rows, band), lambda i, s: (0, 0, 0)),
-            scratch_shapes=[pltpu.VMEM((folds, total, band), jnp.float32)],
+            out_specs=pl.BlockSpec((groups, rows, band), lambda i, *s: (0, 0, 0)),
+            scratch_shapes=[pltpu.VMEM((folds, groups * tall, band), jnp.float32)],
         ),
         out_shape=jax.ShapeDtypeStruct((groups, rows, band), jnp.float32),
-    )(scalars, *arrays, *factors)
+    )(*scalars, *arrays, *factors)
 
 
 CHUNKS = 2
@@ -131,7 +135,7 @@
             out_specs=pl.BlockSpec((height, tk), lambda i, flag: (0, i)),
         ),
         out_shape=jax.ShapeDtypeStruct(a.shape, a.dtype),
-    )(flag.astype(jnp.int32).reshape(1), a, b)
+    )(flag, a, b)
 
 
 def arriving(t, planes):
@@ -153,14 +157,14 @@
             [("bx", "y", 0), ("0", "e", 1), ("0", "m", 1), ("1", "e", 1), ("0", "y", 0), ("1", "m", 1), ("1", "y", 0)]
             + [("b", "e", 1), ("x", "e", 1), ("x", "f", 0)]
             + [("0", "y", 1), ("0", "m", 2), ("0", "e", 2), ("0", "mul", near)]
-            + [("1", "y", 1), ("1", "m", 2), ("1", "e", 2), ("bx", "m", 1)]
-            + [("b", "m", 2), ("1", "mul", near)]
-            + [("0", "sel", 2), ("0", "y", 2), ("0", "e", 3), ("x", "m", 2)]
-            + [("1", "sel", 2), ("1", "y", 2), ("1", "e", 3), ("b", "e", 2), ("b", "mul", slots(0, 1))]
-            + [("0", "sel", 3), ("0", "y", 3)]
-            + [("1", "sel", 3), ("1", "y", 3), ("b", "e", 3)]
-            + [("x", "mul", "own"), ("0", "mul", inner), ("x", "mul", "far"), ("x", "back", 0)]
-            + [("1", "mul", inner), ("0", "mul", (("y", 3),)), ("b", "mul", slots(2, 3)), ("1", "mul", (("y", 3),))]
+            + [("1", "y", 1), ("1", "m", 2), ("1", "e", 2), ("bx", "m", 1), ("1", "mul", near)]
+            + [("b", "m", 2), ("x", "m", 2), ("b", "mul", slots(0, 1))]
+            + [("0", "sel", 2), ("0", "y", 2), ("0", "e", 3)]
+            + [("1", "sel", 2), ("1", "y", 2), ("1", "e", 3), ("b", "e", 2)]
+            + [("0", "sel", 3), ("0", "y", 3), ("0", "mul", inner)]
+            + [("1", "sel", 3), ("1", "y", 3), ("b", "e", 3), ("1", "mul", inner)]
+            + [("x", "mul", "own"), ("x", "mul", "far"), ("x", "back", 0)]
+            + [("0", "mul", (("y", 3),)), ("b", "mul", slots(2, 3)), ("1", "mul", (("y", 3),))]
         )
     chunks = [str(c) for c in range(CHUNKS)]
     last = planes - 1
@@ -213,11 +217,12 @@
         return [(r, 2 * neighbour(r // 2) + r % 2) for r in range(row_size)]
 
     even = line(lambda p: p ^ 1)
-    odd = line(lambda p: p if p in (0, planes - 1) else ((p - 1) ^ 1) + 1)
+    odd = [pair for pair in line(lambda p: ((p - 1) ^ 1) + 1) if pair[0] // 2 not in (0, planes - 1)]
     send = lambda x, pairs: lax.ppermute(x, "row", pairs)
     heading = 1 - 2 * (z % 2)
     reach = jnp.where(heading == 1, planes - 1 - z, z)
 
+    near_end = [(j <= reach).astype(jnp.int32).reshape(1) for j in range(planes)]
     outer = (z == 0) | (z == planes - 1)
 
     def between(pairs, take):
@@ -259,7 +264,7 @@
         blocks, places = [], []
         for kind, j in wanted:
             if stream == "b" and j > 1:
-                blocks.append((j <= reach, have["b", "e", j], have["b", "m", planes - j]))
+                blocks.append((near_end[j], have["b", "e", j], have["b", "m", planes - j]))
             else:
                 blocks.append(have[stream, kind, j])
             places += [(j, 0), (j, 1)] if stream == "b" else [(j, int(kind == "y"))]
@@ -275,9 +280,8 @@
             for g, (j, q) in enumerate(places):
                 parts[j][q].append(jnp.where(outer, 0.0, got[g]))
         else:
-            order = [
-                2 * jnp.mod(z + heading * j, planes) + (y if q == 0 else 1 - y) for j, q in places
-            ]
+            slot, other = jnp.array(places, jnp.int32).T
+            order = 2 * jnp.mod(z + heading * slot, planes) + (y + other) % 2
             have["x", "far", 0] = products(
                 blocks, [have["x", "f", 0]] * folds, [(f * band, 0) for f in range(folds)], rows, band, order
             ).reshape(row_size * rows, band)
@@ -303,7 +307,7 @@
             strips = [factor_band[:, left : left + sizes["x"] * LANE] for _, left in starts_of("x")]
             have[step] = send(jnp.concatenate(strips, axis=0), inward)
         elif move == "sel":
-            have[stream, "slot", j] = choose(j <= reach, have[stream, "e", j], have[stream, "m", planes - j])
+            have[stream, "slot", j] = choose(near_end[j], have[stream, "e", j], have[stream, "m", planes - j])
         elif step == ("bx", "y", 0):
             have["bx", "slot", 0] = jnp.concatenate([own["bx"], send(own["bx"], side)], axis=0)
             for part in ("b", "x"):

time: 263 us -> 251 us (0.954)
  waiting for transfers between devices: 108 us -> 121 us
  starting transfers between devices: 72.9 us -> 60.3 us
  Pallas kernels: 58.1 us -> 51.6 us
  local copies, waits for them, and re-layouts: 17.7 us -> 12.2 us
    ppermute x32, waiting for transfers between devices: 105 us -> 118 us  [body(): send = lambda x, pairs: lax.ppermute(x, 'row', pairs)]
    ppermute x32, starting transfers between devices: 70.7 us -> 58.1 us  [body(): send = lambda x, pairs: lax.ppermute(x, 'row', pairs)]
    pallas_call x10, Pallas kernels: 50.4 us -> 43.9 us  [products(): pl.pallas_call(kernel, grid_spec=pltpu.PrefetchScalarGridSpec(num_scalar_...]
    another operation x7 -> x0, local copies, waits for them, and re-layouts: 4.14 us -> none
  transfers between devices with their start and end apart: 35 -> 35, of which waited for: 10 -> 11; matrix products, arithmetic and copies ran while one was open for 5% -> 4% of each run, Pallas kernels for 22% -> 21%
where the time goes in v3:
time: 251 us; the launch traced here: 250 us
  waiting for transfers between devices  121 us (48%)
  starting transfers between devices  60.3 us (24%)
  Pallas kernels  51.6 us (21%)
  local copies, waits for them, and re-layouts  12.2 us (5%)
  other arithmetic  3.26 us (1%)
    ppermute x32, waiting for transfers between devices, body(): send = lambda x, pairs: lax.ppermute(x, 'row', pairs)  118 us
    ppermute x32, starting transfers between devices, body(): send = lambda x, pairs: lax.ppermute(x, 'row', pairs)  58.1 us
    pallas_call x10, Pallas kernels, products(): pl.pallas_call(kernel, grid_spec=pltpu.PrefetchScalarGridSpec(num_scalar_...  43.9 us
    pallas_call x4, Pallas kernels, choose(): pl.pallas_call(kernel, grid_spec=pltpu.PrefetchScalarGridSpec(num_scalar_...  7.7 us
  transfers between devices with their start and end apart: 35, of which 11 were waited for; matrix products, arithmetic and copies ran while one was open for 4% of the time, Pallas kernels for 21%

profile of v3, /device:TPU:0, one launch (start us, length us, event | category | flops | bytes accessed | tf_op | source)
XLA Modules:
  0.0 250.2 jit_solution(7905681499230293103)
XLA Ops:
  0.0 1.3 fusion.33
  1.4 3.1 %collective-permute-start.22 = (f32[24,6144]{1,0:T(8,128)S(1)}, f32[24,6144]{1,0:T(8,128)S(1)}, u32[]{:S(2)}, u32[]{:S(2)}) collective-permute-start(f32[24,6144]{1,0:T(8,128)S(1)} %pad_maximum_fusion.2.refs_0_), channel_id=1, source_target_pairs={{0,4},{4,0},{8,12},{12,8},{16,20},{20,16},{24,28},{28,24},{1,5},{5... | collective-permute-start | bytes 1769480 | tf_op jit(solution)/shard_map/ppermute | solution.py:221
  4.5 1.5 collective-permute-start.2
  6.0 3.6 %collective-permute-start = (f32[24,6144]{1,0:T(8,128)S(1)}, f32[24,6144]{1,0:T(8,128)}, u32[]{:S(2)}, u32[]{:S(2)}) collective-permute-start(f32[24,6144]{1,0:T(8,128)S(1)} %pad_maximum_fusion.2.refs_0_), channel_id=1, source_target_pairs={{0,8},{4,12},{8,0},{12,4},{16,24},{20,28},{24,16},{28,20},{1,9},{5... | collective-permute-start | bytes 1769480 | tf_op jit(solution)/shard_map/ppermute | solution.py:221
  10.4 1.6 collective-permute-start.23
  12.0 1.8 fusion.32
  13.7 15.4 %collective-permute-done.14 = f32[24,5120]{1,0:T(8,128)S(1)} collective-permute-done((f32[24,5120]{1,0:T(8,128)S(1)}, f32[24,5120]{1,0:T(8,128)S(1)}, u32[]{:S(2)}, u32[]{:S(2)}) %collective-permute-start.14) | collective-permute-done | bytes 491552 | tf_op jit(solution)/shard_map/ppermute | solution.py:221
  29.9 9.0 %collective-permute-done.23.refs_1_ = f32[24,5120]{1,0:T(8,128)S(1)} collective-permute-done((f32[24,5120]{1,0:T(8,128)S(1)}, f32[24,5120]{1,0:T(8,128)S(1)}, u32[]{:S(2)}, u32[]{:S(2)}) %collective-permute-start.23) | collective-permute-done | bytes 491552 | tf_op jit(solution)/shard_map/ppermute | solution.py:221
  38.9 1.8 collective-permute-start.7
  40.8 5.2 %collective-permute-start.15 = (f32[48,2304]{1,0:T(8,128)S(1)}, f32[48,2304]{1,0:T(8,128)S(1)}, u32[]{:S(2)}, u32[]{:S(2)}) collective-permute-start(f32[48,2304]{1,0:T(8,128)S(1)} %slice.184.refs_0_.refs_1_), channel_id=1, source_target_pairs={{0,8},{4,12},{24,16},{28,20},{1,9},{5,13},{25,17},{29,21},{2,10},{... | collective-permute-start | bytes 1327112 | tf_op jit(solution)/shard_map/ppermute | solution.py:221
  46.0 6.2 %collective-permute-done.7.refs_2_ = f32[24,5120]{1,0:T(8,128)S(1)} collective-permute-done((f32[24,5120]{1,0:T(8,128)S(1)}, f32[24,5120]{1,0:T(8,128)S(1)}, u32[]{:S(2)}, u32[]{:S(2)}) %collective-permute-start.7) | collective-permute-done | bytes 491552 | tf_op jit(solution)/shard_map/ppermute | solution.py:221
  52.3 1.4 collective-permute-start.11
  53.7 1.5 collective-permute-start.8
  55.2 1.3 collective-permute-start.10
  56.5 1.6 pad_maximum_fusion
  58.1 6.7 %collective-permute-start.26 = (f32[256,2304]{1,0:T(8,128)}, f32[256,2304]{1,0:T(8,128)S(1)}, u32[]{:S(2)}, u32[]{:S(2)}) collective-permute-start(f32[256,2304]{1,0:T(8,128)} %pad_maximum_fusion), channel_id=1, source_target_pairs={{0,8},{4,12},{24,16},{28,20},{1,9},{5,13},{25,17},{29,21},{2,10},{... | collective-permute-start | bytes 7077896 | tf_op jit(solution)/shard_map/ppermute | solution.py:221
  65.6 1.5 collective-permute-start.4
  72.1 3.4 %collective-permute-start.19 = (f32[48,2816]{1,0:T(8,128)}, f32[48,2816]{1,0:T(8,128)}, u32[]{:S(2)}, u32[]{:S(2)}) collective-permute-start(f32[48,2816]{1,0:T(8,128)} %slice.188.refs_0_), channel_id=1, source_target_pairs={{0,8},{4,12},{8,0},{12,4},{16,24},{20,28},{24,16},{28,20},{1,9},{5... | collective-permute-start | bytes 1622024 | tf_op jit(solution)/shard_map/ppermute | solution.py:221
  75.5 1.3 collective-permute-start.6
  76.9 1.9 shard_map.85.refs_1_
  78.8 44.0 %collective-permute-done.19.refs_1_ = f32[48,2816]{1,0:T(8,128)} collective-permute-done((f32[48,2816]{1,0:T(8,128)}, f32[48,2816]{1,0:T(8,128)}, u32[]{:S(2)}, u32[]{:S(2)}) %collective-permute-start.19) | collective-permute-done | bytes 540704 | tf_op jit(solution)/shard_map/ppermute | solution.py:221
  123.8 1.6 collective-permute-start.16
  125.4 1.4 collective-permute-start.17
  126.8 1.9 shard_map.82.refs_1_
  129.7 7.4 %collective-permute-done.12.refs_2_ = f32[24,5120]{1,0:T(8,128)} collective-permute-done((f32[24,5120]{1,0:T(8,128)}, f32[24,5120]{1,0:T(8,128)}, u32[]{:S(2)}, u32[]{:S(2)}) %collective-permute-start.12) | collective-permute-done | bytes 491552 | tf_op jit(solution)/shard_map/ppermute | solution.py:221
  137.2 1.5 collective-permute-start.20
  140.0 1.9 shard_map.83.refs_3_
  144.0 28.0 %collective-permute-done.13.a_ref = f32[24,5120]{1,0:T(8,128)} collective-permute-done((f32[24,5120]{1,0:T(8,128)}, f32[24,5120]{1,0:T(8,128)}, u32[]{:S(2)}, u32[]{:S(2)}) %collective-permute-start.13) | collective-permute-done | bytes 491552 | tf_op jit(solution)/shard_map/ppermute | solution.py:221
  173.3 1.3 collective-permute-start.21
  174.6 2.0 shard_map.86.refs_3_
  178.5 4.6 %shard_map.91 = f32[3,12,128]{2,1,0:T(8,128)} custom-call(f32[24,5120]{1,0:T(8,128)} %copy-done.5, f32[24,5120]{1,0:T(8,128)} %copy-done.11, f32[24,5120]{1,0:T(8,128)} %copy-done.12, f32[128,32768]{1,0:T(8,128)} %refs_2_.5, f32[128,32768]{1,0:T(8,128)} %refs_2_.5), custom_call_target="tpu_custom_call" | custom-call | tf_op jit(solution)/shard_map/pallas_call | solution.py:97
  183.1 5.2 %shard_map.90 = f32[3,12,128]{2,1,0:T(8,128)} custom-call(f32[24,6144]{1,0:T(8,128)} %copy-done.2, f32[24,6144]{1,0:T(8,128)} %copy-done.7, f32[24,6144]{1,0:T(8,128)} %collective-permute-done.refs_2_, f32[128,32768]{1,0:T(8,128)} %refs_2_.5, f32[128,32768]{1,0:T(8,128)} %refs_2_.5), custom_call_target="tpu_custom_call" | custom-call | tf_op jit(solution)/shard_map/pallas_call | solution.py:97
  188.3 3.4 %shard_map.92 = f32[4,12,128]{2,1,0:T(8,128)} custom-call(f32[48,2816]{1,0:T(8,128)} %slice.188.refs_0_, f32[48,2816]{1,0:T(8,128)} %collective-permute-done.19.refs_1_, f32[128,32768]{1,0:T(8,128)} %refs_2_.5, f32[128,32768]{1,0:T(8,128)} %refs_2_.5), custom_call_target="tpu_custom_call" | custom-call | tf_op jit(solution)/shard_map/pallas_call | solution.py:97
  191.6 1.8 slice.185.refs_2_.refs_3_
  193.4 4.8 %shard_map.87 = f32[4,12,128]{2,1,0:T(8,128)} custom-call(f32[24,5120]{1,0:T(8,128)} %collective-permute-done.8.refs_0_, f32[24,5120]{1,0:T(8,128)} %shard_map.85.refs_1_, f32[24,5120]{1,0:T(8,128)} %collective-permute-done.12.refs_2_, f32[24,5120]{1,0:T(8,128)} %shard_map.86.refs_3_, f32[128,32768]{1,0:T(8,128)} %refs_2_.5, f32[128,32768]{1,0:T(8,128)} %refs_2_.5), custom_call_target="tpu_custom_call" | custom-call | tf_op jit(solution)/shard_map/pallas_call | solution.py:97
  198.3 3.7 %shard_map.88 = f32[8,12,128]{2,1,0:T(8,128)} custom-call(f32[48,2304]{1,0:T(8,128)} %copy-done.1, f32[48,2304]{1,0:T(8,128)} %copy-done.6, f32[48,2304]{1,0:T(8,128)} %slice.185.refs_2_.refs_3_, f32[48,2304]{1,0:T(8,128)} %collective-permute-done.17.refs_3_.refs_4_, f32[128,32768]{1,0:T(8,128)} %refs_2_.5, f32[128,32768]{1,0:T(8,128)} %refs_2_.5), custom_call_target="tpu_custom_call" | custom-call | tf_op jit(solution)/shard_map/pallas_call | solution.py:97
  202.0 5.3 %shard_map.84 = f32[4,12,128]{2,1,0:T(8,128)} custom-call(f32[24,6144]{1,0:T(8,128)} %collective-permute-done.1.refs_0_, f32[24,6144]{1,0:T(8,128)} %shard_map.82.refs_1_, f32[24,6144]{1,0:T(8,128)} %collective-permute-done.5.refs_2_, f32[24,6144]{1,0:T(8,128)} %shard_map.83.refs_3_, f32[128,32768]{1,0:T(8,128)} %refs_2_.5, f32[128,32768]{1,0:T(8,128)} %refs_2_.5), custom_call_target="tpu_custom_call" | custom-call | tf_op jit(solution)/shard_map/pallas_call | solution.py:97
  207.3 4.2 %shard_map.94 = f32[1,12,128]{2,1,0:T(8,128)} custom-call(f32[24,5120]{1,0:T(8,128)} %collective-permute-done.25.refs_0_, f32[128,32768]{1,0:T(8,128)} %refs_2_.5, f32[128,32768]{1,0:T(8,128)} %refs_2_.5), custom_call_target="tpu_custom_call" | custom-call | tf_op jit(solution)/shard_map/pallas_call | solution.py:97
  211.5 3.6 %shard_map.89 = f32[4,12,128]{2,1,0:T(8,128)} custom-call(s32[1]{0:T(128)} %bitcast.1.flag_ref.refs_0_, s32[1]{0:T(128)} %bitcast.2.flag_ref.refs_1_, f32[48,2816]{1,0:T(8,128)} %collective-permute-done.18.refs_2_, f32[48,2816]{1,0:T(8,128)} %collective-permute-done.20.refs_3_, f32[48,2816]{1,0:T(8,128)} %collective-permute-done.21.refs_4_, ...), custom_call_target="tpu_custom_call" | custom-call | tf_op jit(solution)/shard_map/pallas_call | solution.py:97
  215.1 1.4 copy-done
  216.5 4.3 %shard_map.95 = f32[8,12,128]{2,1,0:T(8,128)} custom-call(s32[8]{0:T(128)} %fusion.23.refs_0_, f32[48,2304]{1,0:T(8,128)} %copy-done.1, f32[48,2304]{1,0:T(8,128)} %copy-done.6, f32[48,2304]{1,0:T(8,128)} %slice.185.refs_2_.refs_3_, f32[48,2304]{1,0:T(8,128)} %collective-permute-done.17.refs_3_.refs_4_, f32[256,2304]{1,0:T(8,128)} %copy-done, ...), custom_call_target="tpu_custom_call" | custom-call | tf_op jit(solution)/shard_map/pallas_call | solution.py:97
  221.8 1.4 collective-permute-start.27
  224.1 4.7 %shard_map.93 = f32[1,12,128]{2,1,0:T(8,128)} custom-call(f32[24,6144]{1,0:T(8,128)} %copy-done.8, f32[128,32768]{1,0:T(8,128)} %refs_2_.5, f32[128,32768]{1,0:T(8,128)} %refs_2_.5), custom_call_target="tpu_custom_call" | custom-call | tf_op jit(solution)/shard_map/pallas_call | solution.py:97
  230.3 1.6 collective-permute-start.30
  233.5 2.1 collective-permute-done.29
  236.4 3.0 %collective-permute-done.31 = f32[25,128]{1,0:T(8,128)S(1)} collective-permute-done((f32[25,128]{1,0:T(8,128)S(1)}, f32[25,128]{1,0:T(8,128)S(1)}, u32[]{:S(2)}, u32[]{:S(2)}) %collective-permute-start.31) | collective-permute-done | bytes 12832 | tf_op jit(solution)/shard_map/ppermute | solution.py:221
  240.6 4.5 %collective-permute-start.33 = (f32[25,256]{1,0:T(8,128)S(1)}, f32[25,256]{1,0:T(8,128)S(1)}, u32[]{:S(2)}, u32[]{:S(2)}) collective-permute-start(f32[25,256]{1,0:T(8,128)S(1)} %pad_maximum_fusion.5), channel_id=1, source_target_pairs={{0,16},{4,20},{8,24},{12,28},{16,0},{20,4},{24,8},{28,12},{1,17},{... | collective-permute-start | bytes 76808 | tf_op jit(solution)/shard_map/ppermute | solution.py:221
  245.1 3.9 %collective-permute-done.32 = f32[25,256]{1,0:T(8,128)S(1)} collective-permute-done((f32[25,256]{1,0:T(8,128)S(1)}, f32[25,256]{1,0:T(8,128)S(1)}, u32[]{:S(2)}, u32[]{:S(2)}) %collective-permute-start.32) | collective-permute-done | bytes 25632 | tf_op jit(solution)/shard_map/ppermute | solution.py:221
  (125 shorter events, 23.9 us)
Async XLA Ops:
  1.4 52.3 %collective-permute-start.22 = (f32[24,6144]{1,0:T(8,128)S(1)}, f32[24,6144]{1,0:T(8,128)S(1)}, u32[]{:S(2)}, u32[]{:S(2)}) collective-permute-start(f32[24,6144]{1,0:T(8,128)S(1)} %pad_maximum_fusion.2.refs_0_), channel_id=1, source_target_pairs={{0,4},{4,0},{8,12},{12,8},{16,20},{20,16},{24,28},{28,24},{1,5},{5... | collective-permute-start | bytes 1769480 | tf_op jit(solution)/shard_map/ppermute | solution.py:221
  4.5 50.8 %collective-permute-start.2 = (f32[24,6144]{1,0:T(8,128)S(1)}, f32[24,6144]{1,0:T(8,128)}, u32[]{:S(2)}, u32[]{:S(2)}) collective-permute-start(f32[24,6144]{1,0:T(8,128)S(1)} %pad_maximum_fusion.2.refs_0_), channel_id=1, source_target_pairs={{8,16},{12,20},{16,8},{20,12},{9,17},{13,21},{17,9},{21,13},{10,18... | collective-permute-start | bytes 1769480 | tf_op jit(solution)/shard_map/ppermute | solution.py:221
  6.0 52.1 %collective-permute-start = (f32[24,6144]{1,0:T(8,128)S(1)}, f32[24,6144]{1,0:T(8,128)}, u32[]{:S(2)}, u32[]{:S(2)}) collective-permute-start(f32[24,6144]{1,0:T(8,128)S(1)} %pad_maximum_fusion.2.refs_0_), channel_id=1, source_target_pairs={{0,8},{4,12},{8,0},{12,4},{16,24},{20,28},{24,16},{28,20},{1,9},{5... | collective-permute-start | bytes 1769480 | tf_op jit(solution)/shard_map/ppermute | solution.py:221
  9.7 19.4 %collective-permute-start.14 = (f32[24,5120]{1,0:T(8,128)S(1)}, f32[24,5120]{1,0:T(8,128)S(1)}, u32[]{:S(2)}, u32[]{:S(2)}) collective-permute-start(f32[24,5120]{1,0:T(8,128)S(1)} %pad_maximum_fusion.4), channel_id=1, source_target_pairs={{0,4},{4,0},{8,12},{12,8},{16,20},{20,16},{24,28},{28,24},{1,5},{5... | collective-permute-start | bytes 1474568 | tf_op jit(solution)/shard_map/ppermute | solution.py:221
  10.4 28.5 %copy-start.5 = (f32[24,5120]{1,0:T(8,128)}, f32[24,5120]{1,0:T(8,128)S(1)}, u32[]{:S(2)}) copy-start(f32[24,5120]{1,0:T(8,128)S(1)} %pad_maximum_fusion.3.refs_0_) | copy-start | bytes 1474564
  10.4 28.5 %collective-permute-start.23 = (f32[24,5120]{1,0:T(8,128)S(1)}, f32[24,5120]{1,0:T(8,128)S(1)}, u32[]{:S(2)}, u32[]{:S(2)}) collective-permute-start(f32[24,5120]{1,0:T(8,128)S(1)} %pad_maximum_fusion.3.refs_0_), channel_id=1, source_target_pairs={{0,4},{4,0},{8,12},{12,8},{16,20},{20,16},{24,28},{28,24},{1,5},{5... | collective-permute-start | bytes 1474568 | tf_op jit(solution)/shard_map/ppermute | solution.py:221
  29.2 11.6 %collective-permute-start.9 = (f32[24,5120]{1,0:T(8,128)S(1)}, f32[24,5120]{1,0:T(8,128)S(1)}, u32[]{:S(2)}, u32[]{:S(2)}) collective-permute-start(f32[24,5120]{1,0:T(8,128)S(1)} %pad_maximum_fusion.3.refs_0_), channel_id=1, source_target_pairs={{8,16},{12,20},{16,8},{20,12},{9,17},{13,21},{17,9},{21,13},{10,18... | collective-permute-start | bytes 1474568 | tf_op jit(solution)/shard_map/ppermute | solution.py:221
  38.9 17.7 %copy-start.11 = (f32[24,5120]{1,0:T(8,128)}, f32[24,5120]{1,0:T(8,128)S(1)}, u32[]{:S(2)}) copy-start(f32[24,5120]{1,0:T(8,128)S(1)} %collective-permute-done.23.refs_1_) | copy-start | bytes 1474564
  38.9 13.4 %collective-permute-start.7 = (f32[24,5120]{1,0:T(8,128)S(1)}, f32[24,5120]{1,0:T(8,128)S(1)}, u32[]{:S(2)}, u32[]{:S(2)}) collective-permute-start(f32[24,5120]{1,0:T(8,128)S(1)} %pad_maximum_fusion.3.refs_0_), channel_id=1, source_target_pairs={{0,8},{4,12},{8,0},{12,4},{16,24},{20,28},{24,16},{28,20},{1,9},{5... | collective-permute-start | bytes 1474568 | tf_op jit(solution)/shard_map/ppermute | solution.py:221
  40.8 17.3 %copy-start.1 = (f32[48,2304]{1,0:T(8,128)}, f32[48,2304]{1,0:T(8,128)S(1)}, u32[]{:S(2)}) copy-start(f32[48,2304]{1,0:T(8,128)S(1)} %slice.184.refs_0_.refs_1_) | copy-start | bytes 1327108
  40.8 26.3 %copy-start.9 = (f32[24,5120]{1,0:T(8,128)}, f32[24,5120]{1,0:T(8,128)S(1)}, u32[]{:S(2)}) copy-start(f32[24,5120]{1,0:T(8,128)S(1)} %collective-permute-done.9.b_ref) | copy-start | bytes 1474564
  40.8 24.0 %collective-permute-start.15 = (f32[48,2304]{1,0:T(8,128)S(1)}, f32[48,2304]{1,0:T(8,128)S(1)}, u32[]{:S(2)}, u32[]{:S(2)}) collective-permute-start(f32[48,2304]{1,0:T(8,128)S(1)} %slice.184.refs_0_.refs_1_), channel_id=1, source_target_pairs={{0,8},{4,12},{24,16},{28,20},{1,9},{5,13},{25,17},{29,21},{2,10},{... | collective-permute-start | bytes 1327112 | tf_op jit(solution)/shard_map/ppermute | solution.py:221
  52.3 17.9 %copy-start.12 = (f32[24,5120]{1,0:T(8,128)}, f32[24,5120]{1,0:T(8,128)S(1)}, u32[]{:S(2)}) copy-start(f32[24,5120]{1,0:T(8,128)S(1)} %collective-permute-done.7.refs_2_) | copy-start | bytes 1474564
  52.3 17.9 %collective-permute-start.11 = (f32[24,5120]{1,0:T(8,128)S(1)}, f32[24,5120]{1,0:T(8,128)}, u32[]{:S(2)}, u32[]{:S(2)}) collective-permute-start(f32[24,5120]{1,0:T(8,128)S(1)} %collective-permute-done.7.refs_2_), channel_id=1, source_target_pairs={{8,16},{12,20},{16,8},{20,12},{9,17},{13,21},{17,9},{21,13},{10,18... | collective-permute-start | bytes 1474568 | tf_op jit(solution)/shard_map/ppermute | solution.py:221
  53.7 18.4 %collective-permute-start.8 = (f32[24,5120]{1,0:T(8,128)S(1)}, f32[24,5120]{1,0:T(8,128)}, u32[]{:S(2)}, u32[]{:S(2)}) collective-permute-start(f32[24,5120]{1,0:T(8,128)S(1)} %collective-permute-done.7.refs_2_), channel_id=1, source_target_pairs={{0,4},{4,0},{8,12},{12,8},{16,20},{20,16},{24,28},{28,24},{1,5},{5... | collective-permute-start | bytes 1474568 | tf_op jit(solution)/shard_map/ppermute | solution.py:221
  55.2 12.8 %collective-permute-start.10 = (f32[24,5120]{1,0:T(8,128)S(1)}, f32[24,5120]{1,0:T(8,128)S(1)}, u32[]{:S(2)}, u32[]{:S(2)}) collective-permute-start(f32[24,5120]{1,0:T(8,128)S(1)} %collective-permute-done.9.b_ref), channel_id=1, source_target_pairs={{8,0},{12,4},{16,24},{20,28},{9,1},{13,5},{17,25},{21,29},{10,2},{... | collective-permute-start | bytes 1474568 | tf_op jit(solution)/shard_map/ppermute | solution.py:221
  58.1 157.0 %collective-permute-start.26 = (f32[256,2304]{1,0:T(8,128)}, f32[256,2304]{1,0:T(8,128)S(1)}, u32[]{:S(2)}, u32[]{:S(2)}) collective-permute-start(f32[256,2304]{1,0:T(8,128)} %pad_maximum_fusion), channel_id=1, source_target_pairs={{0,8},{4,12},{24,16},{28,20},{1,9},{5,13},{25,17},{29,21},{2,10},{... | collective-permute-start | bytes 7077896 | tf_op jit(solution)/shard_map/ppermute | solution.py:221
  65.6 10.0 %collective-permute-start.4 = (f32[24,6144]{1,0:T(8,128)}, f32[24,6144]{1,0:T(8,128)}, u32[]{:S(2)}, u32[]{:S(2)}) collective-permute-start(f32[24,6144]{1,0:T(8,128)} %collective-permute-done.refs_2_), channel_id=1, source_target_pairs={{8,16},{12,20},{16,8},{20,12},{9,17},{13,21},{17,9},{21,13},{10,18... | collective-permute-start | bytes 1769480 | tf_op jit(solution)/shard_map/ppermute | solution.py:221
  68.9 55.0 %collective-permute-start.3 = (f32[24,6144]{1,0:T(8,128)}, f32[24,6144]{1,0:T(8,128)}, u32[]{:S(2)}, u32[]{:S(2)}) collective-permute-start(f32[24,6144]{1,0:T(8,128)} %collective-permute-done.2.b_ref), channel_id=1, source_target_pairs={{8,0},{12,4},{16,24},{20,28},{9,1},{13,5},{17,25},{21,29},{10,2},{... | collective-permute-start | bytes 1769480 | tf_op jit(solution)/shard_map/ppermute | solution.py:221
  70.2 55.3 %collective-permute-start.1 = (f32[24,6144]{1,0:T(8,128)}, f32[24,6144]{1,0:T(8,128)}, u32[]{:S(2)}, u32[]{:S(2)}) collective-permute-start(f32[24,6144]{1,0:T(8,128)} %collective-permute-done.refs_2_), channel_id=1, source_target_pairs={{0,4},{4,0},{8,12},{12,8},{16,20},{20,16},{24,28},{28,24},{1,5},{5... | collective-permute-start | bytes 1769480 | tf_op jit(solution)/shard_map/ppermute | solution.py:221
  72.1 50.7 %collective-permute-start.19 = (f32[48,2816]{1,0:T(8,128)}, f32[48,2816]{1,0:T(8,128)}, u32[]{:S(2)}, u32[]{:S(2)}) collective-permute-start(f32[48,2816]{1,0:T(8,128)} %slice.188.refs_0_), channel_id=1, source_target_pairs={{0,8},{4,12},{8,0},{12,4},{16,24},{20,28},{24,16},{28,20},{1,9},{5... | collective-permute-start | bytes 1622024 | tf_op jit(solution)/shard_map/ppermute | solution.py:221
  75.5 63.1 %collective-permute-start.6 = (f32[24,6144]{1,0:T(8,128)}, f32[24,6144]{1,0:T(8,128)}, u32[]{:S(2)}, u32[]{:S(2)}) collective-permute-start(f32[24,6144]{1,0:T(8,128)} %collective-permute-done.4.b_ref), channel_id=1, source_target_pairs={{8,0},{12,4},{16,24},{20,28},{9,1},{13,5},{17,25},{21,29},{10,2},{... | collective-permute-start | bytes 1769480 | tf_op jit(solution)/shard_map/ppermute | solution.py:221
  122.8 14.4 %collective-permute-start.12 = (f32[24,5120]{1,0:T(8,128)}, f32[24,5120]{1,0:T(8,128)}, u32[]{:S(2)}, u32[]{:S(2)}) collective-permute-start(f32[24,5120]{1,0:T(8,128)} %shard_map.85.refs_1_), channel_id=1, source_target_pairs={{0,4},{4,0},{8,12},{12,8},{16,20},{20,16},{24,28},{28,24},{1,5},{5... | collective-permute-start | bytes 1474568 | tf_op jit(solution)/shard_map/ppermute | solution.py:221
  123.8 18.1 %collective-permute-start.16 = (f32[48,5120]{1,0:T(8,128)S(1)}, f32[48,5120]{1,0:T(8,128)}, u32[]{:S(2)}, u32[]{:S(2)}) collective-permute-start(f32[48,5120]{1,0:T(8,128)S(1)} %pad_maximum_fusion.1), channel_id=1, source_target_pairs={{8,16},{12,20},{16,8},{20,12},{9,17},{13,21},{17,9},{21,13},{10,18... | collective-permute-start | bytes 2949128 | tf_op jit(solution)/shard_map/ppermute | solution.py:221
  125.4 3.3 %collective-permute-start.17 = (f32[48,2304]{1,0:T(8,128)}, f32[48,2304]{1,0:T(8,128)}, u32[]{:S(2)}, u32[]{:S(2)}) collective-permute-start(f32[48,2304]{1,0:T(8,128)} %copy-done.6), channel_id=1, source_target_pairs={{8,16},{12,20},{16,8},{20,12},{9,17},{13,21},{17,9},{21,13},{10,18... | collective-permute-start | bytes 1327112 | tf_op jit(solution)/shard_map/ppermute | solution.py:221
  128.7 47.8 %collective-permute-start.5 = (f32[24,6144]{1,0:T(8,128)}, f32[24,6144]{1,0:T(8,128)}, u32[]{:S(2)}, u32[]{:S(2)}) collective-permute-start(f32[24,6144]{1,0:T(8,128)} %shard_map.82.refs_1_), channel_id=1, source_target_pairs={{0,4},{4,0},{8,12},{12,8},{16,20},{20,16},{24,28},{28,24},{1,5},{5... | collective-permute-start | bytes 1769480 | tf_op jit(solution)/shard_map/ppermute | solution.py:221
  137.2 36.1 %collective-permute-start.20 = (f32[48,2816]{1,0:T(8,128)}, f32[48,2816]{1,0:T(8,128)}, u32[]{:S(2)}, u32[]{:S(2)}) collective-permute-start(f32[48,2816]{1,0:T(8,128)} %collective-permute-done.19.refs_1_), channel_id=1, source_target_pairs={{8,16},{12,20},{16,8},{20,12},{9,17},{13,21},{17,9},{21,13},{10,18... | collective-permute-start | bytes 1622024 | tf_op jit(solution)/shard_map/ppermute | solution.py:221
  138.7 33.4 %collective-permute-start.13 = (f32[24,5120]{1,0:T(8,128)}, f32[24,5120]{1,0:T(8,128)}, u32[]{:S(2)}, u32[]{:S(2)}) collective-permute-start(f32[24,5120]{1,0:T(8,128)} %collective-permute-done.11.b_ref), channel_id=1, source_target_pairs={{8,0},{12,4},{16,24},{20,28},{9,1},{13,5},{17,25},{21,29},{10,2},{... | collective-permute-start | bytes 1474568 | tf_op jit(solution)/shard_map/ppermute | solution.py:221
  139.9 37.9 %copy-start.26 = (s32[128]{0:T(128)S(1)}, s32[128]{0:T(128)}, u32[]{:S(2)}) copy-start(s32[128]{0:T(128)} %param.14) | copy-start | bytes 1540
  140.0 37.9 %copy-start.24 = (s32[1,8]{1,0:T(1,128)S(1)}, s32[1,8]{1,0:T(1,128)}, u32[]{:S(2)}) copy-start(s32[1,8]{1,0:T(1,128)} %constant.109) | copy-start | bytes 100
  140.0 37.9 %copy-start.25 = (s32[1,8]{1,0:T(1,128)S(1)}, s32[1,8]{1,0:T(1,128)}, u32[]{:S(2)}) copy-start(s32[1,8]{1,0:T(1,128)} %constant.108) | copy-start | bytes 100
  141.9 81.4 %collective-permute-start.24 = (f32[24,6144]{1,0:T(8,128)}, f32[24,6144]{1,0:T(8,128)S(1)}, u32[]{:S(2)}, u32[]{:S(2)}) collective-permute-start(f32[24,6144]{1,0:T(8,128)} %shard_map.83.refs_3_), channel_id=1, source_target_pairs={{0,4},{4,0},{8,12},{12,8},{16,20},{20,16},{24,28},{28,24},{1,5},{5... | collective-permute-start | bytes 1769480 | tf_op jit(solution)/shard_map/ppermute | solution.py:221
  144.0 39.1 %copy-start.3 = (f32[48,2816]{1,0:T(8,128)}, f32[48,2816]{1,0:T(8,128)S(1)}, u32[]{:S(2)}) copy-start(f32[48,2816]{1,0:T(8,128)S(1)} %slice.187.refs_5_) | copy-start | bytes 1622020
  172.0 39.5 %collective-permute-start.18 = (f32[48,2816]{1,0:T(8,128)S(1)}, f32[48,2816]{1,0:T(8,128)}, u32[]{:S(2)}, u32[]{:S(2)}) collective-permute-start(f32[48,2816]{1,0:T(8,128)S(1)} %slice.187.refs_5_), channel_id=1, source_target_pairs={{8,0},{12,4},{16,24},{20,28},{9,1},{13,5},{17,25},{21,29},{10,2},{... | collective-permute-start | bytes 1622024 | tf_op jit(solution)/shard_map/ppermute | solution.py:221
  173.3 38.2 %collective-permute-start.21 = (f32[48,2816]{1,0:T(8,128)}, f32[48,2816]{1,0:T(8,128)}, u32[]{:S(2)}, u32[]{:S(2)}) collective-permute-start(f32[48,2816]{1,0:T(8,128)} %collective-permute-done.20.refs_3_), channel_id=1, source_target_pairs={{8,0},{12,4},{16,24},{20,28},{9,1},{13,5},{17,25},{21,29},{10,2},{... | collective-permute-start | bytes 1622024 | tf_op jit(solution)/shard_map/ppermute | solution.py:221
  176.6 30.7 %collective-permute-start.25 = (f32[24,5120]{1,0:T(8,128)}, f32[24,5120]{1,0:T(8,128)}, u32[]{:S(2)}, u32[]{:S(2)}) collective-permute-start(f32[24,5120]{1,0:T(8,128)} %shard_map.86.refs_3_), channel_id=1, source_target_pairs={{0,4},{4,0},{8,12},{12,8},{16,20},{20,16},{24,28},{28,24},{1,5},{5... | collective-permute-start | bytes 1474568 | tf_op jit(solution)/shard_map/ppermute | solution.py:221
  221.8 10.6 %copy-start.27 = (s32[128]{0:T(128)S(1)}, s32[128]{0:T(128)}, u32[]{:S(2)}) copy-start(s32[128]{0:T(128)} %param.13) | copy-start | bytes 1540
  221.8 13.8 %copy-start.21 = (f32[128]{0:T(128)S(1)}, f32[128]{0:T(128)}, u32[]{:S(2)}) copy-start(f32[128]{0:T(128)} %param.12) | copy-start | bytes 1540
  221.8 13.8 %copy-start.22 = (f32[128]{0:T(128)S(1)}, f32[128]{0:T(128)}, u32[]{:S(2)}) copy-start(f32[128]{0:T(128)} %param.11) | copy-start | bytes 1540
  221.8 13.8 %copy-start.23 = (f32[128]{0:T(128)S(1)}, f32[128]{0:T(128)}, u32[]{:S(2)}) copy-start(f32[128]{0:T(128)} %param.10) | copy-start | bytes 1540
  221.8 8.3 %collective-permute-start.27 = (f32[96,128]{1,0:T(8,128)S(1)}, f32[96,128]{1,0:T(8,128)S(1)}, u32[]{:S(2)}, u32[]{:S(2)}) collective-permute-start(f32[96,128]{1,0:T(8,128)S(1)} %reshape.107), channel_id=1, source_target_pairs={{8,0},{12,4},{16,24},{20,28},{9,1},{13,5},{17,25},{21,29},{10,2},{... | collective-permute-start | bytes 147464 | tf_op jit(solution)/shard_map/ppermute | solution.py:221
  230.2 2.2 collective-permute-start.28
  230.3 3.2 %collective-permute-start.30 = (f32[24,128]{1,0:T(8,128)S(1)}, f32[24,128]{1,0:T(8,128)S(1)}, u32[]{:S(2)}, u32[]{:S(2)}) collective-permute-start(f32[24,128]{1,0:T(8,128)S(1)} %get-tuple-element.40), channel_id=1, source_target_pairs={{0,3},{1,2},{2,1},{3,0},{4,7},{5,6},{6,5},{7,4},{8,11},{9,10},{10,... | collective-permute-start | bytes 36872 | tf_op jit(solution)/shard_map/ppermute | solution.py:339
  231.9 3.7 %collective-permute-start.29 = (f32[24,128]{1,0:T(8,128)S(1)}, f32[24,128]{1,0:T(8,128)S(1)}, u32[]{:S(2)}, u32[]{:S(2)}) collective-permute-start(f32[24,128]{1,0:T(8,128)S(1)} %get-tuple-element.41), channel_id=1, source_target_pairs={{0,2},{1,3},{2,0},{3,1},{4,6},{5,7},{6,4},{7,5},{8,10},{9,11},{10,... | collective-permute-start | bytes 36872 | tf_op jit(solution)/shard_map/ppermute | solution.py:339
  235.6 3.8 %collective-permute-start.31 = (f32[25,128]{1,0:T(8,128)S(1)}, f32[25,128]{1,0:T(8,128)S(1)}, u32[]{:S(2)}, u32[]{:S(2)}) collective-permute-start(f32[25,128]{1,0:T(8,128)S(1)} %get-tuple-element.42), channel_id=1, source_target_pairs={{0,4},{4,0},{8,12},{12,8},{16,20},{20,16},{24,28},{28,24},{1,5},{5... | collective-permute-start | bytes 38408 | tf_op jit(solution)/shard_map/ppermute | solution.py:221
  239.4 9.6 %collective-permute-start.34 = (f32[25,256]{1,0:T(8,128)S(1)}, f32[25,256]{1,0:T(8,128)S(1)}, u32[]{:S(2)}, u32[]{:S(2)}) collective-permute-start(f32[25,256]{1,0:T(8,128)S(1)} %pad_maximum_fusion.5), channel_id=1, source_target_pairs={{0,24},{4,28},{8,16},{12,20},{16,8},{20,12},{24,0},{28,4},{1,25},{... | collective-permute-start | bytes 76808 | tf_op jit(solution)/shard_map/ppermute | solution.py:221
  240.6 8.4 %collective-permute-start.33 = (f32[25,256]{1,0:T(8,128)S(1)}, f32[25,256]{1,0:T(8,128)S(1)}, u32[]{:S(2)}, u32[]{:S(2)}) collective-permute-start(f32[25,256]{1,0:T(8,128)S(1)} %pad_maximum_fusion.5), channel_id=1, source_target_pairs={{0,16},{4,20},{8,24},{12,28},{16,0},{20,4},{24,8},{28,12},{1,17},{... | collective-permute-start | bytes 76808 | tf_op jit(solution)/shard_map/ppermute | solution.py:221
  245.1 3.9 %collective-permute-start.32 = (f32[25,256]{1,0:T(8,128)S(1)}, f32[25,256]{1,0:T(8,128)S(1)}, u32[]{:S(2)}, u32[]{:S(2)}) collective-permute-start(f32[25,256]{1,0:T(8,128)S(1)} %pad_maximum_fusion.5), channel_id=1, source_target_pairs={{0,8},{4,12},{8,0},{12,4},{16,24},{20,28},{24,16},{28,20},{1,9},{5... | collective-permute-start | bytes 76808 | tf_op jit(solution)/shard_map/ppermute | solution.py:221
  (15 other events, 80.9 us)

commit v4 on v3

--- a/solution.py
+++ b/solution.py
@@ -26,10 +26,9 @@
     return LANE * max(d for d in range(1, 29) if tiles % d == 0 and (d < tiles or tiles == 1))
 
 
-def products(blocks, factors, starts, rows, band, order=None):
+def products(blocks, factors, starts, rows, band, width, order=None, resident=False):
     folds = len(factors)
     arrays, specs, flags, places = [], [], [], []
-    width = (blocks[0][1] if isinstance(blocks[0], tuple) else blocks[0]).shape[1]
     tk = step_width(width)
     steps = width // tk
     total = 0
@@ -51,7 +50,10 @@
     groups = total // (folds * rows)
     scalars = flags + ([] if order is None else [order])
 
-    for fold in range(folds):
+    if resident:
+        specs.append(pl.BlockSpec(memory_space=pltpu.VMEM))
+        factors = factors[:1]
+    for fold in range(0 if resident else folds):
         top, left = starts[fold]
         specs.append(
             pl.BlockSpec(
@@ -82,7 +84,12 @@
             taken += [block[top : top + folds * rows] for top in range(0, block.shape[0], folds * rows)]
         for fold in range(folds):
             hi, lo = split_bf16(jnp.concatenate([t[lows[fold] : lows[fold] + tall] for t in taken], axis=0))
-            f_hi, f_lo = split_bf16(factor_refs[fold][...])
+            if resident:
+                top, left = starts[fold]
+                strip = factor_refs[0][top : top + band, pl.ds(pl.multiple_of(left + step * tk, LANE), tk)]
+            else:
+                strip = factor_refs[fold][...]
+            f_hi, f_lo = split_bf16(strip)
             first = dot_t(jnp.concatenate([hi, lo], axis=0), f_hi)
             acc[fold] += first[: groups * tall] + (first[groups * tall :] + dot_t(hi, f_lo))
 
@@ -154,17 +161,17 @@
         near = slots(0) + (("y", 0),) + slots(1)
         inner = (("y", 1),) + slots(2) + (("y", 2),) + slots(3)
         return (
-            [("bx", "y", 0), ("0", "e", 1), ("0", "m", 1), ("1", "e", 1), ("0", "y", 0), ("1", "m", 1), ("1", "y", 0)]
+            [("0", "e", 1), ("0", "m", 1), ("bx", "y", 0), ("1", "e", 1), ("0", "y", 0), ("1", "m", 1), ("1", "y", 0)]
             + [("b", "e", 1), ("x", "e", 1), ("x", "f", 0)]
             + [("0", "y", 1), ("0", "m", 2), ("0", "e", 2), ("0", "mul", near)]
             + [("1", "y", 1), ("1", "m", 2), ("1", "e", 2), ("bx", "m", 1), ("1", "mul", near)]
-            + [("b", "m", 2), ("x", "m", 2), ("b", "mul", slots(0, 1))]
+            + [("x", "m", 2), ("b", "m", 2)]
             + [("0", "sel", 2), ("0", "y", 2), ("0", "e", 3)]
-            + [("1", "sel", 2), ("1", "y", 2), ("1", "e", 3), ("b", "e", 2)]
-            + [("0", "sel", 3), ("0", "y", 3), ("0", "mul", inner)]
-            + [("1", "sel", 3), ("1", "y", 3), ("b", "e", 3), ("1", "mul", inner)]
-            + [("x", "mul", "own"), ("x", "mul", "far"), ("x", "back", 0)]
-            + [("0", "mul", (("y", 3),)), ("b", "mul", slots(2, 3)), ("1", "mul", (("y", 3),))]
+            + [("1", "sel", 2), ("1", "y", 2), ("1", "e", 3), ("b", "mul", slots(0, 1)), ("b", "e", 2)]
+            + [("0", "sel", 3), ("0", "y", 3), ("0", "mul", inner), ("x", "mul", "own")]
+            + [("1", "sel", 3), ("1", "y", 3), ("b", "e", 3)]
+            + [("x", "mul", "far"), ("x", "back", 0), ("0", "mul", (("y", 3),)), ("b", "mul", slots(2, 3))]
+            + [("1", "mul", inner + (("y", 3),))]
         )
     chunks = [str(c) for c in range(CHUNKS)]
     last = planes - 1
@@ -236,7 +243,7 @@
     pairs_of = lambda share: 2 * round(tiles * share / 2)
     sizes = {"x": pairs_of(18 / 128), "b": pairs_of(22 / 128)} if exports(planes) else {"b": pairs_of(20 / 128)}
     rest = tiles - sum(sizes.values())
-    sizes["1"] = 2 * (rest * 5 // 22)
+    sizes["1"] = 2 * (rest * 9 // 44)
     sizes["0"] = rest - sizes["1"]
     begin, at = {}, 0
     for stream in sizes:
@@ -250,7 +257,7 @@
             [turned[:, f * stride + start : f * stride + start + width] for f in range(folds)], axis=0
         )
 
-    own = {stream: piece(stream) for stream in ("bx", "0", "1")}
+    own = {stream: piece(stream) for stream in ("0", "bx", "1")}
     have = {(stream, "slot", 0): own[stream] for stream in ("0", "1")}
     parts = [[[], []] for _ in range(planes)]
 
@@ -268,23 +275,20 @@
             else:
                 blocks.append(have[stream, kind, j])
             places += [(j, 0), (j, 1)] if stream == "b" else [(j, int(kind == "y"))]
-        got = products(blocks, [factor_band] * folds, starts_of(stream), rows, band)
+        got = products(blocks, [factor_band] * folds, starts_of(stream), rows, band, sizes[stream] * LANE)
         for g, (j, q) in enumerate(places):
             parts[j][q].append(got[g])
 
     def multiply_exported(whose):
-        blocks = [have["x", "slot", 0], have["x", "e", 1], have["x", "m", 1], have["x", "m", 2]]
+        blocks = [have["x", "slot", 0], have["x", "e", 1], have["bx", "m", 1], have["x", "m", 2]]
         places = [(j % planes, q) for j in (0, 1, -1, -2) for q in (0, 1)]
-        if whose == "own":
-            got = products(blocks, [factor_band] * folds, starts_of("x"), rows, band)
-            for g, (j, q) in enumerate(places):
-                parts[j][q].append(jnp.where(outer, 0.0, got[g]))
-        else:
-            slot, other = jnp.array(places, jnp.int32).T
-            order = 2 * jnp.mod(z + heading * slot, planes) + (y + other) % 2
-            have["x", "far", 0] = products(
-                blocks, [have["x", "f", 0]] * folds, [(f * band, 0) for f in range(folds)], rows, band, order
-            ).reshape(row_size * rows, band)
+        slot, other = jnp.array(places, jnp.int32).T
+        order = 2 * jnp.mod(z + heading * slot, planes) + (y + other) % 2
+        factors, starts = [factor_band] * folds, starts_of("x")
+        if whose == "far":
+            factors, starts = [have["x", "f", 0]] * folds, [(f * band, 0) for f in range(folds)]
+        sums = products(blocks, factors, starts, rows, band, sizes["x"] * LANE, order, whose == "far")
+        have["x", whose, 0] = sums.reshape(row_size * rows, band)
 
     def place(sums):
         placed = []
@@ -329,7 +333,7 @@
 
     total = place([[sum(terms) for terms in pair] for pair in parts])
     if exports(planes):
-        total = total + jnp.where(outer, back, 0.0)
+        total = total + jnp.where(outer, back, have["x", "own", 0])
     share = rows * row_size // col_size
     total = total.reshape(col_size, share, band)
 

time: 251 us -> 241 us (0.960)
  local copies, waits for them, and re-layouts: 12.2 us -> 7.99 us
  Pallas kernels: 51.6 us -> 48.8 us
    slice x4 -> x3, local copies, waits for them, and re-layouts: 3.78 us -> 0.1 us  [cut(): return block[:, begin[stream]:begin[stream] + sizes[stream] * LANE]]
    pallas_call x10 -> x9, Pallas kernels: 43.9 us -> 41.1 us  [products(): pl.pallas_call(kernel, grid_spec=pltpu.PrefetchScalarGridSpec(num_scalar_...]
  transfers between devices with their start and end apart: 35 -> 35, of which waited for: 11 -> 13; matrix products, arithmetic and copies ran while one was open for 4% -> 3% of each run, Pallas kernels for 21% -> 20%
where the time goes in v4:
time: 241 us; the launch traced here: 240 us
  waiting for transfers between devices  119 us (49%)
  starting transfers between devices  59.5 us (25%)
  Pallas kernels  48.8 us (20%)
  local copies, waits for them, and re-layouts  7.99 us (3%)
  other arithmetic  3.2 us (1%)
    ppermute x32, waiting for transfers between devices, body(): send = lambda x, pairs: lax.ppermute(x, 'row', pairs)  117 us
    ppermute x32, starting transfers between devices, body(): send = lambda x, pairs: lax.ppermute(x, 'row', pairs)  57.6 us
    pallas_call x9, Pallas kernels, products(): pl.pallas_call(kernel, grid_spec=pltpu.PrefetchScalarGridSpec(num_scalar_...  41.1 us
    pallas_call x4, Pallas kernels, choose(): pl.pallas_call(kernel, grid_spec=pltpu.PrefetchScalarGridSpec(num_scalar_...  7.71 us
  transfers between devices with their start and end apart: 35, of which 13 were waited for; matrix products, arithmetic and copies ran while one was open for 3% of the time, Pallas kernels for 20%

profile of v4, /device:TPU:0, one launch (start us, length us, event | category | flops | bytes accessed | tf_op | source)
XLA Modules:
  0.0 240.2 jit_solution(9235979003112670389)
XLA Ops:
  1.3 3.1 %collective-permute-start.22 = (f32[24,4608]{1,0:T(8,128)S(1)}, f32[24,4608]{1,0:T(8,128)S(1)}, u32[]{:S(2)}, u32[]{:S(2)}) collective-permute-start(f32[24,4608]{1,0:T(8,128)S(1)} %pad_maximum_fusion.4.refs_0_), channel_id=1, source_target_pairs={{0,4},{4,0},{8,12},{12,8},{16,20},{20,16},{24,28},{28,24},{1,5},{5... | collective-permute-start | bytes 1327112 | tf_op jit(solution)/shard_map/ppermute | solution.py:228
  4.4 1.6 collective-permute-start.13
  6.8 2.0 collective-permute-start.7
  8.8 1.8 fusion.18
  10.6 4.8 %collective-permute-done.22.refs_1_ = f32[24,4608]{1,0:T(8,128)S(1)} collective-permute-done((f32[24,4608]{1,0:T(8,128)S(1)}, f32[24,4608]{1,0:T(8,128)S(1)}, u32[]{:S(2)}, u32[]{:S(2)}) %collective-permute-start.22) | collective-permute-done | bytes 442400 | tf_op jit(solution)/shard_map/ppermute | solution.py:228
  16.1 22.7 %collective-permute-done.7 = f32[24,5120]{1,0:T(8,128)S(1)} collective-permute-done((f32[24,5120]{1,0:T(8,128)S(1)}, f32[24,5120]{1,0:T(8,128)S(1)}, u32[]{:S(2)}, u32[]{:S(2)}) %collective-permute-start.7) | collective-permute-done | bytes 491552 | tf_op jit(solution)/shard_map/ppermute | solution.py:228
  38.8 1.5 collective-permute-start.2
  40.5 1.8 collective-permute-start.14
  42.3 1.4 collective-permute-start.17
  45.0 6.5 %collective-permute-start.24 = (f32[48,2304]{1,0:T(8,128)S(1)}, f32[48,2304]{1,0:T(8,128)S(1)}, u32[]{:S(2)}, u32[]{:S(2)}) collective-permute-start(f32[48,2304]{1,0:T(8,128)S(1)} %slice.175.refs_1_), channel_id=1, source_target_pairs={{0,8},{4,12},{24,16},{28,20},{1,9},{5,13},{25,17},{29,21},{2,10},{... | collective-permute-start | bytes 1327112 | tf_op jit(solution)/shard_map/ppermute | solution.py:228
  51.5 1.6 pad_maximum_fusion
  53.1 10.0 %collective-permute-start.26 = (f32[256,2304]{1,0:T(8,128)}, f32[256,2304]{1,0:T(8,128)}, u32[]{:S(2)}, u32[]{:S(2)}) collective-permute-start(f32[256,2304]{1,0:T(8,128)} %pad_maximum_fusion), channel_id=1, source_target_pairs={{0,8},{4,12},{24,16},{28,20},{1,9},{5,13},{25,17},{29,21},{2,10},{... | collective-permute-start | bytes 7077896 | tf_op jit(solution)/shard_map/ppermute | solution.py:228
  63.3 1.6 collective-permute-start.1
  64.8 1.3 collective-permute-start.3
  66.2 1.5 collective-permute-start.4
  67.7 1.9 shard_map.95.refs_1_
  69.6 51.8 %collective-permute-done.10.refs_1_ = f32[48,2816]{1,0:T(8,128)} collective-permute-done((f32[48,2816]{1,0:T(8,128)S(1)}, f32[48,2816]{1,0:T(8,128)}, u32[]{:S(2)}, u32[]{:S(2)}) %collective-permute-start.10) | collective-permute-done | bytes 540704 | tf_op jit(solution)/shard_map/ppermute | solution.py:228
  122.6 1.3 collective-permute-start.19
  124.6 5.4 %collective-permute-done.18.refs_2_ = f32[24,4608]{1,0:T(8,128)} collective-permute-done((f32[24,4608]{1,0:T(8,128)}, f32[24,4608]{1,0:T(8,128)}, u32[]{:S(2)}, u32[]{:S(2)}) %collective-permute-start.18) | collective-permute-done | bytes 442400 | tf_op jit(solution)/shard_map/ppermute | solution.py:228
  131.3 9.2 %collective-permute-done.19.a_ref = f32[24,4608]{1,0:T(8,128)} collective-permute-done((f32[24,4608]{1,0:T(8,128)}, f32[24,4608]{1,0:T(8,128)}, u32[]{:S(2)}, u32[]{:S(2)}) %collective-permute-start.19) | collective-permute-done | bytes 442400 | tf_op jit(solution)/shard_map/ppermute | solution.py:228
  140.5 1.5 collective-permute-start.11
  142.0 1.9 shard_map.96.refs_3_
  143.9 1.6 collective-permute-start.20
  145.5 1.9 shard_map.91.refs_1_
  147.4 1.6 collective-permute-done.6.a_ref
  149.0 1.7 collective-permute-start.5
  150.8 2.0 shard_map.92.refs_3_
  153.2 1.3 collective-permute-start.9
  154.5 2.8 %collective-permute-done.20.refs_4_ = f32[24,4608]{1,0:T(8,128)} collective-permute-done((f32[24,4608]{1,0:T(8,128)}, f32[24,4608]{1,0:T(8,128)}, u32[]{:S(2)}, u32[]{:S(2)}) %collective-permute-start.20) | collective-permute-done | bytes 442400 | tf_op jit(solution)/shard_map/ppermute | solution.py:228
  159.3 4.4 %shard_map.99 = f32[3,12,128]{2,1,0:T(8,128)} custom-call(f32[24,4608]{1,0:T(8,128)} %copy-done.8, f32[24,4608]{1,0:T(8,128)} %copy-done.16, f32[24,4608]{1,0:T(8,128)} %copy-done.17, f32[128,32768]{1,0:T(8,128)} %refs_6_.5, f32[128,32768]{1,0:T(8,128)} %refs_6_.5), custom_call_target="tpu_custom_call" | custom-call | tf_op jit(solution)/shard_map/pallas_call | solution.py:104
  163.7 5.5 %shard_map.98 = f32[3,12,128]{2,1,0:T(8,128)} custom-call(f32[24,6656]{1,0:T(8,128)} %copy-done.2, f32[24,6656]{1,0:T(8,128)} %copy-done.9, f32[24,6656]{1,0:T(8,128)} %collective-permute-done.refs_2_, f32[128,32768]{1,0:T(8,128)} %refs_6_.5, f32[128,32768]{1,0:T(8,128)} %refs_6_.5), custom_call_target="tpu_custom_call" | custom-call | tf_op jit(solution)/shard_map/pallas_call | solution.py:104
  169.1 3.4 %shard_map.100 = f32[4,12,128]{2,1,0:T(8,128)} custom-call(f32[48,2816]{1,0:T(8,128)} %copy-done.3, f32[48,2816]{1,0:T(8,128)} %collective-permute-done.10.refs_1_, f32[128,32768]{1,0:T(8,128)} %refs_6_.5, f32[128,32768]{1,0:T(8,128)} %refs_6_.5), custom_call_target="tpu_custom_call" | custom-call | tf_op jit(solution)/shard_map/pallas_call | solution.py:104
  172.5 4.4 %shard_map.103 = f32[8,12,128]{2,1,0:T(8,128)} custom-call(s32[8]{0:T(128)} %fusion.14.refs_0_, f32[48,2304]{1,0:T(8,128)} %copy-done.1, f32[48,2304]{1,0:T(8,128)} %copy-done.6, f32[48,5120]{1,0:T(8,128)} %copy-done, f32[48,2304]{1,0:T(8,128)} %copy-done.7, f32[128,32768]{1,0:T(8,128)} %refs_6_.5, f32[128,32768]{1,0:T(8,128)} %refs_6_.5), custom_call_target="tpu_custom_call" | custom-call | tf_op jit(solution)/shard_map/pallas_call | solution.py:104
  177.7 4.7 %shard_map.97 = f32[5,12,128]{2,1,0:T(8,128)} custom-call(f32[24,4608]{1,0:T(8,128)} %copy-done.13, f32[24,4608]{1,0:T(8,128)} %shard_map.95.refs_1_, f32[24,4608]{1,0:T(8,128)} %collective-permute-done.18.refs_2_, f32[24,4608]{1,0:T(8,128)} %shard_map.96.refs_3_, f32[24,4608]{1,0:T(8,128)} %collective-permute-done.20.refs_4_, f32[128,32768]{1,0:T(8,128)} %refs_6_.5, ...), custom_call_target="tpu_custom_call" | custom-call | tf_op jit(solution)/shard_map/pallas_call | solution.py:104
  183.2 5.6 %shard_map.93 = f32[4,12,128]{2,1,0:T(8,128)} custom-call(f32[24,6656]{1,0:T(8,128)} %collective-permute-done.1.refs_0_, f32[24,6656]{1,0:T(8,128)} %shard_map.91.refs_1_, f32[24,6656]{1,0:T(8,128)} %copy-done.11, f32[24,6656]{1,0:T(8,128)} %shard_map.92.refs_3_, f32[128,32768]{1,0:T(8,128)} %refs_6_.5, f32[128,32768]{1,0:T(8,128)} %refs_6_.5), custom_call_target="tpu_custom_call" | custom-call | tf_op jit(solution)/shard_map/pallas_call | solution.py:104
  189.6 3.6 %shard_map.94 = f32[4,12,128]{2,1,0:T(8,128)} custom-call(s32[1]{0:T(128)} %bitcast.1.flag_ref.refs_0_, s32[1]{0:T(128)} %bitcast.2.flag_ref.refs_1_, f32[48,2816]{1,0:T(8,128)} %copy-done.12, f32[48,2816]{1,0:T(8,128)} %collective-permute-done.11.refs_3_, f32[48,2816]{1,0:T(8,128)} %collective-permute-done.12.refs_4_, f32[48,2816]{1,0:T(8,128)} %copy-done.4, ...), custom_call_target="tpu_custom_call" | custom-call | tf_op jit(solution)/shard_map/pallas_call | solution.py:104
  193.2 4.8 %shard_map.102 = f32[8,12,128]{2,1,0:T(8,128)} custom-call(s32[8]{0:T(128)} %fusion.14.refs_0_, f32[48,2304]{1,0:T(8,128)} %copy-done.1, f32[48,2304]{1,0:T(8,128)} %copy-done.6, f32[48,5120]{1,0:T(8,128)} %copy-done, f32[48,2304]{1,0:T(8,128)} %copy-done.7, f32[256,2304]{1,0:T(8,128)} %collective-permute-done.26.refs_5_), custom_call_target="tpu_custom_call" | custom-call | tf_op jit(solution)/shard_map/pallas_call | solution.py:104
  198.9 1.4 collective-permute-start.27
  201.2 4.9 %shard_map.101 = f32[1,12,128]{2,1,0:T(8,128)} custom-call(f32[24,6656]{1,0:T(8,128)} %copy-done.10, f32[128,32768]{1,0:T(8,128)} %refs_6_.5, f32[128,32768]{1,0:T(8,128)} %refs_6_.5), custom_call_target="tpu_custom_call" | custom-call | tf_op jit(solution)/shard_map/pallas_call | solution.py:104
  207.4 12.0 %collective-permute-done.27 = f32[96,128]{1,0:T(8,128)S(1)} collective-permute-done((f32[96,128]{1,0:T(8,128)S(1)}, f32[96,128]{1,0:T(8,128)S(1)}, u32[]{:S(2)}, u32[]{:S(2)}) %collective-permute-start.27) | collective-permute-done | bytes 49184 | tf_op jit(solution)/shard_map/ppermute | solution.py:228
  219.6 1.5 collective-permute-start.29
  221.4 1.3 collective-permute-done.30
  223.4 1.6 collective-permute-start.31
  225.0 2.2 collective-permute-done.31
  227.2 5.1 %collective-permute-start.32 = (f32[25,256]{1,0:T(8,128)S(1)}, f32[25,256]{1,0:T(8,128)S(1)}, u32[]{:S(2)}, u32[]{:S(2)}) collective-permute-start(f32[25,256]{1,0:T(8,128)S(1)} %pad_maximum_fusion.5), channel_id=1, source_target_pairs={{0,8},{4,12},{8,0},{12,4},{16,24},{20,28},{24,16},{28,20},{1,9},{5... | collective-permute-start | bytes 76808 | tf_op jit(solution)/shard_map/ppermute | solution.py:228
  233.4 1.4 collective-permute-start.34
  234.8 2.9 %collective-permute-done.33 = f32[25,256]{1,0:T(8,128)S(1)} collective-permute-done((f32[25,256]{1,0:T(8,128)S(1)}, f32[25,256]{1,0:T(8,128)S(1)}, u32[]{:S(2)}, u32[]{:S(2)}) %collective-permute-start.33) | collective-permute-done | bytes 25632 | tf_op jit(solution)/shard_map/ppermute | solution.py:228
  237.7 1.4 collective-permute-done.34
  (131 shorter events, 18.5 us)
Async XLA Ops:
  1.3 14.1 %collective-permute-start.22 = (f32[24,4608]{1,0:T(8,128)S(1)}, f32[24,4608]{1,0:T(8,128)S(1)}, u32[]{:S(2)}, u32[]{:S(2)}) collective-permute-start(f32[24,4608]{1,0:T(8,128)S(1)} %pad_maximum_fusion.4.refs_0_), channel_id=1, source_target_pairs={{0,4},{4,0},{8,12},{12,8},{16,20},{20,16},{24,28},{28,24},{1,5},{5... | collective-permute-start | bytes 1327112 | tf_op jit(solution)/shard_map/ppermute | solution.py:228
  4.4 36.1 %collective-permute-start.13 = (f32[24,4608]{1,0:T(8,128)S(1)}, f32[24,4608]{1,0:T(8,128)S(1)}, u32[]{:S(2)}, u32[]{:S(2)}) collective-permute-start(f32[24,4608]{1,0:T(8,128)S(1)} %pad_maximum_fusion.4.refs_0_), channel_id=1, source_target_pairs={{0,8},{4,12},{8,0},{12,4},{16,24},{20,28},{24,16},{28,20},{1,9},{5... | collective-permute-start | bytes 1327112 | tf_op jit(solution)/shard_map/ppermute | solution.py:228
  6.1 32.7 %copy-start.2 = (f32[24,6656]{1,0:T(8,128)}, f32[24,6656]{1,0:T(8,128)S(1)}, u32[]{:S(2)}) copy-start(f32[24,6656]{1,0:T(8,128)S(1)} %pad_maximum_fusion.2.refs_0_) | copy-start | bytes 1916932
  6.1 37.6 %collective-permute-start.21 = (f32[24,6656]{1,0:T(8,128)S(1)}, f32[24,6656]{1,0:T(8,128)S(1)}, u32[]{:S(2)}, u32[]{:S(2)}) collective-permute-start(f32[24,6656]{1,0:T(8,128)S(1)} %pad_maximum_fusion.2.refs_0_), channel_id=1, source_target_pairs={{0,4},{4,0},{8,12},{12,8},{16,20},{20,16},{24,28},{28,24},{1,5},{5... | collective-permute-start | bytes 1916936 | tf_op jit(solution)/shard_map/ppermute | solution.py:228
  6.7 38.3 %collective-permute-start = (f32[24,6656]{1,0:T(8,128)S(1)}, f32[24,6656]{1,0:T(8,128)}, u32[]{:S(2)}, u32[]{:S(2)}) collective-permute-start(f32[24,6656]{1,0:T(8,128)S(1)} %pad_maximum_fusion.2.refs_0_), channel_id=1, source_target_pairs={{0,8},{4,12},{8,0},{12,4},{16,24},{20,28},{24,16},{28,20},{1,9},{5... | collective-permute-start | bytes 1916936 | tf_op jit(solution)/shard_map/ppermute | solution.py:228
  6.8 32.0 %collective-permute-start.7 = (f32[24,5120]{1,0:T(8,128)S(1)}, f32[24,5120]{1,0:T(8,128)S(1)}, u32[]{:S(2)}, u32[]{:S(2)}) collective-permute-start(f32[24,5120]{1,0:T(8,128)S(1)} %pad_maximum_fusion.3), channel_id=1, source_target_pairs={{0,4},{4,0},{8,12},{12,8},{16,20},{20,16},{24,28},{28,24},{1,5},{5... | collective-permute-start | bytes 1474568 | tf_op jit(solution)/shard_map/ppermute | solution.py:228
  15.4 36.1 %copy-start.16 = (f32[24,4608]{1,0:T(8,128)}, f32[24,4608]{1,0:T(8,128)S(1)}, u32[]{:S(2)}) copy-start(f32[24,4608]{1,0:T(8,128)S(1)} %collective-permute-done.22.refs_1_) | copy-start | bytes 1327108
  15.4 26.9 %collective-permute-start.15 = (f32[24,4608]{1,0:T(8,128)S(1)}, f32[24,4608]{1,0:T(8,128)S(1)}, u32[]{:S(2)}, u32[]{:S(2)}) collective-permute-start(f32[24,4608]{1,0:T(8,128)S(1)} %pad_maximum_fusion.4.refs_0_), channel_id=1, source_target_pairs={{8,16},{12,20},{16,8},{20,12},{9,17},{13,21},{17,9},{21,13},{10,18... | collective-permute-start | bytes 1327112 | tf_op jit(solution)/shard_map/ppermute | solution.py:228
  38.8 14.3 %collective-permute-start.2 = (f32[24,6656]{1,0:T(8,128)S(1)}, f32[24,6656]{1,0:T(8,128)}, u32[]{:S(2)}, u32[]{:S(2)}) collective-permute-start(f32[24,6656]{1,0:T(8,128)S(1)} %pad_maximum_fusion.2.refs_0_), channel_id=1, source_target_pairs={{8,16},{12,20},{16,8},{20,12},{9,17},{13,21},{17,9},{21,13},{10,18... | collective-permute-start | bytes 1916936 | tf_op jit(solution)/shard_map/ppermute | solution.py:228
  40.4 81.4 %copy-start.17 = (f32[24,4608]{1,0:T(8,128)}, f32[24,4608]{1,0:T(8,128)S(1)}, u32[]{:S(2)}) copy-start(f32[24,4608]{1,0:T(8,128)S(1)} %collective-permute-done.13.refs_2_) | copy-start | bytes 1327108
  40.5 22.7 %collective-permute-start.14 = (f32[24,4608]{1,0:T(8,128)S(1)}, f32[24,4608]{1,0:T(8,128)S(1)}, u32[]{:S(2)}, u32[]{:S(2)}) collective-permute-start(f32[24,4608]{1,0:T(8,128)S(1)} %collective-permute-done.13.refs_2_), channel_id=1, source_target_pairs={{0,4},{4,0},{8,12},{12,8},{16,20},{20,16},{24,28},{28,24},{1,5},{5... | collective-permute-start | bytes 1327112 | tf_op jit(solution)/shard_map/ppermute | solution.py:228
  42.3 25.4 %copy-start.14 = (f32[24,4608]{1,0:T(8,128)}, f32[24,4608]{1,0:T(8,128)S(1)}, u32[]{:S(2)}) copy-start(f32[24,4608]{1,0:T(8,128)S(1)} %collective-permute-done.15.b_ref) | copy-start | bytes 1327108
  42.3 22.6 %collective-permute-start.17 = (f32[24,4608]{1,0:T(8,128)S(1)}, f32[24,4608]{1,0:T(8,128)}, u32[]{:S(2)}, u32[]{:S(2)}) collective-permute-start(f32[24,4608]{1,0:T(8,128)S(1)} %collective-permute-done.13.refs_2_), channel_id=1, source_target_pairs={{8,16},{12,20},{16,8},{20,12},{9,17},{13,21},{17,9},{21,13},{10,18... | collective-permute-start | bytes 1327112 | tf_op jit(solution)/shard_map/ppermute | solution.py:228
  43.7 19.5 %collective-permute-start.16 = (f32[24,4608]{1,0:T(8,128)S(1)}, f32[24,4608]{1,0:T(8,128)S(1)}, u32[]{:S(2)}, u32[]{:S(2)}) collective-permute-start(f32[24,4608]{1,0:T(8,128)S(1)} %collective-permute-done.15.b_ref), channel_id=1, source_target_pairs={{8,0},{12,4},{16,24},{20,28},{9,1},{13,5},{17,25},{21,29},{10,2},{... | collective-permute-start | bytes 1327112 | tf_op jit(solution)/shard_map/ppermute | solution.py:228
  45.0 21.1 %collective-permute-start.24 = (f32[48,2304]{1,0:T(8,128)S(1)}, f32[48,2304]{1,0:T(8,128)S(1)}, u32[]{:S(2)}, u32[]{:S(2)}) collective-permute-start(f32[48,2304]{1,0:T(8,128)S(1)} %slice.175.refs_1_), channel_id=1, source_target_pairs={{0,8},{4,12},{24,16},{28,20},{1,9},{5,13},{25,17},{29,21},{2,10},{... | collective-permute-start | bytes 1327112 | tf_op jit(solution)/shard_map/ppermute | solution.py:228
  53.1 140.1 %collective-permute-start.26 = (f32[256,2304]{1,0:T(8,128)}, f32[256,2304]{1,0:T(8,128)}, u32[]{:S(2)}, u32[]{:S(2)}) collective-permute-start(f32[256,2304]{1,0:T(8,128)} %pad_maximum_fusion), channel_id=1, source_target_pairs={{0,8},{4,12},{24,16},{28,20},{1,9},{5,13},{25,17},{29,21},{2,10},{... | collective-permute-start | bytes 7077896 | tf_op jit(solution)/shard_map/ppermute | solution.py:228
  63.1 84.3 %copy-start.3 = (f32[48,2816]{1,0:T(8,128)}, f32[48,2816]{1,0:T(8,128)S(1)}, u32[]{:S(2)}) copy-start(f32[48,2816]{1,0:T(8,128)S(1)} %slice.150.refs_0_) | copy-start | bytes 1622020
  63.2 58.1 %collective-permute-start.10 = (f32[48,2816]{1,0:T(8,128)S(1)}, f32[48,2816]{1,0:T(8,128)}, u32[]{:S(2)}, u32[]{:S(2)}) collective-permute-start(f32[48,2816]{1,0:T(8,128)S(1)} %slice.150.refs_0_), channel_id=1, source_target_pairs={{0,8},{4,12},{8,0},{12,4},{16,24},{20,28},{24,16},{28,20},{1,9},{5... | collective-permute-start | bytes 1622024 | tf_op jit(solution)/shard_map/ppermute | solution.py:228
  63.3 58.6 %collective-permute-start.1 = (f32[24,6656]{1,0:T(8,128)}, f32[24,6656]{1,0:T(8,128)}, u32[]{:S(2)}, u32[]{:S(2)}) collective-permute-start(f32[24,6656]{1,0:T(8,128)} %collective-permute-done.refs_2_), channel_id=1, source_target_pairs={{0,4},{4,0},{8,12},{12,8},{16,20},{20,16},{24,28},{28,24},{1,5},{5... | collective-permute-start | bytes 1916936 | tf_op jit(solution)/shard_map/ppermute | solution.py:228
  64.8 57.7 %collective-permute-start.3 = (f32[24,6656]{1,0:T(8,128)}, f32[24,6656]{1,0:T(8,128)}, u32[]{:S(2)}, u32[]{:S(2)}) collective-permute-start(f32[24,6656]{1,0:T(8,128)} %collective-permute-done.2.b_ref), channel_id=1, source_target_pairs={{8,0},{12,4},{16,24},{20,28},{9,1},{13,5},{17,25},{21,29},{10,2},{... | collective-permute-start | bytes 1916936 | tf_op jit(solution)/shard_map/ppermute | solution.py:228
  66.2 81.3 %copy-start.6 = (f32[48,2304]{1,0:T(8,128)}, f32[48,2304]{1,0:T(8,128)S(1)}, u32[]{:S(2)}) copy-start(f32[48,2304]{1,0:T(8,128)S(1)} %collective-permute-done.24.refs_2_) | copy-start | bytes 1327108
  66.2 57.7 %collective-permute-start.4 = (f32[24,6656]{1,0:T(8,128)}, f32[24,6656]{1,0:T(8,128)}, u32[]{:S(2)}, u32[]{:S(2)}) collective-permute-start(f32[24,6656]{1,0:T(8,128)} %collective-permute-done.refs_2_), channel_id=1, source_target_pairs={{8,16},{12,20},{16,8},{20,12},{9,17},{13,21},{17,9},{21,13},{10,18... | collective-permute-start | bytes 1916936 | tf_op jit(solution)/shard_map/ppermute | solution.py:228
  121.3 8.7 %collective-permute-start.18 = (f32[24,4608]{1,0:T(8,128)}, f32[24,4608]{1,0:T(8,128)}, u32[]{:S(2)}, u32[]{:S(2)}) collective-permute-start(f32[24,4608]{1,0:T(8,128)} %shard_map.95.refs_1_), channel_id=1, source_target_pairs={{0,4},{4,0},{8,12},{12,8},{16,20},{20,16},{24,28},{28,24},{1,5},{5... | collective-permute-start | bytes 1327112 | tf_op jit(solution)/shard_map/ppermute | solution.py:228
  121.8 31.0 %collective-permute-start.8 = (f32[48,5120]{1,0:T(8,128)S(1)}, f32[48,5120]{1,0:T(8,128)S(1)}, u32[]{:S(2)}, u32[]{:S(2)}) collective-permute-start(f32[48,5120]{1,0:T(8,128)S(1)} %pad_maximum_fusion.1), channel_id=1, source_target_pairs={{8,16},{12,20},{16,8},{20,12},{9,17},{13,21},{17,9},{21,13},{10,18... | collective-permute-start | bytes 2949128 | tf_op jit(solution)/shard_map/ppermute | solution.py:228
  122.6 18.0 %collective-permute-start.19 = (f32[24,4608]{1,0:T(8,128)}, f32[24,4608]{1,0:T(8,128)}, u32[]{:S(2)}, u32[]{:S(2)}) collective-permute-start(f32[24,4608]{1,0:T(8,128)} %collective-permute-done.17.b_ref), channel_id=1, source_target_pairs={{8,0},{12,4},{16,24},{20,28},{9,1},{13,5},{17,25},{21,29},{10,2},{... | collective-permute-start | bytes 1327112 | tf_op jit(solution)/shard_map/ppermute | solution.py:228
  123.9 20.0 %collective-permute-start.25 = (f32[48,2304]{1,0:T(8,128)S(1)}, f32[48,2304]{1,0:T(8,128)S(1)}, u32[]{:S(2)}, u32[]{:S(2)}) collective-permute-start(f32[48,2304]{1,0:T(8,128)S(1)} %collective-permute-done.24.refs_2_), channel_id=1, source_target_pairs={{8,16},{12,20},{16,8},{20,12},{9,17},{13,21},{17,9},{21,13},{10,18... | collective-permute-start | bytes 1327112 | tf_op jit(solution)/shard_map/ppermute | solution.py:228
  130.0 19.0 %collective-permute-start.6 = (f32[24,6656]{1,0:T(8,128)}, f32[24,6656]{1,0:T(8,128)}, u32[]{:S(2)}, u32[]{:S(2)}) collective-permute-start(f32[24,6656]{1,0:T(8,128)} %collective-permute-done.4.b_ref), channel_id=1, source_target_pairs={{8,0},{12,4},{16,24},{20,28},{9,1},{13,5},{17,25},{21,29},{10,2},{... | collective-permute-start | bytes 1916936 | tf_op jit(solution)/shard_map/ppermute | solution.py:228
  140.5 12.7 %collective-permute-start.11 = (f32[48,2816]{1,0:T(8,128)}, f32[48,2816]{1,0:T(8,128)}, u32[]{:S(2)}, u32[]{:S(2)}) collective-permute-start(f32[48,2816]{1,0:T(8,128)} %collective-permute-done.10.refs_1_), channel_id=1, source_target_pairs={{8,16},{12,20},{16,8},{20,12},{9,17},{13,21},{17,9},{21,13},{10,18... | collective-permute-start | bytes 1622024 | tf_op jit(solution)/shard_map/ppermute | solution.py:228
  143.9 14.9 %copy-start.29 = (s32[128]{0:T(128)S(1)}, s32[128]{0:T(128)}, u32[]{:S(2)}) copy-start(s32[128]{0:T(128)} %param.15) | copy-start | bytes 1540
  143.9 14.9 %copy-start.27 = (s32[1,8]{1,0:T(1,128)S(1)}, s32[1,8]{1,0:T(1,128)}, u32[]{:S(2)}) copy-start(s32[1,8]{1,0:T(1,128)} %constant.119) | copy-start | bytes 100
  143.9 14.9 %copy-start.28 = (s32[1,8]{1,0:T(1,128)S(1)}, s32[1,8]{1,0:T(1,128)}, u32[]{:S(2)}) copy-start(s32[1,8]{1,0:T(1,128)} %constant.118) | copy-start | bytes 100
  143.9 13.4 %collective-permute-start.20 = (f32[24,4608]{1,0:T(8,128)}, f32[24,4608]{1,0:T(8,128)}, u32[]{:S(2)}, u32[]{:S(2)}) collective-permute-start(f32[24,4608]{1,0:T(8,128)} %shard_map.96.refs_3_), channel_id=1, source_target_pairs={{0,4},{4,0},{8,12},{12,8},{16,20},{20,16},{24,28},{28,24},{1,5},{5... | collective-permute-start | bytes 1327112 | tf_op jit(solution)/shard_map/ppermute | solution.py:228
  149.0 33.3 %collective-permute-start.5 = (f32[24,6656]{1,0:T(8,128)}, f32[24,6656]{1,0:T(8,128)S(1)}, u32[]{:S(2)}, u32[]{:S(2)}) collective-permute-start(f32[24,6656]{1,0:T(8,128)} %shard_map.91.refs_1_), channel_id=1, source_target_pairs={{0,4},{4,0},{8,12},{12,8},{16,20},{20,16},{24,28},{28,24},{1,5},{5... | collective-permute-start | bytes 1916936 | tf_op jit(solution)/shard_map/ppermute | solution.py:228
  152.8 47.5 %collective-permute-start.23 = (f32[24,6656]{1,0:T(8,128)}, f32[24,6656]{1,0:T(8,128)S(1)}, u32[]{:S(2)}, u32[]{:S(2)}) collective-permute-start(f32[24,6656]{1,0:T(8,128)} %shard_map.92.refs_3_), channel_id=1, source_target_pairs={{0,4},{4,0},{8,12},{12,8},{16,20},{20,16},{24,28},{28,24},{1,5},{5... | collective-permute-start | bytes 1916936 | tf_op jit(solution)/shard_map/ppermute | solution.py:228
  153.2 35.5 %collective-permute-start.9 = (f32[48,2816]{1,0:T(8,128)S(1)}, f32[48,2816]{1,0:T(8,128)S(1)}, u32[]{:S(2)}, u32[]{:S(2)}) collective-permute-start(f32[48,2816]{1,0:T(8,128)S(1)} %slice.149.refs_5_), channel_id=1, source_target_pairs={{8,0},{12,4},{16,24},{20,28},{9,1},{13,5},{17,25},{21,29},{10,2},{... | collective-permute-start | bytes 1622024 | tf_op jit(solution)/shard_map/ppermute | solution.py:228
  157.3 31.5 %collective-permute-start.12 = (f32[48,2816]{1,0:T(8,128)}, f32[48,2816]{1,0:T(8,128)}, u32[]{:S(2)}, u32[]{:S(2)}) collective-permute-start(f32[48,2816]{1,0:T(8,128)} %collective-permute-done.11.refs_3_), channel_id=1, source_target_pairs={{8,0},{12,4},{16,24},{20,28},{9,1},{13,5},{17,25},{21,29},{10,2},{... | collective-permute-start | bytes 1622024 | tf_op jit(solution)/shard_map/ppermute | solution.py:228
  198.9 22.6 %copy-start.30 = (s32[128]{0:T(128)S(1)}, s32[128]{0:T(128)}, u32[]{:S(2)}) copy-start(s32[128]{0:T(128)} %param.14) | copy-start | bytes 1540
  198.9 24.5 %copy-start.24 = (f32[128]{0:T(128)S(1)}, f32[128]{0:T(128)}, u32[]{:S(2)}) copy-start(f32[128]{0:T(128)} %param.13) | copy-start | bytes 1540
  198.9 24.5 %copy-start.25 = (f32[128]{0:T(128)S(1)}, f32[128]{0:T(128)}, u32[]{:S(2)}) copy-start(f32[128]{0:T(128)} %param.12) | copy-start | bytes 1540
  198.9 24.5 %copy-start.26 = (f32[128]{0:T(128)S(1)}, f32[128]{0:T(128)}, u32[]{:S(2)}) copy-start(f32[128]{0:T(128)} %param.11) | copy-start | bytes 1540
  198.9 20.6 %collective-permute-start.27 = (f32[96,128]{1,0:T(8,128)S(1)}, f32[96,128]{1,0:T(8,128)S(1)}, u32[]{:S(2)}, u32[]{:S(2)}) collective-permute-start(f32[96,128]{1,0:T(8,128)S(1)} %reshape.100), channel_id=1, source_target_pairs={{8,0},{12,4},{16,24},{20,28},{9,1},{13,5},{17,25},{21,29},{10,2},{... | collective-permute-start | bytes 147464 | tf_op jit(solution)/shard_map/ppermute | solution.py:228
  219.5 3.3 %collective-permute-start.30 = (f32[24,128]{1,0:T(8,128)S(1)}, f32[24,128]{1,0:T(8,128)S(1)}, u32[]{:S(2)}, u32[]{:S(2)}) collective-permute-start(f32[24,128]{1,0:T(8,128)S(1)} %get-tuple-element.40), channel_id=1, source_target_pairs={{0,3},{1,2},{2,1},{3,0},{4,7},{5,6},{6,5},{7,4},{8,11},{9,10},{10,... | collective-permute-start | bytes 36872 | tf_op jit(solution)/shard_map/ppermute | solution.py:343
  219.6 3.8 %collective-permute-start.29 = (f32[24,128]{1,0:T(8,128)S(1)}, f32[24,128]{1,0:T(8,128)S(1)}, u32[]{:S(2)}, u32[]{:S(2)}) collective-permute-start(f32[24,128]{1,0:T(8,128)S(1)} %get-tuple-element.41), channel_id=1, source_target_pairs={{0,2},{1,3},{2,0},{3,1},{4,6},{5,7},{6,4},{7,5},{8,10},{9,11},{10,... | collective-permute-start | bytes 36872 | tf_op jit(solution)/shard_map/ppermute | solution.py:343
  221.1 2.2 collective-permute-start.28
  223.4 3.8 %collective-permute-start.31 = (f32[25,128]{1,0:T(8,128)S(1)}, f32[25,128]{1,0:T(8,128)S(1)}, u32[]{:S(2)}, u32[]{:S(2)}) collective-permute-start(f32[25,128]{1,0:T(8,128)S(1)} %get-tuple-element.42), channel_id=1, source_target_pairs={{0,4},{4,0},{8,12},{12,8},{16,20},{20,16},{24,28},{28,24},{1,5},{5... | collective-permute-start | bytes 38408 | tf_op jit(solution)/shard_map/ppermute | solution.py:228
  227.2 7.6 %collective-permute-start.32 = (f32[25,256]{1,0:T(8,128)S(1)}, f32[25,256]{1,0:T(8,128)S(1)}, u32[]{:S(2)}, u32[]{:S(2)}) collective-permute-start(f32[25,256]{1,0:T(8,128)S(1)} %pad_maximum_fusion.5), channel_id=1, source_target_pairs={{0,8},{4,12},{8,0},{12,4},{16,24},{20,28},{24,16},{28,20},{1,9},{5... | collective-permute-start | bytes 76808 | tf_op jit(solution)/shard_map/ppermute | solution.py:228
  232.3 5.4 %collective-permute-start.33 = (f32[25,256]{1,0:T(8,128)S(1)}, f32[25,256]{1,0:T(8,128)S(1)}, u32[]{:S(2)}, u32[]{:S(2)}) collective-permute-start(f32[25,256]{1,0:T(8,128)S(1)} %pad_maximum_fusion.5), channel_id=1, source_target_pairs={{0,16},{4,20},{8,24},{12,28},{16,0},{20,4},{24,8},{28,12},{1,17},{... | collective-permute-start | bytes 76808 | tf_op jit(solution)/shard_map/ppermute | solution.py:228
  233.4 5.7 %collective-permute-start.34 = (f32[25,256]{1,0:T(8,128)S(1)}, f32[25,256]{1,0:T(8,128)S(1)}, u32[]{:S(2)}, u32[]{:S(2)}) collective-permute-start(f32[25,256]{1,0:T(8,128)S(1)} %pad_maximum_fusion.5), channel_id=1, source_target_pairs={{0,24},{4,28},{8,16},{12,20},{16,8},{20,12},{24,0},{28,4},{1,25},{... | collective-permute-start | bytes 76808 | tf_op jit(solution)/shard_map/ppermute | solution.py:228
  (18 other events, 118.2 us)

commit v5 on v4

--- a/solution.py
+++ b/solution.py
@@ -167,11 +167,12 @@
             + [("1", "y", 1), ("1", "m", 2), ("1", "e", 2), ("bx", "m", 1), ("1", "mul", near)]
             + [("x", "m", 2), ("b", "m", 2)]
             + [("0", "sel", 2), ("0", "y", 2), ("0", "e", 3)]
-            + [("1", "sel", 2), ("1", "y", 2), ("1", "e", 3), ("b", "mul", slots(0, 1)), ("b", "e", 2)]
-            + [("0", "sel", 3), ("0", "y", 3), ("0", "mul", inner), ("x", "mul", "own")]
+            + [("1", "sel", 2), ("1", "y", 2), ("1", "e", 3), ("b", "mul", slots(0, 1))]
+            + [("0", "mul", (("y", 1),) + slots(2)), ("b", "e", 2)]
+            + [("0", "sel", 3), ("0", "y", 3), ("x", "mul", "own")]
             + [("1", "sel", 3), ("1", "y", 3), ("b", "e", 3)]
-            + [("x", "mul", "far"), ("x", "back", 0), ("0", "mul", (("y", 3),)), ("b", "mul", slots(2, 3))]
-            + [("1", "mul", inner + (("y", 3),))]
+            + [("x", "mul", "far"), ("x", "back", 0), ("0", "mul", (("y", 2),) + slots(3) + (("y", 3),))]
+            + [("1", "mul", inner + (("y", 3),)), ("b", "mul", slots(2, 3))]
         )
     chunks = [str(c) for c in range(CHUNKS)]
     last = planes - 1
@@ -288,7 +289,7 @@
         if whose == "far":
             factors, starts = [have["x", "f", 0]] * folds, [(f * band, 0) for f in range(folds)]
         sums = products(blocks, factors, starts, rows, band, sizes["x"] * LANE, order, whose == "far")
-        have["x", whose, 0] = sums.reshape(row_size * rows, band)
+        have["x", whose, 0] = sums
 
     def place(sums):
         placed = []
@@ -299,7 +300,7 @@
                 mine = jnp.where(at == j, sums[j][0], mine)
                 other = jnp.where(at == j, sums[j][1], other)
             placed += [jnp.where(y == 0, mine, other), jnp.where(y == 0, other, mine)]
-        return jnp.concatenate(placed, axis=0)
+        return jnp.stack(placed)
 
     for step in plan(planes):
         stream, move, j = step

time: 241 us -> 235 us (0.975)
  waiting for transfers between devices: 119 us -> 113 us
  local copies, waits for them, and re-layouts: 7.99 us -> 5.14 us
  starting transfers between devices: 59.5 us -> 62.2 us
    ppermute x32, waiting for transfers between devices: 117 us -> 111 us  [body(): send = lambda x, pairs: lax.ppermute(x, 'row', pairs)]
    ppermute x32, starting transfers between devices: 57.6 us -> 60.3 us  [body(): send = lambda x, pairs: lax.ppermute(x, 'row', pairs)]
  transfers between devices with their start and end apart: 35 -> 35, of which waited for: 13 -> 13; matrix products, arithmetic and copies ran while one was open for 3% -> 2% of each run, Pallas kernels for 20% -> 21%
where the time goes in v5:
time: 235 us; the launch traced here: 234 us
  waiting for transfers between devices  113 us (48%)
  starting transfers between devices  62.2 us (26%)
  Pallas kernels  49.2 us (21%)
  local copies, waits for them, and re-layouts  5.14 us (2%)
  other arithmetic  3.2 us (1%)
    ppermute x32, waiting for transfers between devices, body(): send = lambda x, pairs: lax.ppermute(x, 'row', pairs)  111 us
    ppermute x32, starting transfers between devices, body(): send = lambda x, pairs: lax.ppermute(x, 'row', pairs)  60.3 us
    pallas_call x9, Pallas kernels, products(): pl.pallas_call(kernel, grid_spec=pltpu.PrefetchScalarGridSpec(num_scalar_...  41.4 us
    pallas_call x4, Pallas kernels, choose(): pl.pallas_call(kernel, grid_spec=pltpu.PrefetchScalarGridSpec(num_scalar_...  7.73 us
  transfers between devices with their start and end apart: 35, of which 13 were waited for; matrix products, arithmetic and copies ran while one was open for 2% of the time, Pallas kernels for 21%

profile of v5, /device:TPU:0, one launch (start us, length us, event | category | flops | bytes accessed | tf_op | source)
XLA Modules:
  0.0 234.2 jit_solution(17093898163873541064)
XLA Ops:
  1.3 3.1 %collective-permute-start.23 = (f32[24,4608]{1,0:T(8,128)S(1)}, f32[24,4608]{1,0:T(8,128)S(1)}, u32[]{:S(2)}, u32[]{:S(2)}) collective-permute-start(f32[24,4608]{1,0:T(8,128)S(1)} %pad_maximum_fusion.4.refs_0_), channel_id=1, source_target_pairs={{0,4},{4,0},{8,12},{12,8},{16,20},{20,16},{24,28},{28,24},{1,5},{5... | collective-permute-start | bytes 1327112 | tf_op jit(solution)/shard_map/ppermute | solution.py:229
  4.4 1.6 collective-permute-start.7
  6.8 2.0 collective-permute-start.15
  8.8 1.8 fusion.18
  10.6 4.8 %collective-permute-done.23.refs_1_ = f32[24,4608]{1,0:T(8,128)S(1)} collective-permute-done((f32[24,4608]{1,0:T(8,128)S(1)}, f32[24,4608]{1,0:T(8,128)S(1)}, u32[]{:S(2)}, u32[]{:S(2)}) %collective-permute-start.23) | collective-permute-done | bytes 442400 | tf_op jit(solution)/shard_map/ppermute | solution.py:229
  16.1 22.7 %collective-permute-done.15 = f32[24,5120]{1,0:T(8,128)S(1)} collective-permute-done((f32[24,5120]{1,0:T(8,128)S(1)}, f32[24,5120]{1,0:T(8,128)S(1)}, u32[]{:S(2)}, u32[]{:S(2)}) %collective-permute-start.15) | collective-permute-done | bytes 491552 | tf_op jit(solution)/shard_map/ppermute | solution.py:229
  38.8 1.5 collective-permute-start
  40.4 1.8 collective-permute-start.8
  42.9 1.3 collective-permute-start.10
  44.2 7.2 %collective-permute-start.24 = (f32[48,2304]{1,0:T(8,128)S(1)}, f32[48,2304]{1,0:T(8,128)S(1)}, u32[]{:S(2)}, u32[]{:S(2)}) collective-permute-start(f32[48,2304]{1,0:T(8,128)S(1)} %slice.180.refs_1_), channel_id=1, source_target_pairs={{0,8},{4,12},{24,16},{28,20},{1,9},{5,13},{25,17},{29,21},{2,10},{... | collective-permute-start | bytes 1327112 | tf_op jit(solution)/shard_map/ppermute | solution.py:229
  51.5 1.5 pad_maximum_fusion
  53.0 10.1 %collective-permute-start.26 = (f32[256,2304]{1,0:T(8,128)}, f32[256,2304]{1,0:T(8,128)}, u32[]{:S(2)}, u32[]{:S(2)}) collective-permute-start(f32[256,2304]{1,0:T(8,128)} %pad_maximum_fusion), channel_id=1, source_target_pairs={{0,8},{4,12},{24,16},{28,20},{1,9},{5,13},{25,17},{29,21},{2,10},{... | collective-permute-start | bytes 7077896 | tf_op jit(solution)/shard_map/ppermute | solution.py:229
  63.1 1.5 collective-permute-start.3
  64.6 1.5 collective-permute-start.21
  66.1 1.3 collective-permute-start.1
  67.5 3.9 %collective-permute-start.18 = (f32[48,2816]{1,0:T(8,128)S(1)}, f32[48,2816]{1,0:T(8,128)}, u32[]{:S(2)}, u32[]{:S(2)}) collective-permute-start(f32[48,2816]{1,0:T(8,128)S(1)} %slice.157.refs_0_), channel_id=1, source_target_pairs={{0,8},{4,12},{8,0},{12,4},{16,24},{20,28},{24,16},{28,20},{1,9},{5... | collective-permute-start | bytes 1622024 | tf_op jit(solution)/shard_map/ppermute | solution.py:229
  71.5 1.3 collective-permute-start.5
  72.7 48.5 %collective-permute-done.18.refs_1_ = f32[48,2816]{1,0:T(8,128)} collective-permute-done((f32[48,2816]{1,0:T(8,128)S(1)}, f32[48,2816]{1,0:T(8,128)}, u32[]{:S(2)}, u32[]{:S(2)}) %collective-permute-start.18) | collective-permute-done | bytes 540704 | tf_op jit(solution)/shard_map/ppermute | solution.py:229
  122.1 1.9 shard_map.94.refs_1_
  125.8 6.7 %collective-permute-done.12.refs_2_ = f32[24,4608]{1,0:T(8,128)S(1)} collective-permute-done((f32[24,4608]{1,0:T(8,128)}, f32[24,4608]{1,0:T(8,128)S(1)}, u32[]{:S(2)}, u32[]{:S(2)}) %collective-permute-start.12) | collective-permute-done | bytes 442400 | tf_op jit(solution)/shard_map/ppermute | solution.py:229
  132.5 1.5 collective-permute-start.19
  134.0 3.6 %collective-permute-done.13.a_ref = f32[24,4608]{1,0:T(8,128)S(1)} collective-permute-done((f32[24,4608]{1,0:T(8,128)}, f32[24,4608]{1,0:T(8,128)S(1)}, u32[]{:S(2)}, u32[]{:S(2)}) %collective-permute-start.13) | collective-permute-done | bytes 442400 | tf_op jit(solution)/shard_map/ppermute | solution.py:229
  139.1 1.9 shard_map.95.refs_3_
  141.0 1.6 collective-permute-start.14
  142.5 2.0 shard_map.91.refs_1_
  144.5 2.0 shard_map.92.refs_1_
  147.3 1.4 collective-permute-start.6
  148.7 1.3 collective-permute-start.17
  150.0 4.4 %collective-permute-done.14.refs_4_ = f32[24,4608]{1,0:T(8,128)} collective-permute-done((f32[24,4608]{1,0:T(8,128)}, f32[24,4608]{1,0:T(8,128)}, u32[]{:S(2)}, u32[]{:S(2)}) %collective-permute-start.14) | collective-permute-done | bytes 442400 | tf_op jit(solution)/shard_map/ppermute | solution.py:229
  156.4 4.4 %shard_map.100 = f32[3,12,128]{2,1,0:T(8,128)} custom-call(f32[24,4608]{1,0:T(8,128)} %copy-done.8, f32[24,4608]{1,0:T(8,128)} %copy-done.18, f32[24,4608]{1,0:T(8,128)} %copy-done.19, f32[128,32768]{1,0:T(8,128)} %refs_6_.5, f32[128,32768]{1,0:T(8,128)} %refs_6_.5), custom_call_target="tpu_custom_call" | custom-call | tf_op jit(solution)/shard_map/pallas_call | solution.py:104
  160.8 5.5 %shard_map.99 = f32[3,12,128]{2,1,0:T(8,128)} custom-call(f32[24,6656]{1,0:T(8,128)} %copy-done.2, f32[24,6656]{1,0:T(8,128)} %copy-done.9, f32[24,6656]{1,0:T(8,128)} %collective-permute-done.2.refs_2_, f32[128,32768]{1,0:T(8,128)} %refs_6_.5, f32[128,32768]{1,0:T(8,128)} %refs_6_.5), custom_call_target="tpu_custom_call" | custom-call | tf_op jit(solution)/shard_map/pallas_call | solution.py:104
  166.2 3.4 %shard_map.101 = f32[4,12,128]{2,1,0:T(8,128)} custom-call(f32[48,2816]{1,0:T(8,128)} %copy-done.3, f32[48,2816]{1,0:T(8,128)} %collective-permute-done.18.refs_1_, f32[128,32768]{1,0:T(8,128)} %refs_6_.5, f32[128,32768]{1,0:T(8,128)} %refs_6_.5), custom_call_target="tpu_custom_call" | custom-call | tf_op jit(solution)/shard_map/pallas_call | solution.py:104
  169.6 5.4 %shard_map.98 = f32[2,12,128]{2,1,0:T(8,128)} custom-call(f32[24,6656]{1,0:T(8,128)} %collective-permute-done.21.refs_0_, f32[24,6656]{1,0:T(8,128)} %shard_map.91.refs_1_, f32[128,32768]{1,0:T(8,128)} %refs_6_.5, f32[128,32768]{1,0:T(8,128)} %refs_6_.5), custom_call_target="tpu_custom_call" | custom-call | tf_op jit(solution)/shard_map/pallas_call | solution.py:104
  175.0 4.4 %shard_map.103 = f32[8,12,128]{2,1,0:T(8,128)} custom-call(s32[8]{0:T(128)} %fusion.14.refs_0_, f32[48,2304]{1,0:T(8,128)} %copy-done.1, f32[48,2304]{1,0:T(8,128)} %copy-done.6, f32[48,5120]{1,0:T(8,128)} %copy-done, f32[48,2304]{1,0:T(8,128)} %copy-done.7, f32[128,32768]{1,0:T(8,128)} %refs_6_.5, f32[128,32768]{1,0:T(8,128)} %refs_6_.5), custom_call_target="tpu_custom_call" | custom-call | tf_op jit(solution)/shard_map/pallas_call | solution.py:104
  179.3 4.7 %shard_map.96 = f32[5,12,128]{2,1,0:T(8,128)} custom-call(f32[24,4608]{1,0:T(8,128)} %copy-done.12, f32[24,4608]{1,0:T(8,128)} %shard_map.94.refs_1_, f32[24,4608]{1,0:T(8,128)} %copy-done.13, f32[24,4608]{1,0:T(8,128)} %shard_map.95.refs_3_, f32[24,4608]{1,0:T(8,128)} %collective-permute-done.14.refs_4_, f32[128,32768]{1,0:T(8,128)} %refs_6_.5, ...), custom_call_target="tpu_custom_call" | custom-call | tf_op jit(solution)/shard_map/pallas_call | solution.py:104
  184.0 5.2 %collective-permute-done.20.refs_4_ = f32[48,2816]{1,0:T(8,128)} collective-permute-done((f32[48,2816]{1,0:T(8,128)}, f32[48,2816]{1,0:T(8,128)}, u32[]{:S(2)}, u32[]{:S(2)}) %collective-permute-start.20) | collective-permute-done | bytes 540704 | tf_op jit(solution)/shard_map/ppermute | solution.py:229
  189.2 3.6 %shard_map.97 = f32[4,12,128]{2,1,0:T(8,128)} custom-call(s32[1]{0:T(128)} %bitcast.flag_ref.refs_0_, s32[1]{0:T(128)} %bitcast.2.flag_ref.refs_1_, f32[48,2816]{1,0:T(8,128)} %copy-done.11, f32[48,2816]{1,0:T(8,128)} %collective-permute-done.19.refs_3_, f32[48,2816]{1,0:T(8,128)} %collective-permute-done.20.refs_4_, f32[48,2816]{1,0:T(8,128)} %copy-done.4, ...), custom_call_target="tpu_custom_call" | custom-call | tf_op jit(solution)/shard_map/pallas_call | solution.py:104
  192.8 4.8 %shard_map.102 = f32[8,12,128]{2,1,0:T(8,128)} custom-call(s32[8]{0:T(128)} %fusion.14.refs_0_, f32[48,2304]{1,0:T(8,128)} %copy-done.1, f32[48,2304]{1,0:T(8,128)} %copy-done.6, f32[48,5120]{1,0:T(8,128)} %copy-done, f32[48,2304]{1,0:T(8,128)} %copy-done.7, f32[256,2304]{1,0:T(8,128)} %collective-permute-done.26.refs_5_), custom_call_target="tpu_custom_call" | custom-call | tf_op jit(solution)/shard_map/pallas_call | solution.py:104
  197.7 1.4 collective-permute-start.27
  200.0 5.4 %shard_map.93 = f32[3,12,128]{2,1,0:T(8,128)} custom-call(f32[24,6656]{1,0:T(8,128)} %copy-done.10, f32[24,6656]{1,0:T(8,128)} %shard_map.92.refs_1_, f32[24,6656]{1,0:T(8,128)} %collective-permute-done.6.refs_2_, f32[128,32768]{1,0:T(8,128)} %refs_6_.5, f32[128,32768]{1,0:T(8,128)} %refs_6_.5), custom_call_target="tpu_custom_call" | custom-call | tf_op jit(solution)/shard_map/pallas_call | solution.py:104
  206.3 7.3 %collective-permute-done.27 = f32[8,12,128]{2,1,0:T(8,128)S(1)} collective-permute-done((f32[8,12,128]{2,1,0:T(8,128)}, f32[8,12,128]{2,1,0:T(8,128)S(1)}, u32[]{:S(2)}, u32[]{:S(2)}) %collective-permute-start.27) | collective-permute-done | bytes 49184 | tf_op jit(solution)/shard_map/ppermute | solution.py:229
  213.8 1.6 collective-permute-start.29
  215.7 1.3 collective-permute-done.30
  218.4 3.0 %collective-permute-done.31 = f32[25,128]{1,0:T(8,128)S(1)} collective-permute-done((f32[25,128]{1,0:T(8,128)S(1)}, f32[25,128]{1,0:T(8,128)S(1)}, u32[]{:S(2)}, u32[]{:S(2)}) %collective-permute-start.31) | collective-permute-done | bytes 12832 | tf_op jit(solution)/shard_map/ppermute | solution.py:229
  221.5 4.8 %collective-permute-start.32 = (f32[25,256]{1,0:T(8,128)S(1)}, f32[25,256]{1,0:T(8,128)S(1)}, u32[]{:S(2)}, u32[]{:S(2)}) collective-permute-start(f32[25,256]{1,0:T(8,128)S(1)} %pad_maximum_fusion.5), channel_id=1, source_target_pairs={{0,8},{4,12},{8,0},{12,4},{16,24},{20,28},{24,16},{28,20},{1,9},{5... | collective-permute-start | bytes 76808 | tf_op jit(solution)/shard_map/ppermute | solution.py:229
  227.4 1.4 collective-permute-start.34
  228.8 2.9 %collective-permute-done.33 = f32[25,256]{1,0:T(8,128)S(1)} collective-permute-done((f32[25,256]{1,0:T(8,128)S(1)}, f32[25,256]{1,0:T(8,128)S(1)}, u32[]{:S(2)}, u32[]{:S(2)}) %collective-permute-start.33) | collective-permute-done | bytes 25632 | tf_op jit(solution)/shard_map/ppermute | solution.py:229
  231.7 1.4 collective-permute-done.34
  (139 shorter events, 16.0 us)
Async XLA Ops:
  1.3 14.1 %collective-permute-start.23 = (f32[24,4608]{1,0:T(8,128)S(1)}, f32[24,4608]{1,0:T(8,128)S(1)}, u32[]{:S(2)}, u32[]{:S(2)}) collective-permute-start(f32[24,4608]{1,0:T(8,128)S(1)} %pad_maximum_fusion.4.refs_0_), channel_id=1, source_target_pairs={{0,4},{4,0},{8,12},{12,8},{16,20},{20,16},{24,28},{28,24},{1,5},{5... | collective-permute-start | bytes 1327112 | tf_op jit(solution)/shard_map/ppermute | solution.py:229
  4.4 36.0 %collective-permute-start.7 = (f32[24,4608]{1,0:T(8,128)S(1)}, f32[24,4608]{1,0:T(8,128)S(1)}, u32[]{:S(2)}, u32[]{:S(2)}) collective-permute-start(f32[24,4608]{1,0:T(8,128)S(1)} %pad_maximum_fusion.4.refs_0_), channel_id=1, source_target_pairs={{0,8},{4,12},{8,0},{12,4},{16,24},{20,28},{24,16},{28,20},{1,9},{5... | collective-permute-start | bytes 1327112 | tf_op jit(solution)/shard_map/ppermute | solution.py:229
  6.1 32.7 %copy-start.2 = (f32[24,6656]{1,0:T(8,128)}, f32[24,6656]{1,0:T(8,128)S(1)}, u32[]{:S(2)}) copy-start(f32[24,6656]{1,0:T(8,128)S(1)} %pad_maximum_fusion.2.refs_0_) | copy-start | bytes 1916932
  6.1 36.8 %collective-permute-start.22 = (f32[24,6656]{1,0:T(8,128)S(1)}, f32[24,6656]{1,0:T(8,128)S(1)}, u32[]{:S(2)}, u32[]{:S(2)}) collective-permute-start(f32[24,6656]{1,0:T(8,128)S(1)} %pad_maximum_fusion.2.refs_0_), channel_id=1, source_target_pairs={{0,4},{4,0},{8,12},{12,8},{16,20},{20,16},{24,28},{28,24},{1,5},{5... | collective-permute-start | bytes 1916936 | tf_op jit(solution)/shard_map/ppermute | solution.py:229
  6.7 37.6 %collective-permute-start.2 = (f32[24,6656]{1,0:T(8,128)S(1)}, f32[24,6656]{1,0:T(8,128)}, u32[]{:S(2)}, u32[]{:S(2)}) collective-permute-start(f32[24,6656]{1,0:T(8,128)S(1)} %pad_maximum_fusion.2.refs_0_), channel_id=1, source_target_pairs={{0,8},{4,12},{8,0},{12,4},{16,24},{20,28},{24,16},{28,20},{1,9},{5... | collective-permute-start | bytes 1916936 | tf_op jit(solution)/shard_map/ppermute | solution.py:229
  6.8 32.0 %collective-permute-start.15 = (f32[24,5120]{1,0:T(8,128)S(1)}, f32[24,5120]{1,0:T(8,128)S(1)}, u32[]{:S(2)}, u32[]{:S(2)}) collective-permute-start(f32[24,5120]{1,0:T(8,128)S(1)} %pad_maximum_fusion.3), channel_id=1, source_target_pairs={{0,4},{4,0},{8,12},{12,8},{16,20},{20,16},{24,28},{28,24},{1,5},{5... | collective-permute-start | bytes 1474568 | tf_op jit(solution)/shard_map/ppermute | solution.py:229
  15.4 36.1 %copy-start.18 = (f32[24,4608]{1,0:T(8,128)}, f32[24,4608]{1,0:T(8,128)S(1)}, u32[]{:S(2)}) copy-start(f32[24,4608]{1,0:T(8,128)S(1)} %collective-permute-done.23.refs_1_) | copy-start | bytes 1327108
  15.4 26.8 %collective-permute-start.9 = (f32[24,4608]{1,0:T(8,128)S(1)}, f32[24,4608]{1,0:T(8,128)S(1)}, u32[]{:S(2)}, u32[]{:S(2)}) collective-permute-start(f32[24,4608]{1,0:T(8,128)S(1)} %pad_maximum_fusion.4.refs_0_), channel_id=1, source_target_pairs={{8,16},{12,20},{16,8},{20,12},{9,17},{13,21},{17,9},{21,13},{10,18... | collective-permute-start | bytes 1327112 | tf_op jit(solution)/shard_map/ppermute | solution.py:229
  38.8 14.2 %collective-permute-start = (f32[24,6656]{1,0:T(8,128)S(1)}, f32[24,6656]{1,0:T(8,128)}, u32[]{:S(2)}, u32[]{:S(2)}) collective-permute-start(f32[24,6656]{1,0:T(8,128)S(1)} %pad_maximum_fusion.2.refs_0_), channel_id=1, source_target_pairs={{8,16},{12,20},{16,8},{20,12},{9,17},{13,21},{17,9},{21,13},{10,18... | collective-permute-start | bytes 1916936 | tf_op jit(solution)/shard_map/ppermute | solution.py:229
  40.4 81.6 %copy-start.19 = (f32[24,4608]{1,0:T(8,128)}, f32[24,4608]{1,0:T(8,128)S(1)}, u32[]{:S(2)}) copy-start(f32[24,4608]{1,0:T(8,128)S(1)} %collective-permute-done.7.refs_2_) | copy-start | bytes 1327108
  40.4 22.7 %collective-permute-start.8 = (f32[24,4608]{1,0:T(8,128)S(1)}, f32[24,4608]{1,0:T(8,128)S(1)}, u32[]{:S(2)}, u32[]{:S(2)}) collective-permute-start(f32[24,4608]{1,0:T(8,128)S(1)} %collective-permute-done.7.refs_2_), channel_id=1, source_target_pairs={{0,4},{4,0},{8,12},{12,8},{16,20},{20,16},{24,28},{28,24},{1,5},{5... | collective-permute-start | bytes 1327112 | tf_op jit(solution)/shard_map/ppermute | solution.py:229
  42.2 79.8 %copy-start.14 = (f32[24,4608]{1,0:T(8,128)}, f32[24,4608]{1,0:T(8,128)S(1)}, u32[]{:S(2)}) copy-start(f32[24,4608]{1,0:T(8,128)S(1)} %collective-permute-done.9.b_ref) | copy-start | bytes 1327108
  42.2 23.9 %collective-permute-start.11 = (f32[24,4608]{1,0:T(8,128)S(1)}, f32[24,4608]{1,0:T(8,128)S(1)}, u32[]{:S(2)}, u32[]{:S(2)}) collective-permute-start(f32[24,4608]{1,0:T(8,128)S(1)} %collective-permute-done.7.refs_2_), channel_id=1, source_target_pairs={{8,16},{12,20},{16,8},{20,12},{9,17},{13,21},{17,9},{21,13},{10,18... | collective-permute-start | bytes 1327112 | tf_op jit(solution)/shard_map/ppermute | solution.py:229
  42.9 21.7 %collective-permute-start.10 = (f32[24,4608]{1,0:T(8,128)S(1)}, f32[24,4608]{1,0:T(8,128)S(1)}, u32[]{:S(2)}, u32[]{:S(2)}) collective-permute-start(f32[24,4608]{1,0:T(8,128)S(1)} %collective-permute-done.9.b_ref), channel_id=1, source_target_pairs={{8,0},{12,4},{16,24},{20,28},{9,1},{13,5},{17,25},{21,29},{10,2},{... | collective-permute-start | bytes 1327112 | tf_op jit(solution)/shard_map/ppermute | solution.py:229
  44.2 23.2 %collective-permute-start.24 = (f32[48,2304]{1,0:T(8,128)S(1)}, f32[48,2304]{1,0:T(8,128)S(1)}, u32[]{:S(2)}, u32[]{:S(2)}) collective-permute-start(f32[48,2304]{1,0:T(8,128)S(1)} %slice.180.refs_1_), channel_id=1, source_target_pairs={{0,8},{4,12},{24,16},{28,20},{1,9},{5,13},{25,17},{29,21},{2,10},{... | collective-permute-start | bytes 1327112 | tf_op jit(solution)/shard_map/ppermute | solution.py:229
  53.0 139.8 %collective-permute-start.26 = (f32[256,2304]{1,0:T(8,128)}, f32[256,2304]{1,0:T(8,128)}, u32[]{:S(2)}, u32[]{:S(2)}) collective-permute-start(f32[256,2304]{1,0:T(8,128)} %pad_maximum_fusion), channel_id=1, source_target_pairs={{0,8},{4,12},{24,16},{28,20},{1,9},{5,13},{25,17},{29,21},{2,10},{... | collective-permute-start | bytes 7077896 | tf_op jit(solution)/shard_map/ppermute | solution.py:229
  63.1 58.9 %copy-start.12 = (f32[24,4608]{1,0:T(8,128)}, f32[24,4608]{1,0:T(8,128)S(1)}, u32[]{:S(2)}) copy-start(f32[24,4608]{1,0:T(8,128)S(1)} %collective-permute-done.8.refs_0_) | copy-start | bytes 1327108
  63.1 8.4 %collective-permute-start.3 = (f32[24,6656]{1,0:T(8,128)}, f32[24,6656]{1,0:T(8,128)}, u32[]{:S(2)}, u32[]{:S(2)}) collective-permute-start(f32[24,6656]{1,0:T(8,128)} %collective-permute-done.2.refs_2_), channel_id=1, source_target_pairs={{8,16},{12,20},{16,8},{20,12},{9,17},{13,21},{17,9},{21,13},{10,18... | collective-permute-start | bytes 1916936 | tf_op jit(solution)/shard_map/ppermute | solution.py:229
  64.6 59.4 %collective-permute-start.21 = (f32[24,6656]{1,0:T(8,128)}, f32[24,6656]{1,0:T(8,128)}, u32[]{:S(2)}, u32[]{:S(2)}) collective-permute-start(f32[24,6656]{1,0:T(8,128)} %collective-permute-done.2.refs_2_), channel_id=1, source_target_pairs={{0,4},{4,0},{8,12},{12,8},{16,20},{20,16},{24,28},{28,24},{1,5},{5... | collective-permute-start | bytes 1916936 | tf_op jit(solution)/shard_map/ppermute | solution.py:229
  66.1 55.9 %copy-start.15 = (f32[24,4608]{1,0:T(8,128)}, f32[24,4608]{1,0:T(8,128)S(1)}, u32[]{:S(2)}) copy-start(f32[24,4608]{1,0:T(8,128)S(1)} %collective-permute-done.11.b_ref) | copy-start | bytes 1327108
  66.1 58.4 %collective-permute-start.1 = (f32[24,6656]{1,0:T(8,128)}, f32[24,6656]{1,0:T(8,128)}, u32[]{:S(2)}, u32[]{:S(2)}) collective-permute-start(f32[24,6656]{1,0:T(8,128)} %collective-permute-done.b_ref), channel_id=1, source_target_pairs={{8,0},{12,4},{16,24},{20,28},{9,1},{13,5},{17,25},{21,29},{10,2},{... | collective-permute-start | bytes 1916936 | tf_op jit(solution)/shard_map/ppermute | solution.py:229
  67.5 77.0 %copy-start.3 = (f32[48,2816]{1,0:T(8,128)}, f32[48,2816]{1,0:T(8,128)S(1)}, u32[]{:S(2)}) copy-start(f32[48,2816]{1,0:T(8,128)S(1)} %slice.157.refs_0_) | copy-start | bytes 1622020
  67.5 77.0 %copy-start.6 = (f32[48,2304]{1,0:T(8,128)}, f32[48,2304]{1,0:T(8,128)S(1)}, u32[]{:S(2)}) copy-start(f32[48,2304]{1,0:T(8,128)S(1)} %collective-permute-done.24.refs_2_) | copy-start | bytes 1327108
  67.5 53.8 %collective-permute-start.18 = (f32[48,2816]{1,0:T(8,128)S(1)}, f32[48,2816]{1,0:T(8,128)}, u32[]{:S(2)}, u32[]{:S(2)}) collective-permute-start(f32[48,2816]{1,0:T(8,128)S(1)} %slice.157.refs_0_), channel_id=1, source_target_pairs={{0,8},{4,12},{8,0},{12,4},{16,24},{20,28},{24,16},{28,20},{1,9},{5... | collective-permute-start | bytes 1622024 | tf_op jit(solution)/shard_map/ppermute | solution.py:229
  71.5 69.5 %collective-permute-start.5 = (f32[24,6656]{1,0:T(8,128)}, f32[24,6656]{1,0:T(8,128)}, u32[]{:S(2)}, u32[]{:S(2)}) collective-permute-start(f32[24,6656]{1,0:T(8,128)} %collective-permute-done.3.b_ref), channel_id=1, source_target_pairs={{8,0},{12,4},{16,24},{20,28},{9,1},{13,5},{17,25},{21,29},{10,2},{... | collective-permute-start | bytes 1916936 | tf_op jit(solution)/shard_map/ppermute | solution.py:229
  121.3 25.8 %collective-permute-start.16 = (f32[48,5120]{1,0:T(8,128)S(1)}, f32[48,5120]{1,0:T(8,128)S(1)}, u32[]{:S(2)}, u32[]{:S(2)}) collective-permute-start(f32[48,5120]{1,0:T(8,128)S(1)} %pad_maximum_fusion.1), channel_id=1, source_target_pairs={{8,16},{12,20},{16,8},{20,12},{9,17},{13,21},{17,9},{21,13},{10,18... | collective-permute-start | bytes 2949128 | tf_op jit(solution)/shard_map/ppermute | solution.py:229
  124.0 8.6 %collective-permute-start.12 = (f32[24,4608]{1,0:T(8,128)}, f32[24,4608]{1,0:T(8,128)S(1)}, u32[]{:S(2)}, u32[]{:S(2)}) collective-permute-start(f32[24,4608]{1,0:T(8,128)} %shard_map.94.refs_1_), channel_id=1, source_target_pairs={{0,4},{4,0},{8,12},{12,8},{16,20},{20,16},{24,28},{28,24},{1,5},{5... | collective-permute-start | bytes 1327112 | tf_op jit(solution)/shard_map/ppermute | solution.py:229
  124.5 13.1 %collective-permute-start.13 = (f32[24,4608]{1,0:T(8,128)}, f32[24,4608]{1,0:T(8,128)S(1)}, u32[]{:S(2)}, u32[]{:S(2)}) collective-permute-start(f32[24,4608]{1,0:T(8,128)} %copy-done.15), channel_id=1, source_target_pairs={{8,0},{12,4},{16,24},{20,28},{9,1},{13,5},{17,25},{21,29},{10,2},{... | collective-permute-start | bytes 1327112 | tf_op jit(solution)/shard_map/ppermute | solution.py:229
  132.5 16.2 %collective-permute-start.19 = (f32[48,2816]{1,0:T(8,128)}, f32[48,2816]{1,0:T(8,128)}, u32[]{:S(2)}, u32[]{:S(2)}) collective-permute-start(f32[48,2816]{1,0:T(8,128)} %collective-permute-done.18.refs_1_), channel_id=1, source_target_pairs={{8,16},{12,20},{16,8},{20,12},{9,17},{13,21},{17,9},{21,13},{10,18... | collective-permute-start | bytes 1622024 | tf_op jit(solution)/shard_map/ppermute | solution.py:229
  138.4 8.1 %collective-permute-start.25 = (f32[48,2304]{1,0:T(8,128)S(1)}, f32[48,2304]{1,0:T(8,128)S(1)}, u32[]{:S(2)}, u32[]{:S(2)}) collective-permute-start(f32[48,2304]{1,0:T(8,128)S(1)} %collective-permute-done.24.refs_2_), channel_id=1, source_target_pairs={{8,16},{12,20},{16,8},{20,12},{9,17},{13,21},{17,9},{21,13},{10,18... | collective-permute-start | bytes 1327112 | tf_op jit(solution)/shard_map/ppermute | solution.py:229
  141.0 13.4 %collective-permute-start.14 = (f32[24,4608]{1,0:T(8,128)}, f32[24,4608]{1,0:T(8,128)}, u32[]{:S(2)}, u32[]{:S(2)}) collective-permute-start(f32[24,4608]{1,0:T(8,128)} %shard_map.95.refs_3_), channel_id=1, source_target_pairs={{0,4},{4,0},{8,12},{12,8},{16,20},{20,16},{24,28},{28,24},{1,5},{5... | collective-permute-start | bytes 1327112 | tf_op jit(solution)/shard_map/ppermute | solution.py:229
  146.5 52.6 %collective-permute-start.4 = (f32[24,6656]{1,0:T(8,128)}, f32[24,6656]{1,0:T(8,128)S(1)}, u32[]{:S(2)}, u32[]{:S(2)}) collective-permute-start(f32[24,6656]{1,0:T(8,128)} %shard_map.91.refs_1_), channel_id=1, source_target_pairs={{0,4},{4,0},{8,12},{12,8},{16,20},{20,16},{24,28},{28,24},{1,5},{5... | collective-permute-start | bytes 1916936 | tf_op jit(solution)/shard_map/ppermute | solution.py:229
  147.3 51.9 %collective-permute-start.6 = (f32[24,6656]{1,0:T(8,128)}, f32[24,6656]{1,0:T(8,128)}, u32[]{:S(2)}, u32[]{:S(2)}) collective-permute-start(f32[24,6656]{1,0:T(8,128)} %shard_map.92.refs_1_), channel_id=1, source_target_pairs={{0,4},{4,0},{8,12},{12,8},{16,20},{20,16},{24,28},{28,24},{1,5},{5... | collective-permute-start | bytes 1916936 | tf_op jit(solution)/shard_map/ppermute | solution.py:229
  148.7 35.3 %collective-permute-start.17 = (f32[48,2816]{1,0:T(8,128)S(1)}, f32[48,2816]{1,0:T(8,128)S(1)}, u32[]{:S(2)}, u32[]{:S(2)}) collective-permute-start(f32[48,2816]{1,0:T(8,128)S(1)} %slice.156.refs_5_), channel_id=1, source_target_pairs={{8,0},{12,4},{16,24},{20,28},{9,1},{13,5},{17,25},{21,29},{10,2},{... | collective-permute-start | bytes 1622024 | tf_op jit(solution)/shard_map/ppermute | solution.py:229
  154.4 34.8 %collective-permute-start.20 = (f32[48,2816]{1,0:T(8,128)}, f32[48,2816]{1,0:T(8,128)}, u32[]{:S(2)}, u32[]{:S(2)}) collective-permute-start(f32[48,2816]{1,0:T(8,128)} %collective-permute-done.19.refs_3_), channel_id=1, source_target_pairs={{8,0},{12,4},{16,24},{20,28},{9,1},{13,5},{17,25},{21,29},{10,2},{... | collective-permute-start | bytes 1622024 | tf_op jit(solution)/shard_map/ppermute | solution.py:229
  197.6 16.1 %copy-start.20 = (f32[8,12,128]{2,1,0:T(8,128)S(1)}, f32[8,12,128]{2,1,0:T(8,128)}, u32[]{:S(2)}) copy-start(f32[8,12,128]{2,1,0:T(8,128)} %shard_map.103) | copy-start | bytes 147460
  197.6 18.0 %copy-start.33 = (s32[128]{0:T(128)S(1)}, s32[128]{0:T(128)}, u32[]{:S(2)}) copy-start(s32[128]{0:T(128)} %param.14) | copy-start | bytes 1540
  197.6 19.9 %copy-start.27 = (f32[128]{0:T(128)S(1)}, f32[128]{0:T(128)}, u32[]{:S(2)}) copy-start(f32[128]{0:T(128)} %param.13) | copy-start | bytes 1540
  197.7 19.9 %copy-start.28 = (f32[128]{0:T(128)S(1)}, f32[128]{0:T(128)}, u32[]{:S(2)}) copy-start(f32[128]{0:T(128)} %param.12) | copy-start | bytes 1540
  197.7 19.9 %copy-start.29 = (f32[128]{0:T(128)S(1)}, f32[128]{0:T(128)}, u32[]{:S(2)}) copy-start(f32[128]{0:T(128)} %param.11) | copy-start | bytes 1540
  197.7 16.0 %collective-permute-start.27 = (f32[8,12,128]{2,1,0:T(8,128)}, f32[8,12,128]{2,1,0:T(8,128)S(1)}, u32[]{:S(2)}, u32[]{:S(2)}) collective-permute-start(f32[8,12,128]{2,1,0:T(8,128)} %shard_map.102), channel_id=1, source_target_pairs={{8,0},{12,4},{16,24},{20,28},{9,1},{13,5},{17,25},{21,29},{10,2},{... | collective-permute-start | bytes 147464 | tf_op jit(solution)/shard_map/ppermute | solution.py:229
  213.7 3.3 %collective-permute-start.30 = (f32[24,128]{1,0:T(8,128)S(1)}, f32[24,128]{1,0:T(8,128)S(1)}, u32[]{:S(2)}, u32[]{:S(2)}) collective-permute-start(f32[24,128]{1,0:T(8,128)S(1)} %get-tuple-element.34), channel_id=1, source_target_pairs={{0,3},{1,2},{2,1},{3,0},{4,7},{5,6},{6,5},{7,4},{8,11},{9,10},{10,... | collective-permute-start | bytes 36872 | tf_op jit(solution)/shard_map/ppermute | solution.py:344
  213.8 3.8 %collective-permute-start.29 = (f32[24,128]{1,0:T(8,128)S(1)}, f32[24,128]{1,0:T(8,128)S(1)}, u32[]{:S(2)}, u32[]{:S(2)}) collective-permute-start(f32[24,128]{1,0:T(8,128)S(1)} %get-tuple-element.35), channel_id=1, source_target_pairs={{0,2},{1,3},{2,0},{3,1},{4,6},{5,7},{6,4},{7,5},{8,10},{9,11},{10,... | collective-permute-start | bytes 36872 | tf_op jit(solution)/shard_map/ppermute | solution.py:344
  215.4 2.2 collective-permute-start.28
  217.6 3.8 %collective-permute-start.31 = (f32[25,128]{1,0:T(8,128)S(1)}, f32[25,128]{1,0:T(8,128)S(1)}, u32[]{:S(2)}, u32[]{:S(2)}) collective-permute-start(f32[25,128]{1,0:T(8,128)S(1)} %get-tuple-element.36), channel_id=1, source_target_pairs={{0,4},{4,0},{8,12},{12,8},{16,20},{20,16},{24,28},{28,24},{1,5},{5... | collective-permute-start | bytes 38408 | tf_op jit(solution)/shard_map/ppermute | solution.py:229
  221.5 7.3 %collective-permute-start.32 = (f32[25,256]{1,0:T(8,128)S(1)}, f32[25,256]{1,0:T(8,128)S(1)}, u32[]{:S(2)}, u32[]{:S(2)}) collective-permute-start(f32[25,256]{1,0:T(8,128)S(1)} %pad_maximum_fusion.5), channel_id=1, source_target_pairs={{0,8},{4,12},{8,0},{12,4},{16,24},{20,28},{24,16},{28,20},{1,9},{5... | collective-permute-start | bytes 76808 | tf_op jit(solution)/shard_map/ppermute | solution.py:229
  226.3 5.4 %collective-permute-start.33 = (f32[25,256]{1,0:T(8,128)S(1)}, f32[25,256]{1,0:T(8,128)S(1)}, u32[]{:S(2)}, u32[]{:S(2)}) collective-permute-start(f32[25,256]{1,0:T(8,128)S(1)} %pad_maximum_fusion.5), channel_id=1, source_target_pairs={{0,16},{4,20},{8,24},{12,28},{16,0},{20,4},{24,8},{28,12},{1,17},{... | collective-permute-start | bytes 76808 | tf_op jit(solution)/shard_map/ppermute | solution.py:229
  227.4 5.7 %collective-permute-start.34 = (f32[25,256]{1,0:T(8,128)S(1)}, f32[25,256]{1,0:T(8,128)S(1)}, u32[]{:S(2)}, u32[]{:S(2)}) collective-permute-start(f32[25,256]{1,0:T(8,128)S(1)} %pad_maximum_fusion.5), channel_id=1, source_target_pairs={{0,24},{4,28},{8,16},{12,20},{16,8},{20,12},{24,0},{28,4},{1,25},{... | collective-permute-start | bytes 76808 | tf_op jit(solution)/shard_map/ppermute | solution.py:229
  (21 other events, 161.9 us)

commit v6 on v5

--- a/solution.py
+++ b/solution.py
@@ -26,7 +26,7 @@
     return LANE * max(d for d in range(1, 29) if tiles % d == 0 and (d < tiles or tiles == 1))
 
 
-def products(blocks, factors, starts, rows, band, width, order=None, resident=False):
+def products(blocks, factors, starts, rows, band, width, order=None, resident=False, limit=None):
     folds = len(factors)
     arrays, specs, flags, places = [], [], [], []
     tk = step_width(width)
@@ -110,6 +110,7 @@
             out_specs=pl.BlockSpec((groups, rows, band), lambda i, *s: (0, 0, 0)),
             scratch_shapes=[pltpu.VMEM((folds, groups * tall, band), jnp.float32)],
         ),
+        compiler_params=pltpu.CompilerParams(vmem_limit_bytes=limit),
         out_shape=jax.ShapeDtypeStruct((groups, rows, band), jnp.float32),
     )(*scalars, *arrays, *factors)
 
@@ -288,7 +289,7 @@
         factors, starts = [factor_band] * folds, starts_of("x")
         if whose == "far":
             factors, starts = [have["x", "f", 0]] * folds, [(f * band, 0) for f in range(folds)]
-        sums = products(blocks, factors, starts, rows, band, sizes["x"] * LANE, order, whose == "far")
+        sums = products(blocks, factors, starts, rows, band, sizes["x"] * LANE, order, whose == "far", limit=66_900_000 if whose == "far" else None)
         have["x", whose, 0] = sums
 
     def place(sums):

time: 235 us -> 234 us (level)
  no operation moved by 1% of the time
where the time goes in v6:
time: 234 us
  waiting for transfers between devices  113 us (48%)
  starting transfers between devices  61.3 us (26%)
  Pallas kernels  49.2 us (21%)
  local copies, waits for them, and re-layouts  5.09 us (2%)
  other arithmetic  3.22 us (1%)
    ppermute x32, waiting for transfers between devices, body(): send = lambda x, pairs: lax.ppermute(x, 'row', pairs)  111 us
    ppermute x32, starting transfers between devices, body(): send = lambda x, pairs: lax.ppermute(x, 'row', pairs)  59.4 us
    pallas_call x9, Pallas kernels, products(): pl.pallas_call(kernel, grid_spec=pltpu.PrefetchScalarGridSpec(num_scalar_...  41.4 us
    pallas_call x4, Pallas kernels, choose(): pl.pallas_call(kernel, grid_spec=pltpu.PrefetchScalarGridSpec(num_scalar_...  7.79 us
  transfers between devices with their start and end apart: 35, of which 13 were waited for; matrix products, arithmetic and copies ran while one was open for 2% of the time, Pallas kernels for 21%

profile of v6, /device:TPU:0, one launch (start us, length us, event | category | flops | bytes accessed | tf_op | source)
XLA Modules:
  0.0 233.5 jit_solution(12268462967550134154)
XLA Ops:
  1.3 3.1 %collective-permute-start.23 = (f32[24,4608]{1,0:T(8,128)S(1)}, f32[24,4608]{1,0:T(8,128)S(1)}, u32[]{:S(2)}, u32[]{:S(2)}) collective-permute-start(f32[24,4608]{1,0:T(8,128)S(1)} %pad_maximum_fusion.4.refs_0_), channel_id=1, source_target_pairs={{0,4},{4,0},{8,12},{12,8},{16,20},{20,16},{24,28},{28,24},{1,5},{5... | collective-permute-start | bytes 1327112 | tf_op jit(solution)/shard_map/ppermute | solution.py:230
  4.4 1.6 collective-permute-start.7
  6.8 2.0 collective-permute-start.15
  8.8 1.8 fusion.18
  10.6 4.8 %collective-permute-done.23.refs_1_ = f32[24,4608]{1,0:T(8,128)S(1)} collective-permute-done((f32[24,4608]{1,0:T(8,128)S(1)}, f32[24,4608]{1,0:T(8,128)S(1)}, u32[]{:S(2)}, u32[]{:S(2)}) %collective-permute-start.23) | collective-permute-done | bytes 442400 | tf_op jit(solution)/shard_map/ppermute | solution.py:230
  16.1 22.7 %collective-permute-done.15 = f32[24,5120]{1,0:T(8,128)S(1)} collective-permute-done((f32[24,5120]{1,0:T(8,128)S(1)}, f32[24,5120]{1,0:T(8,128)S(1)}, u32[]{:S(2)}, u32[]{:S(2)}) %collective-permute-start.15) | collective-permute-done | bytes 491552 | tf_op jit(solution)/shard_map/ppermute | solution.py:230
  38.8 1.5 collective-permute-start
  40.4 1.8 collective-permute-start.8
  42.9 1.3 collective-permute-start.10
  44.2 7.2 %collective-permute-start.24 = (f32[48,2304]{1,0:T(8,128)S(1)}, f32[48,2304]{1,0:T(8,128)S(1)}, u32[]{:S(2)}, u32[]{:S(2)}) collective-permute-start(f32[48,2304]{1,0:T(8,128)S(1)} %slice.180.refs_1_), channel_id=1, source_target_pairs={{0,8},{4,12},{24,16},{28,20},{1,9},{5,13},{25,17},{29,21},{2,10},{... | collective-permute-start | bytes 1327112 | tf_op jit(solution)/shard_map/ppermute | solution.py:230
  51.5 1.6 pad_maximum_fusion
  53.0 10.0 %collective-permute-start.26 = (f32[256,2304]{1,0:T(8,128)}, f32[256,2304]{1,0:T(8,128)}, u32[]{:S(2)}, u32[]{:S(2)}) collective-permute-start(f32[256,2304]{1,0:T(8,128)} %pad_maximum_fusion), channel_id=1, source_target_pairs={{0,8},{4,12},{24,16},{28,20},{1,9},{5,13},{25,17},{29,21},{2,10},{... | collective-permute-start | bytes 7077896 | tf_op jit(solution)/shard_map/ppermute | solution.py:230
  63.1 1.6 collective-permute-start.3
  64.7 1.5 collective-permute-start.21
  66.2 1.3 collective-permute-start.1
  67.6 3.9 %collective-permute-start.18 = (f32[48,2816]{1,0:T(8,128)S(1)}, f32[48,2816]{1,0:T(8,128)}, u32[]{:S(2)}, u32[]{:S(2)}) collective-permute-start(f32[48,2816]{1,0:T(8,128)S(1)} %slice.157.refs_0_), channel_id=1, source_target_pairs={{0,8},{4,12},{8,0},{12,4},{16,24},{20,28},{24,16},{28,20},{1,9},{5... | collective-permute-start | bytes 1622024 | tf_op jit(solution)/shard_map/ppermute | solution.py:230
  71.5 1.3 collective-permute-start.5
  72.7 48.5 %collective-permute-done.18.refs_1_ = f32[48,2816]{1,0:T(8,128)} collective-permute-done((f32[48,2816]{1,0:T(8,128)S(1)}, f32[48,2816]{1,0:T(8,128)}, u32[]{:S(2)}, u32[]{:S(2)}) %collective-permute-start.18) | collective-permute-done | bytes 540704 | tf_op jit(solution)/shard_map/ppermute | solution.py:230
  122.1 1.9 shard_map.94.refs_1_
  125.8 6.7 %collective-permute-done.12.refs_2_ = f32[24,4608]{1,0:T(8,128)S(1)} collective-permute-done((f32[24,4608]{1,0:T(8,128)}, f32[24,4608]{1,0:T(8,128)S(1)}, u32[]{:S(2)}, u32[]{:S(2)}) %collective-permute-start.12) | collective-permute-done | bytes 442400 | tf_op jit(solution)/shard_map/ppermute | solution.py:230
  132.5 1.5 collective-permute-start.19
  134.0 3.6 %collective-permute-done.13.a_ref = f32[24,4608]{1,0:T(8,128)S(1)} collective-permute-done((f32[24,4608]{1,0:T(8,128)}, f32[24,4608]{1,0:T(8,128)S(1)}, u32[]{:S(2)}, u32[]{:S(2)}) %collective-permute-start.13) | collective-permute-done | bytes 442400 | tf_op jit(solution)/shard_map/ppermute | solution.py:230
  139.1 1.9 shard_map.95.refs_3_
  141.0 1.6 collective-permute-start.14
  142.5 2.0 shard_map.91.refs_1_
  144.5 2.0 shard_map.92.refs_1_
  147.3 1.4 collective-permute-start.6
  148.8 1.3 collective-permute-start.17
  150.1 4.3 %collective-permute-done.14.refs_4_ = f32[24,4608]{1,0:T(8,128)} collective-permute-done((f32[24,4608]{1,0:T(8,128)}, f32[24,4608]{1,0:T(8,128)}, u32[]{:S(2)}, u32[]{:S(2)}) %collective-permute-start.14) | collective-permute-done | bytes 442400 | tf_op jit(solution)/shard_map/ppermute | solution.py:230
  156.4 4.4 %shard_map.100 = f32[3,12,128]{2,1,0:T(8,128)} custom-call(f32[24,4608]{1,0:T(8,128)} %copy-done.8, f32[24,4608]{1,0:T(8,128)} %copy-done.18, f32[24,4608]{1,0:T(8,128)} %copy-done.19, f32[128,32768]{1,0:T(8,128)} %refs_6_.5, f32[128,32768]{1,0:T(8,128)} %refs_6_.5), custom_call_target="tpu_custom_call" | custom-call | tf_op jit(solution)/shard_map/pallas_call | solution.py:104
  160.8 5.5 %shard_map.99 = f32[3,12,128]{2,1,0:T(8,128)} custom-call(f32[24,6656]{1,0:T(8,128)} %copy-done.2, f32[24,6656]{1,0:T(8,128)} %copy-done.9, f32[24,6656]{1,0:T(8,128)} %collective-permute-done.2.refs_2_, f32[128,32768]{1,0:T(8,128)} %refs_6_.5, f32[128,32768]{1,0:T(8,128)} %refs_6_.5), custom_call_target="tpu_custom_call" | custom-call | tf_op jit(solution)/shard_map/pallas_call | solution.py:104
  166.2 3.4 %shard_map.101 = f32[4,12,128]{2,1,0:T(8,128)} custom-call(f32[48,2816]{1,0:T(8,128)} %copy-done.3, f32[48,2816]{1,0:T(8,128)} %collective-permute-done.18.refs_1_, f32[128,32768]{1,0:T(8,128)} %refs_6_.5, f32[128,32768]{1,0:T(8,128)} %refs_6_.5), custom_call_target="tpu_custom_call" | custom-call | tf_op jit(solution)/shard_map/pallas_call | solution.py:104
  169.6 5.4 %shard_map.98 = f32[2,12,128]{2,1,0:T(8,128)} custom-call(f32[24,6656]{1,0:T(8,128)} %collective-permute-done.21.refs_0_, f32[24,6656]{1,0:T(8,128)} %shard_map.91.refs_1_, f32[128,32768]{1,0:T(8,128)} %refs_6_.5, f32[128,32768]{1,0:T(8,128)} %refs_6_.5), custom_call_target="tpu_custom_call" | custom-call | tf_op jit(solution)/shard_map/pallas_call | solution.py:104
  175.0 4.4 %shard_map.103 = f32[8,12,128]{2,1,0:T(8,128)} custom-call(s32[8]{0:T(128)} %fusion.14.refs_0_, f32[48,2304]{1,0:T(8,128)} %copy-done.1, f32[48,2304]{1,0:T(8,128)} %copy-done.6, f32[48,5120]{1,0:T(8,128)} %copy-done, f32[48,2304]{1,0:T(8,128)} %copy-done.7, f32[128,32768]{1,0:T(8,128)} %refs_6_.5, f32[128,32768]{1,0:T(8,128)} %refs_6_.5), custom_call_target="tpu_custom_call" | custom-call | tf_op jit(solution)/shard_map/pallas_call | solution.py:104
  179.3 4.7 %shard_map.96 = f32[5,12,128]{2,1,0:T(8,128)} custom-call(f32[24,4608]{1,0:T(8,128)} %copy-done.12, f32[24,4608]{1,0:T(8,128)} %shard_map.94.refs_1_, f32[24,4608]{1,0:T(8,128)} %copy-done.13, f32[24,4608]{1,0:T(8,128)} %shard_map.95.refs_3_, f32[24,4608]{1,0:T(8,128)} %collective-permute-done.14.refs_4_, f32[128,32768]{1,0:T(8,128)} %refs_6_.5, ...), custom_call_target="tpu_custom_call" | custom-call | tf_op jit(solution)/shard_map/pallas_call | solution.py:104
  184.0 5.1 %collective-permute-done.20.refs_4_ = f32[48,2816]{1,0:T(8,128)S(1)} collective-permute-done((f32[48,2816]{1,0:T(8,128)}, f32[48,2816]{1,0:T(8,128)S(1)}, u32[]{:S(2)}, u32[]{:S(2)}) %collective-permute-start.20) | collective-permute-done | bytes 540704 | tf_op jit(solution)/shard_map/ppermute | solution.py:230
  189.9 3.6 %shard_map.97 = f32[4,12,128]{2,1,0:T(8,128)} custom-call(s32[1]{0:T(128)} %bitcast.flag_ref.refs_0_, s32[1]{0:T(128)} %bitcast.2.flag_ref.refs_1_, f32[48,2816]{1,0:T(8,128)} %copy-done.10, f32[48,2816]{1,0:T(8,128)} %collective-permute-done.19.refs_3_, f32[48,2816]{1,0:T(8,128)} %copy-done.11, f32[48,2816]{1,0:T(8,128)} %copy-done.4, ...), custom_call_target="tpu_custom_call" | custom-call | tf_op jit(solution)/shard_map/pallas_call | solution.py:104
  193.5 4.8 %shard_map.102 = f32[8,12,128]{2,1,0:T(8,128)} custom-call(s32[8]{0:T(128)} %fusion.14.refs_0_, f32[48,2304]{1,0:T(8,128)} %copy-done.1, f32[48,2304]{1,0:T(8,128)} %copy-done.6, f32[48,5120]{1,0:T(8,128)} %copy-done, f32[48,2304]{1,0:T(8,128)} %copy-done.7, f32[256,2304]{1,0:T(8,128)} %collective-permute-done.26.refs_5_), custom_call_target="tpu_custom_call" | custom-call | tf_op jit(solution)/shard_map/pallas_call | solution.py:104
  198.3 1.4 collective-permute-start.27
  199.8 5.5 %shard_map.93 = f32[3,12,128]{2,1,0:T(8,128)} custom-call(f32[24,6656]{1,0:T(8,128)} %collective-permute-done.4.refs_0_, f32[24,6656]{1,0:T(8,128)} %shard_map.92.refs_1_, f32[24,6656]{1,0:T(8,128)} %collective-permute-done.6.refs_2_, f32[128,32768]{1,0:T(8,128)} %refs_6_.5, f32[128,32768]{1,0:T(8,128)} %refs_6_.5), custom_call_target="tpu_custom_call" | custom-call | tf_op jit(solution)/shard_map/pallas_call | solution.py:104
  206.2 7.7 %collective-permute-done.27 = f32[8,12,128]{2,1,0:T(8,128)S(1)} collective-permute-done((f32[8,12,128]{2,1,0:T(8,128)}, f32[8,12,128]{2,1,0:T(8,128)S(1)}, u32[]{:S(2)}, u32[]{:S(2)}) %collective-permute-start.27) | collective-permute-done | bytes 49184 | tf_op jit(solution)/shard_map/ppermute | solution.py:230
  214.0 1.6 collective-permute-start.29
  215.8 1.3 collective-permute-done.30
  218.6 3.0 %collective-permute-done.31 = f32[25,128]{1,0:T(8,128)S(1)} collective-permute-done((f32[25,128]{1,0:T(8,128)S(1)}, f32[25,128]{1,0:T(8,128)S(1)}, u32[]{:S(2)}, u32[]{:S(2)}) %collective-permute-start.31) | collective-permute-done | bytes 12832 | tf_op jit(solution)/shard_map/ppermute | solution.py:230
  221.6 4.0 %collective-permute-start.32 = (f32[25,256]{1,0:T(8,128)S(1)}, f32[25,256]{1,0:T(8,128)S(1)}, u32[]{:S(2)}, u32[]{:S(2)}) collective-permute-start(f32[25,256]{1,0:T(8,128)S(1)} %pad_maximum_fusion.5), channel_id=1, source_target_pairs={{0,8},{4,12},{8,0},{12,4},{16,24},{20,28},{24,16},{28,20},{1,9},{5... | collective-permute-start | bytes 76808 | tf_op jit(solution)/shard_map/ppermute | solution.py:230
  226.7 1.4 collective-permute-start.34
  228.1 2.9 %collective-permute-done.33 = f32[25,256]{1,0:T(8,128)S(1)} collective-permute-done((f32[25,256]{1,0:T(8,128)S(1)}, f32[25,256]{1,0:T(8,128)S(1)}, u32[]{:S(2)}, u32[]{:S(2)}) %collective-permute-start.33) | collective-permute-done | bytes 25632 | tf_op jit(solution)/shard_map/ppermute | solution.py:230
  231.0 1.4 collective-permute-done.34
  (139 shorter events, 15.9 us)
Async XLA Ops:
  1.3 14.1 %collective-permute-start.23 = (f32[24,4608]{1,0:T(8,128)S(1)}, f32[24,4608]{1,0:T(8,128)S(1)}, u32[]{:S(2)}, u32[]{:S(2)}) collective-permute-start(f32[24,4608]{1,0:T(8,128)S(1)} %pad_maximum_fusion.4.refs_0_), channel_id=1, source_target_pairs={{0,4},{4,0},{8,12},{12,8},{16,20},{20,16},{24,28},{28,24},{1,5},{5... | collective-permute-start | bytes 1327112 | tf_op jit(solution)/shard_map/ppermute | solution.py:230
  4.4 36.0 %collective-permute-start.7 = (f32[24,4608]{1,0:T(8,128)S(1)}, f32[24,4608]{1,0:T(8,128)S(1)}, u32[]{:S(2)}, u32[]{:S(2)}) collective-permute-start(f32[24,4608]{1,0:T(8,128)S(1)} %pad_maximum_fusion.4.refs_0_), channel_id=1, source_target_pairs={{0,8},{4,12},{8,0},{12,4},{16,24},{20,28},{24,16},{28,20},{1,9},{5... | collective-permute-start | bytes 1327112 | tf_op jit(solution)/shard_map/ppermute | solution.py:230
  6.1 32.7 %copy-start.2 = (f32[24,6656]{1,0:T(8,128)}, f32[24,6656]{1,0:T(8,128)S(1)}, u32[]{:S(2)}) copy-start(f32[24,6656]{1,0:T(8,128)S(1)} %pad_maximum_fusion.2.refs_0_) | copy-start | bytes 1916932
  6.1 36.8 %collective-permute-start.22 = (f32[24,6656]{1,0:T(8,128)S(1)}, f32[24,6656]{1,0:T(8,128)S(1)}, u32[]{:S(2)}, u32[]{:S(2)}) collective-permute-start(f32[24,6656]{1,0:T(8,128)S(1)} %pad_maximum_fusion.2.refs_0_), channel_id=1, source_target_pairs={{0,4},{4,0},{8,12},{12,8},{16,20},{20,16},{24,28},{28,24},{1,5},{5... | collective-permute-start | bytes 1916936 | tf_op jit(solution)/shard_map/ppermute | solution.py:230
  6.7 37.6 %collective-permute-start.2 = (f32[24,6656]{1,0:T(8,128)S(1)}, f32[24,6656]{1,0:T(8,128)}, u32[]{:S(2)}, u32[]{:S(2)}) collective-permute-start(f32[24,6656]{1,0:T(8,128)S(1)} %pad_maximum_fusion.2.refs_0_), channel_id=1, source_target_pairs={{0,8},{4,12},{8,0},{12,4},{16,24},{20,28},{24,16},{28,20},{1,9},{5... | collective-permute-start | bytes 1916936 | tf_op jit(solution)/shard_map/ppermute | solution.py:230
  6.8 32.0 %collective-permute-start.15 = (f32[24,5120]{1,0:T(8,128)S(1)}, f32[24,5120]{1,0:T(8,128)S(1)}, u32[]{:S(2)}, u32[]{:S(2)}) collective-permute-start(f32[24,5120]{1,0:T(8,128)S(1)} %pad_maximum_fusion.3), channel_id=1, source_target_pairs={{0,4},{4,0},{8,12},{12,8},{16,20},{20,16},{24,28},{28,24},{1,5},{5... | collective-permute-start | bytes 1474568 | tf_op jit(solution)/shard_map/ppermute | solution.py:230
  15.4 36.1 %copy-start.18 = (f32[24,4608]{1,0:T(8,128)}, f32[24,4608]{1,0:T(8,128)S(1)}, u32[]{:S(2)}) copy-start(f32[24,4608]{1,0:T(8,128)S(1)} %collective-permute-done.23.refs_1_) | copy-start | bytes 1327108
  15.4 26.8 %collective-permute-start.9 = (f32[24,4608]{1,0:T(8,128)S(1)}, f32[24,4608]{1,0:T(8,128)S(1)}, u32[]{:S(2)}, u32[]{:S(2)}) collective-permute-start(f32[24,4608]{1,0:T(8,128)S(1)} %pad_maximum_fusion.4.refs_0_), channel_id=1, source_target_pairs={{8,16},{12,20},{16,8},{20,12},{9,17},{13,21},{17,9},{21,13},{10,18... | collective-permute-start | bytes 1327112 | tf_op jit(solution)/shard_map/ppermute | solution.py:230
  38.8 14.3 %collective-permute-start = (f32[24,6656]{1,0:T(8,128)S(1)}, f32[24,6656]{1,0:T(8,128)}, u32[]{:S(2)}, u32[]{:S(2)}) collective-permute-start(f32[24,6656]{1,0:T(8,128)S(1)} %pad_maximum_fusion.2.refs_0_), channel_id=1, source_target_pairs={{8,16},{12,20},{16,8},{20,12},{9,17},{13,21},{17,9},{21,13},{10,18... | collective-permute-start | bytes 1916936 | tf_op jit(solution)/shard_map/ppermute | solution.py:230
  40.4 81.6 %copy-start.19 = (f32[24,4608]{1,0:T(8,128)}, f32[24,4608]{1,0:T(8,128)S(1)}, u32[]{:S(2)}) copy-start(f32[24,4608]{1,0:T(8,128)S(1)} %collective-permute-done.7.refs_2_) | copy-start | bytes 1327108
  40.4 22.7 %collective-permute-start.8 = (f32[24,4608]{1,0:T(8,128)S(1)}, f32[24,4608]{1,0:T(8,128)S(1)}, u32[]{:S(2)}, u32[]{:S(2)}) collective-permute-start(f32[24,4608]{1,0:T(8,128)S(1)} %collective-permute-done.7.refs_2_), channel_id=1, source_target_pairs={{0,4},{4,0},{8,12},{12,8},{16,20},{20,16},{24,28},{28,24},{1,5},{5... | collective-permute-start | bytes 1327112 | tf_op jit(solution)/shard_map/ppermute | solution.py:230
  42.2 79.8 %copy-start.14 = (f32[24,4608]{1,0:T(8,128)}, f32[24,4608]{1,0:T(8,128)S(1)}, u32[]{:S(2)}) copy-start(f32[24,4608]{1,0:T(8,128)S(1)} %collective-permute-done.9.b_ref) | copy-start | bytes 1327108
  42.2 24.0 %collective-permute-start.11 = (f32[24,4608]{1,0:T(8,128)S(1)}, f32[24,4608]{1,0:T(8,128)S(1)}, u32[]{:S(2)}, u32[]{:S(2)}) collective-permute-start(f32[24,4608]{1,0:T(8,128)S(1)} %collective-permute-done.7.refs_2_), channel_id=1, source_target_pairs={{8,16},{12,20},{16,8},{20,12},{9,17},{13,21},{17,9},{21,13},{10,18... | collective-permute-start | bytes 1327112 | tf_op jit(solution)/shard_map/ppermute | solution.py:230
  42.9 21.7 %collective-permute-start.10 = (f32[24,4608]{1,0:T(8,128)S(1)}, f32[24,4608]{1,0:T(8,128)S(1)}, u32[]{:S(2)}, u32[]{:S(2)}) collective-permute-start(f32[24,4608]{1,0:T(8,128)S(1)} %collective-permute-done.9.b_ref), channel_id=1, source_target_pairs={{8,0},{12,4},{16,24},{20,28},{9,1},{13,5},{17,25},{21,29},{10,2},{... | collective-permute-start | bytes 1327112 | tf_op jit(solution)/shard_map/ppermute | solution.py:230
  44.2 23.3 %collective-permute-start.24 = (f32[48,2304]{1,0:T(8,128)S(1)}, f32[48,2304]{1,0:T(8,128)S(1)}, u32[]{:S(2)}, u32[]{:S(2)}) collective-permute-start(f32[48,2304]{1,0:T(8,128)S(1)} %slice.180.refs_1_), channel_id=1, source_target_pairs={{0,8},{4,12},{24,16},{28,20},{1,9},{5,13},{25,17},{29,21},{2,10},{... | collective-permute-start | bytes 1327112 | tf_op jit(solution)/shard_map/ppermute | solution.py:230
  53.0 140.4 %collective-permute-start.26 = (f32[256,2304]{1,0:T(8,128)}, f32[256,2304]{1,0:T(8,128)}, u32[]{:S(2)}, u32[]{:S(2)}) collective-permute-start(f32[256,2304]{1,0:T(8,128)} %pad_maximum_fusion), channel_id=1, source_target_pairs={{0,8},{4,12},{24,16},{28,20},{1,9},{5,13},{25,17},{29,21},{2,10},{... | collective-permute-start | bytes 7077896 | tf_op jit(solution)/shard_map/ppermute | solution.py:230
  63.1 58.9 %copy-start.12 = (f32[24,4608]{1,0:T(8,128)}, f32[24,4608]{1,0:T(8,128)S(1)}, u32[]{:S(2)}) copy-start(f32[24,4608]{1,0:T(8,128)S(1)} %collective-permute-done.8.refs_0_) | copy-start | bytes 1327108
  63.1 8.4 %collective-permute-start.3 = (f32[24,6656]{1,0:T(8,128)}, f32[24,6656]{1,0:T(8,128)}, u32[]{:S(2)}, u32[]{:S(2)}) collective-permute-start(f32[24,6656]{1,0:T(8,128)} %collective-permute-done.2.refs_2_), channel_id=1, source_target_pairs={{8,16},{12,20},{16,8},{20,12},{9,17},{13,21},{17,9},{21,13},{10,18... | collective-permute-start | bytes 1916936 | tf_op jit(solution)/shard_map/ppermute | solution.py:230
  64.7 57.4 %copy-start.16 = (f32[24,4608]{1,0:T(8,128)}, f32[24,4608]{1,0:T(8,128)S(1)}, u32[]{:S(2)}) copy-start(f32[24,4608]{1,0:T(8,128)S(1)} %collective-permute-done.10.a_ref) | copy-start | bytes 1327108
  64.7 59.3 %collective-permute-start.21 = (f32[24,6656]{1,0:T(8,128)}, f32[24,6656]{1,0:T(8,128)}, u32[]{:S(2)}, u32[]{:S(2)}) collective-permute-start(f32[24,6656]{1,0:T(8,128)} %collective-permute-done.2.refs_2_), channel_id=1, source_target_pairs={{0,4},{4,0},{8,12},{12,8},{16,20},{20,16},{24,28},{28,24},{1,5},{5... | collective-permute-start | bytes 1916936 | tf_op jit(solution)/shard_map/ppermute | solution.py:230
  66.2 55.9 %copy-start.15 = (f32[24,4608]{1,0:T(8,128)}, f32[24,4608]{1,0:T(8,128)S(1)}, u32[]{:S(2)}) copy-start(f32[24,4608]{1,0:T(8,128)S(1)} %collective-permute-done.11.b_ref) | copy-start | bytes 1327108
  66.2 58.3 %collective-permute-start.1 = (f32[24,6656]{1,0:T(8,128)}, f32[24,6656]{1,0:T(8,128)}, u32[]{:S(2)}, u32[]{:S(2)}) collective-permute-start(f32[24,6656]{1,0:T(8,128)} %collective-permute-done.b_ref), channel_id=1, source_target_pairs={{8,0},{12,4},{16,24},{20,28},{9,1},{13,5},{17,25},{21,29},{10,2},{... | collective-permute-start | bytes 1916936 | tf_op jit(solution)/shard_map/ppermute | solution.py:230
  67.5 77.0 %copy-start.3 = (f32[48,2816]{1,0:T(8,128)}, f32[48,2816]{1,0:T(8,128)S(1)}, u32[]{:S(2)}) copy-start(f32[48,2816]{1,0:T(8,128)S(1)} %slice.157.refs_0_) | copy-start | bytes 1622020
  67.5 77.0 %copy-start.6 = (f32[48,2304]{1,0:T(8,128)}, f32[48,2304]{1,0:T(8,128)S(1)}, u32[]{:S(2)}) copy-start(f32[48,2304]{1,0:T(8,128)S(1)} %collective-permute-done.24.refs_2_) | copy-start | bytes 1327108
  67.6 53.7 %collective-permute-start.18 = (f32[48,2816]{1,0:T(8,128)S(1)}, f32[48,2816]{1,0:T(8,128)}, u32[]{:S(2)}, u32[]{:S(2)}) collective-permute-start(f32[48,2816]{1,0:T(8,128)S(1)} %slice.157.refs_0_), channel_id=1, source_target_pairs={{0,8},{4,12},{8,0},{12,4},{16,24},{20,28},{24,16},{28,20},{1,9},{5... | collective-permute-start | bytes 1622024 | tf_op jit(solution)/shard_map/ppermute | solution.py:230
  71.5 69.5 %collective-permute-start.5 = (f32[24,6656]{1,0:T(8,128)}, f32[24,6656]{1,0:T(8,128)}, u32[]{:S(2)}, u32[]{:S(2)}) collective-permute-start(f32[24,6656]{1,0:T(8,128)} %collective-permute-done.3.b_ref), channel_id=1, source_target_pairs={{8,0},{12,4},{16,24},{20,28},{9,1},{13,5},{17,25},{21,29},{10,2},{... | collective-permute-start | bytes 1916936 | tf_op jit(solution)/shard_map/ppermute | solution.py:230
  121.3 25.9 %collective-permute-start.16 = (f32[48,5120]{1,0:T(8,128)S(1)}, f32[48,5120]{1,0:T(8,128)S(1)}, u32[]{:S(2)}, u32[]{:S(2)}) collective-permute-start(f32[48,5120]{1,0:T(8,128)S(1)} %pad_maximum_fusion.1), channel_id=1, source_target_pairs={{8,16},{12,20},{16,8},{20,12},{9,17},{13,21},{17,9},{21,13},{10,18... | collective-permute-start | bytes 2949128 | tf_op jit(solution)/shard_map/ppermute | solution.py:230
  124.0 8.6 %collective-permute-start.12 = (f32[24,4608]{1,0:T(8,128)}, f32[24,4608]{1,0:T(8,128)S(1)}, u32[]{:S(2)}, u32[]{:S(2)}) collective-permute-start(f32[24,4608]{1,0:T(8,128)} %shard_map.94.refs_1_), channel_id=1, source_target_pairs={{0,4},{4,0},{8,12},{12,8},{16,20},{20,16},{24,28},{28,24},{1,5},{5... | collective-permute-start | bytes 1327112 | tf_op jit(solution)/shard_map/ppermute | solution.py:230
  124.5 13.1 %collective-permute-start.13 = (f32[24,4608]{1,0:T(8,128)}, f32[24,4608]{1,0:T(8,128)S(1)}, u32[]{:S(2)}, u32[]{:S(2)}) collective-permute-start(f32[24,4608]{1,0:T(8,128)} %copy-done.15), channel_id=1, source_target_pairs={{8,0},{12,4},{16,24},{20,28},{9,1},{13,5},{17,25},{21,29},{10,2},{... | collective-permute-start | bytes 1327112 | tf_op jit(solution)/shard_map/ppermute | solution.py:230
  132.5 16.2 %collective-permute-start.19 = (f32[48,2816]{1,0:T(8,128)}, f32[48,2816]{1,0:T(8,128)}, u32[]{:S(2)}, u32[]{:S(2)}) collective-permute-start(f32[48,2816]{1,0:T(8,128)} %collective-permute-done.18.refs_1_), channel_id=1, source_target_pairs={{8,16},{12,20},{16,8},{20,12},{9,17},{13,21},{17,9},{21,13},{10,18... | collective-permute-start | bytes 1622024 | tf_op jit(solution)/shard_map/ppermute | solution.py:230
  138.4 8.2 %collective-permute-start.25 = (f32[48,2304]{1,0:T(8,128)S(1)}, f32[48,2304]{1,0:T(8,128)S(1)}, u32[]{:S(2)}, u32[]{:S(2)}) collective-permute-start(f32[48,2304]{1,0:T(8,128)S(1)} %collective-permute-done.24.refs_2_), channel_id=1, source_target_pairs={{8,16},{12,20},{16,8},{20,12},{9,17},{13,21},{17,9},{21,13},{10,18... | collective-permute-start | bytes 1327112 | tf_op jit(solution)/shard_map/ppermute | solution.py:230
  141.0 13.4 %collective-permute-start.14 = (f32[24,4608]{1,0:T(8,128)}, f32[24,4608]{1,0:T(8,128)}, u32[]{:S(2)}, u32[]{:S(2)}) collective-permute-start(f32[24,4608]{1,0:T(8,128)} %shard_map.95.refs_3_), channel_id=1, source_target_pairs={{0,4},{4,0},{8,12},{12,8},{16,20},{20,16},{24,28},{28,24},{1,5},{5... | collective-permute-start | bytes 1327112 | tf_op jit(solution)/shard_map/ppermute | solution.py:230
  146.5 53.2 %collective-permute-start.4 = (f32[24,6656]{1,0:T(8,128)}, f32[24,6656]{1,0:T(8,128)}, u32[]{:S(2)}, u32[]{:S(2)}) collective-permute-start(f32[24,6656]{1,0:T(8,128)} %shard_map.91.refs_1_), channel_id=1, source_target_pairs={{0,4},{4,0},{8,12},{12,8},{16,20},{20,16},{24,28},{28,24},{1,5},{5... | collective-permute-start | bytes 1916936 | tf_op jit(solution)/shard_map/ppermute | solution.py:230
  147.3 52.5 %collective-permute-start.6 = (f32[24,6656]{1,0:T(8,128)}, f32[24,6656]{1,0:T(8,128)}, u32[]{:S(2)}, u32[]{:S(2)}) collective-permute-start(f32[24,6656]{1,0:T(8,128)} %shard_map.92.refs_1_), channel_id=1, source_target_pairs={{0,4},{4,0},{8,12},{12,8},{16,20},{20,16},{24,28},{28,24},{1,5},{5... | collective-permute-start | bytes 1916936 | tf_op jit(solution)/shard_map/ppermute | solution.py:230
  148.8 35.3 %collective-permute-start.17 = (f32[48,2816]{1,0:T(8,128)S(1)}, f32[48,2816]{1,0:T(8,128)S(1)}, u32[]{:S(2)}, u32[]{:S(2)}) collective-permute-start(f32[48,2816]{1,0:T(8,128)S(1)} %slice.156.refs_5_), channel_id=1, source_target_pairs={{8,0},{12,4},{16,24},{20,28},{9,1},{13,5},{17,25},{21,29},{10,2},{... | collective-permute-start | bytes 1622024 | tf_op jit(solution)/shard_map/ppermute | solution.py:230
  154.4 34.7 %collective-permute-start.20 = (f32[48,2816]{1,0:T(8,128)}, f32[48,2816]{1,0:T(8,128)S(1)}, u32[]{:S(2)}, u32[]{:S(2)}) collective-permute-start(f32[48,2816]{1,0:T(8,128)} %collective-permute-done.19.refs_3_), channel_id=1, source_target_pairs={{8,0},{12,4},{16,24},{20,28},{9,1},{13,5},{17,25},{21,29},{10,2},{... | collective-permute-start | bytes 1622024 | tf_op jit(solution)/shard_map/ppermute | solution.py:230
  198.3 17.5 %copy-start.33 = (s32[128]{0:T(128)S(1)}, s32[128]{0:T(128)}, u32[]{:S(2)}) copy-start(s32[128]{0:T(128)} %param.14) | copy-start | bytes 1540
  198.3 19.4 %copy-start.27 = (f32[128]{0:T(128)S(1)}, f32[128]{0:T(128)}, u32[]{:S(2)}) copy-start(f32[128]{0:T(128)} %param.13) | copy-start | bytes 1540
  198.3 19.4 %copy-start.28 = (f32[128]{0:T(128)S(1)}, f32[128]{0:T(128)}, u32[]{:S(2)}) copy-start(f32[128]{0:T(128)} %param.12) | copy-start | bytes 1540
  198.3 19.4 %copy-start.29 = (f32[128]{0:T(128)S(1)}, f32[128]{0:T(128)}, u32[]{:S(2)}) copy-start(f32[128]{0:T(128)} %param.11) | copy-start | bytes 1540
  198.3 15.5 %collective-permute-start.27 = (f32[8,12,128]{2,1,0:T(8,128)}, f32[8,12,128]{2,1,0:T(8,128)S(1)}, u32[]{:S(2)}, u32[]{:S(2)}) collective-permute-start(f32[8,12,128]{2,1,0:T(8,128)} %shard_map.102), channel_id=1, source_target_pairs={{8,0},{12,4},{16,24},{20,28},{9,1},{13,5},{17,25},{21,29},{10,2},{... | collective-permute-start | bytes 147464 | tf_op jit(solution)/shard_map/ppermute | solution.py:230
  213.9 3.3 %collective-permute-start.30 = (f32[24,128]{1,0:T(8,128)S(1)}, f32[24,128]{1,0:T(8,128)S(1)}, u32[]{:S(2)}, u32[]{:S(2)}) collective-permute-start(f32[24,128]{1,0:T(8,128)S(1)} %get-tuple-element.34), channel_id=1, source_target_pairs={{0,3},{1,2},{2,1},{3,0},{4,7},{5,6},{6,5},{7,4},{8,11},{9,10},{10,... | collective-permute-start | bytes 36872 | tf_op jit(solution)/shard_map/ppermute | solution.py:345
  214.0 3.8 %collective-permute-start.29 = (f32[24,128]{1,0:T(8,128)S(1)}, f32[24,128]{1,0:T(8,128)S(1)}, u32[]{:S(2)}, u32[]{:S(2)}) collective-permute-start(f32[24,128]{1,0:T(8,128)S(1)} %get-tuple-element.35), channel_id=1, source_target_pairs={{0,2},{1,3},{2,0},{3,1},{4,6},{5,7},{6,4},{7,5},{8,10},{9,11},{10,... | collective-permute-start | bytes 36872 | tf_op jit(solution)/shard_map/ppermute | solution.py:345
  215.5 2.2 collective-permute-start.28
  217.8 3.8 %collective-permute-start.31 = (f32[25,128]{1,0:T(8,128)S(1)}, f32[25,128]{1,0:T(8,128)S(1)}, u32[]{:S(2)}, u32[]{:S(2)}) collective-permute-start(f32[25,128]{1,0:T(8,128)S(1)} %get-tuple-element.36), channel_id=1, source_target_pairs={{0,4},{4,0},{8,12},{12,8},{16,20},{20,16},{24,28},{28,24},{1,5},{5... | collective-permute-start | bytes 38408 | tf_op jit(solution)/shard_map/ppermute | solution.py:230
  221.6 6.5 %collective-permute-start.32 = (f32[25,256]{1,0:T(8,128)S(1)}, f32[25,256]{1,0:T(8,128)S(1)}, u32[]{:S(2)}, u32[]{:S(2)}) collective-permute-start(f32[25,256]{1,0:T(8,128)S(1)} %pad_maximum_fusion.5), channel_id=1, source_target_pairs={{0,8},{4,12},{8,0},{12,4},{16,24},{20,28},{24,16},{28,20},{1,9},{5... | collective-permute-start | bytes 76808 | tf_op jit(solution)/shard_map/ppermute | solution.py:230
  225.6 5.4 %collective-permute-start.33 = (f32[25,256]{1,0:T(8,128)S(1)}, f32[25,256]{1,0:T(8,128)S(1)}, u32[]{:S(2)}, u32[]{:S(2)}) collective-permute-start(f32[25,256]{1,0:T(8,128)S(1)} %pad_maximum_fusion.5), channel_id=1, source_target_pairs={{0,16},{4,20},{8,24},{12,28},{16,0},{20,4},{24,8},{28,12},{1,17},{... | collective-permute-start | bytes 76808 | tf_op jit(solution)/shard_map/ppermute | solution.py:230
  226.7 5.7 %collective-permute-start.34 = (f32[25,256]{1,0:T(8,128)S(1)}, f32[25,256]{1,0:T(8,128)S(1)}, u32[]{:S(2)}, u32[]{:S(2)}) collective-permute-start(f32[25,256]{1,0:T(8,128)S(1)} %pad_maximum_fusion.5), channel_id=1, source_target_pairs={{0,24},{4,28},{8,16},{12,20},{16,8},{20,12},{24,0},{28,4},{1,25},{... | collective-permute-start | bytes 76808 | tf_op jit(solution)/shard_map/ppermute | solution.py:230
  (21 other events, 170.7 us)

commit v7 on v6

--- a/solution.py
+++ b/solution.py
@@ -352,9 +352,10 @@
 
     power = jnp.concatenate([power, site_plant[None, :].astype(jnp.float32)], axis=0)
     pair = jnp.concatenate([power, send(power, side)], axis=1)
-    table = jnp.concatenate(
-        [pair] + [send(pair, line(lambda p, k=k: p ^ k)) for k in range(1, planes)], axis=1
-    )
+    came = []
+    for k in range(1, planes):
+        came.append(send(pair, line(lambda p, k=k: p ^ k)))
+    table = jnp.concatenate([pair] + came, axis=1)
     plant = table[share].astype(jnp.int32)
     mine = PLANTS // row_size
     onehot = (plant[:, None] == row * mine + jnp.arange(mine, dtype=jnp.int32)[None, :]).astype(jnp.float32)

time: 234 us -> 234 us (level)
  no operation moved by 1% of the time
where the time goes in v7:
time: 234 us
  waiting for transfers between devices  113 us (48%)
  starting transfers between devices  61.3 us (26%)
  Pallas kernels  49.2 us (21%)
  local copies, waits for them, and re-layouts  5.09 us (2%)
  other arithmetic  3.22 us (1%)
    ppermute x32, waiting for transfers between devices, body(): send = lambda x, pairs: lax.ppermute(x, 'row', pairs)  111 us
    ppermute x32, starting transfers between devices, body(): send = lambda x, pairs: lax.ppermute(x, 'row', pairs)  59.4 us
    pallas_call x9, Pallas kernels, products(): pl.pallas_call(kernel, grid_spec=pltpu.PrefetchScalarGridSpec(num_scalar_...  41.4 us
    pallas_call x4, Pallas kernels, choose(): pl.pallas_call(kernel, grid_spec=pltpu.PrefetchScalarGridSpec(num_scalar_...  7.79 us
  transfers between devices with their start and end apart: 35, of which 13 were waited for; matrix products, arithmetic and copies ran while one was open for 2% of the time, Pallas kernels for 21%

profile of v7, /device:TPU:0, one launch (start us, length us, event | category | flops | bytes accessed | tf_op | source)
XLA Modules:
  0.0 233.5 jit_solution(12268462967550134154)
XLA Ops:
  1.3 3.1 %collective-permute-start.23 = (f32[24,4608]{1,0:T(8,128)S(1)}, f32[24,4608]{1,0:T(8,128)S(1)}, u32[]{:S(2)}, u32[]{:S(2)}) collective-permute-start(f32[24,4608]{1,0:T(8,128)S(1)} %pad_maximum_fusion.4.refs_0_), channel_id=1, source_target_pairs={{0,4},{4,0},{8,12},{12,8},{16,20},{20,16},{24,28},{28,24},{1,5},{5... | collective-permute-start | bytes 1327112 | tf_op jit(solution)/shard_map/ppermute | solution.py:230
  4.4 1.6 collective-permute-start.7
  6.8 2.0 collective-permute-start.15
  8.8 1.8 fusion.18
  10.6 4.8 %collective-permute-done.23.refs_1_ = f32[24,4608]{1,0:T(8,128)S(1)} collective-permute-done((f32[24,4608]{1,0:T(8,128)S(1)}, f32[24,4608]{1,0:T(8,128)S(1)}, u32[]{:S(2)}, u32[]{:S(2)}) %collective-permute-start.23) | collective-permute-done | bytes 442400 | tf_op jit(solution)/shard_map/ppermute | solution.py:230
  16.1 22.7 %collective-permute-done.15 = f32[24,5120]{1,0:T(8,128)S(1)} collective-permute-done((f32[24,5120]{1,0:T(8,128)S(1)}, f32[24,5120]{1,0:T(8,128)S(1)}, u32[]{:S(2)}, u32[]{:S(2)}) %collective-permute-start.15) | collective-permute-done | bytes 491552 | tf_op jit(solution)/shard_map/ppermute | solution.py:230
  38.8 1.5 collective-permute-start
  40.4 1.8 collective-permute-start.8
  42.9 1.3 collective-permute-start.10
  44.2 7.2 %collective-permute-start.24 = (f32[48,2304]{1,0:T(8,128)S(1)}, f32[48,2304]{1,0:T(8,128)S(1)}, u32[]{:S(2)}, u32[]{:S(2)}) collective-permute-start(f32[48,2304]{1,0:T(8,128)S(1)} %slice.180.refs_1_), channel_id=1, source_target_pairs={{0,8},{4,12},{24,16},{28,20},{1,9},{5,13},{25,17},{29,21},{2,10},{... | collective-permute-start | bytes 1327112 | tf_op jit(solution)/shard_map/ppermute | solution.py:230
  51.5 1.6 pad_maximum_fusion
  53.0 10.0 %collective-permute-start.26 = (f32[256,2304]{1,0:T(8,128)}, f32[256,2304]{1,0:T(8,128)}, u32[]{:S(2)}, u32[]{:S(2)}) collective-permute-start(f32[256,2304]{1,0:T(8,128)} %pad_maximum_fusion), channel_id=1, source_target_pairs={{0,8},{4,12},{24,16},{28,20},{1,9},{5,13},{25,17},{29,21},{2,10},{... | collective-permute-start | bytes 7077896 | tf_op jit(solution)/shard_map/ppermute | solution.py:230
  63.1 1.6 collective-permute-start.3
  64.7 1.5 collective-permute-start.21
  66.2 1.3 collective-permute-start.1
  67.6 3.9 %collective-permute-start.18 = (f32[48,2816]{1,0:T(8,128)S(1)}, f32[48,2816]{1,0:T(8,128)}, u32[]{:S(2)}, u32[]{:S(2)}) collective-permute-start(f32[48,2816]{1,0:T(8,128)S(1)} %slice.157.refs_0_), channel_id=1, source_target_pairs={{0,8},{4,12},{8,0},{12,4},{16,24},{20,28},{24,16},{28,20},{1,9},{5... | collective-permute-start | bytes 1622024 | tf_op jit(solution)/shard_map/ppermute | solution.py:230
  71.5 1.3 collective-permute-start.5
  72.7 48.5 %collective-permute-done.18.refs_1_ = f32[48,2816]{1,0:T(8,128)} collective-permute-done((f32[48,2816]{1,0:T(8,128)S(1)}, f32[48,2816]{1,0:T(8,128)}, u32[]{:S(2)}, u32[]{:S(2)}) %collective-permute-start.18) | collective-permute-done | bytes 540704 | tf_op jit(solution)/shard_map/ppermute | solution.py:230
  122.1 1.9 shard_map.94.refs_1_
  125.8 6.7 %collective-permute-done.12.refs_2_ = f32[24,4608]{1,0:T(8,128)S(1)} collective-permute-done((f32[24,4608]{1,0:T(8,128)}, f32[24,4608]{1,0:T(8,128)S(1)}, u32[]{:S(2)}, u32[]{:S(2)}) %collective-permute-start.12) | collective-permute-done | bytes 442400 | tf_op jit(solution)/shard_map/ppermute | solution.py:230
  132.5 1.5 collective-permute-start.19
  134.0 3.6 %collective-permute-done.13.a_ref = f32[24,4608]{1,0:T(8,128)S(1)} collective-permute-done((f32[24,4608]{1,0:T(8,128)}, f32[24,4608]{1,0:T(8,128)S(1)}, u32[]{:S(2)}, u32[]{:S(2)}) %collective-permute-start.13) | collective-permute-done | bytes 442400 | tf_op jit(solution)/shard_map/ppermute | solution.py:230
  139.1 1.9 shard_map.95.refs_3_
  141.0 1.6 collective-permute-start.14
  142.5 2.0 shard_map.91.refs_1_
  144.5 2.0 shard_map.92.refs_1_
  147.3 1.4 collective-permute-start.6
  148.8 1.3 collective-permute-start.17
  150.1 4.3 %collective-permute-done.14.refs_4_ = f32[24,4608]{1,0:T(8,128)} collective-permute-done((f32[24,4608]{1,0:T(8,128)}, f32[24,4608]{1,0:T(8,128)}, u32[]{:S(2)}, u32[]{:S(2)}) %collective-permute-start.14) | collective-permute-done | bytes 442400 | tf_op jit(solution)/shard_map/ppermute | solution.py:230
  156.4 4.4 %shard_map.100 = f32[3,12,128]{2,1,0:T(8,128)} custom-call(f32[24,4608]{1,0:T(8,128)} %copy-done.8, f32[24,4608]{1,0:T(8,128)} %copy-done.18, f32[24,4608]{1,0:T(8,128)} %copy-done.19, f32[128,32768]{1,0:T(8,128)} %refs_6_.5, f32[128,32768]{1,0:T(8,128)} %refs_6_.5), custom_call_target="tpu_custom_call" | custom-call | tf_op jit(solution)/shard_map/pallas_call | solution.py:104
  160.8 5.5 %shard_map.99 = f32[3,12,128]{2,1,0:T(8,128)} custom-call(f32[24,6656]{1,0:T(8,128)} %copy-done.2, f32[24,6656]{1,0:T(8,128)} %copy-done.9, f32[24,6656]{1,0:T(8,128)} %collective-permute-done.2.refs_2_, f32[128,32768]{1,0:T(8,128)} %refs_6_.5, f32[128,32768]{1,0:T(8,128)} %refs_6_.5), custom_call_target="tpu_custom_call" | custom-call | tf_op jit(solution)/shard_map/pallas_call | solution.py:104
  166.2 3.4 %shard_map.101 = f32[4,12,128]{2,1,0:T(8,128)} custom-call(f32[48,2816]{1,0:T(8,128)} %copy-done.3, f32[48,2816]{1,0:T(8,128)} %collective-permute-done.18.refs_1_, f32[128,32768]{1,0:T(8,128)} %refs_6_.5, f32[128,32768]{1,0:T(8,128)} %refs_6_.5), custom_call_target="tpu_custom_call" | custom-call | tf_op jit(solution)/shard_map/pallas_call | solution.py:104
  169.6 5.4 %shard_map.98 = f32[2,12,128]{2,1,0:T(8,128)} custom-call(f32[24,6656]{1,0:T(8,128)} %collective-permute-done.21.refs_0_, f32[24,6656]{1,0:T(8,128)} %shard_map.91.refs_1_, f32[128,32768]{1,0:T(8,128)} %refs_6_.5, f32[128,32768]{1,0:T(8,128)} %refs_6_.5), custom_call_target="tpu_custom_call" | custom-call | tf_op jit(solution)/shard_map/pallas_call | solution.py:104
  175.0 4.4 %shard_map.103 = f32[8,12,128]{2,1,0:T(8,128)} custom-call(s32[8]{0:T(128)} %fusion.14.refs_0_, f32[48,2304]{1,0:T(8,128)} %copy-done.1, f32[48,2304]{1,0:T(8,128)} %copy-done.6, f32[48,5120]{1,0:T(8,128)} %copy-done, f32[48,2304]{1,0:T(8,128)} %copy-done.7, f32[128,32768]{1,0:T(8,128)} %refs_6_.5, f32[128,32768]{1,0:T(8,128)} %refs_6_.5), custom_call_target="tpu_custom_call" | custom-call | tf_op jit(solution)/shard_map/pallas_call | solution.py:104
  179.3 4.7 %shard_map.96 = f32[5,12,128]{2,1,0:T(8,128)} custom-call(f32[24,4608]{1,0:T(8,128)} %copy-done.12, f32[24,4608]{1,0:T(8,128)} %shard_map.94.refs_1_, f32[24,4608]{1,0:T(8,128)} %copy-done.13, f32[24,4608]{1,0:T(8,128)} %shard_map.95.refs_3_, f32[24,4608]{1,0:T(8,128)} %collective-permute-done.14.refs_4_, f32[128,32768]{1,0:T(8,128)} %refs_6_.5, ...), custom_call_target="tpu_custom_call" | custom-call | tf_op jit(solution)/shard_map/pallas_call | solution.py:104
  184.0 5.1 %collective-permute-done.20.refs_4_ = f32[48,2816]{1,0:T(8,128)S(1)} collective-permute-done((f32[48,2816]{1,0:T(8,128)}, f32[48,2816]{1,0:T(8,128)S(1)}, u32[]{:S(2)}, u32[]{:S(2)}) %collective-permute-start.20) | collective-permute-done | bytes 540704 | tf_op jit(solution)/shard_map/ppermute | solution.py:230
  189.9 3.6 %shard_map.97 = f32[4,12,128]{2,1,0:T(8,128)} custom-call(s32[1]{0:T(128)} %bitcast.flag_ref.refs_0_, s32[1]{0:T(128)} %bitcast.2.flag_ref.refs_1_, f32[48,2816]{1,0:T(8,128)} %copy-done.10, f32[48,2816]{1,0:T(8,128)} %collective-permute-done.19.refs_3_, f32[48,2816]{1,0:T(8,128)} %copy-done.11, f32[48,2816]{1,0:T(8,128)} %copy-done.4, ...), custom_call_target="tpu_custom_call" | custom-call | tf_op jit(solution)/shard_map/pallas_call | solution.py:104
  193.5 4.8 %shard_map.102 = f32[8,12,128]{2,1,0:T(8,128)} custom-call(s32[8]{0:T(128)} %fusion.14.refs_0_, f32[48,2304]{1,0:T(8,128)} %copy-done.1, f32[48,2304]{1,0:T(8,128)} %copy-done.6, f32[48,5120]{1,0:T(8,128)} %copy-done, f32[48,2304]{1,0:T(8,128)} %copy-done.7, f32[256,2304]{1,0:T(8,128)} %collective-permute-done.26.refs_5_), custom_call_target="tpu_custom_call" | custom-call | tf_op jit(solution)/shard_map/pallas_call | solution.py:104
  198.3 1.4 collective-permute-start.27
  199.8 5.5 %shard_map.93 = f32[3,12,128]{2,1,0:T(8,128)} custom-call(f32[24,6656]{1,0:T(8,128)} %collective-permute-done.4.refs_0_, f32[24,6656]{1,0:T(8,128)} %shard_map.92.refs_1_, f32[24,6656]{1,0:T(8,128)} %collective-permute-done.6.refs_2_, f32[128,32768]{1,0:T(8,128)} %refs_6_.5, f32[128,32768]{1,0:T(8,128)} %refs_6_.5), custom_call_target="tpu_custom_call" | custom-call | tf_op jit(solution)/shard_map/pallas_call | solution.py:104
  206.2 7.7 %collective-permute-done.27 = f32[8,12,128]{2,1,0:T(8,128)S(1)} collective-permute-done((f32[8,12,128]{2,1,0:T(8,128)}, f32[8,12,128]{2,1,0:T(8,128)S(1)}, u32[]{:S(2)}, u32[]{:S(2)}) %collective-permute-start.27) | collective-permute-done | bytes 49184 | tf_op jit(solution)/shard_map/ppermute | solution.py:230
  214.0 1.6 collective-permute-start.29
  215.8 1.3 collective-permute-done.30
  218.6 3.0 %collective-permute-done.31 = f32[25,128]{1,0:T(8,128)S(1)} collective-permute-done((f32[25,128]{1,0:T(8,128)S(1)}, f32[25,128]{1,0:T(8,128)S(1)}, u32[]{:S(2)}, u32[]{:S(2)}) %collective-permute-start.31) | collective-permute-done | bytes 12832 | tf_op jit(solution)/shard_map/ppermute | solution.py:230
  221.6 4.0 %collective-permute-start.32 = (f32[25,256]{1,0:T(8,128)S(1)}, f32[25,256]{1,0:T(8,128)S(1)}, u32[]{:S(2)}, u32[]{:S(2)}) collective-permute-start(f32[25,256]{1,0:T(8,128)S(1)} %pad_maximum_fusion.5), channel_id=1, source_target_pairs={{0,8},{4,12},{8,0},{12,4},{16,24},{20,28},{24,16},{28,20},{1,9},{5... | collective-permute-start | bytes 76808 | tf_op jit(solution)/shard_map/ppermute | solution.py:230
  226.7 1.4 collective-permute-start.34
  228.1 2.9 %collective-permute-done.33 = f32[25,256]{1,0:T(8,128)S(1)} collective-permute-done((f32[25,256]{1,0:T(8,128)S(1)}, f32[25,256]{1,0:T(8,128)S(1)}, u32[]{:S(2)}, u32[]{:S(2)}) %collective-permute-start.33) | collective-permute-done | bytes 25632 | tf_op jit(solution)/shard_map/ppermute | solution.py:230
  231.0 1.4 collective-permute-done.34
  (139 shorter events, 15.9 us)
Async XLA Ops:
  1.3 14.1 %collective-permute-start.23 = (f32[24,4608]{1,0:T(8,128)S(1)}, f32[24,4608]{1,0:T(8,128)S(1)}, u32[]{:S(2)}, u32[]{:S(2)}) collective-permute-start(f32[24,4608]{1,0:T(8,128)S(1)} %pad_maximum_fusion.4.refs_0_), channel_id=1, source_target_pairs={{0,4},{4,0},{8,12},{12,8},{16,20},{20,16},{24,28},{28,24},{1,5},{5... | collective-permute-start | bytes 1327112 | tf_op jit(solution)/shard_map/ppermute | solution.py:230
  4.4 36.0 %collective-permute-start.7 = (f32[24,4608]{1,0:T(8,128)S(1)}, f32[24,4608]{1,0:T(8,128)S(1)}, u32[]{:S(2)}, u32[]{:S(2)}) collective-permute-start(f32[24,4608]{1,0:T(8,128)S(1)} %pad_maximum_fusion.4.refs_0_), channel_id=1, source_target_pairs={{0,8},{4,12},{8,0},{12,4},{16,24},{20,28},{24,16},{28,20},{1,9},{5... | collective-permute-start | bytes 1327112 | tf_op jit(solution)/shard_map/ppermute | solution.py:230
  6.1 32.7 %copy-start.2 = (f32[24,6656]{1,0:T(8,128)}, f32[24,6656]{1,0:T(8,128)S(1)}, u32[]{:S(2)}) copy-start(f32[24,6656]{1,0:T(8,128)S(1)} %pad_maximum_fusion.2.refs_0_) | copy-start | bytes 1916932
  6.1 36.8 %collective-permute-start.22 = (f32[24,6656]{1,0:T(8,128)S(1)}, f32[24,6656]{1,0:T(8,128)S(1)}, u32[]{:S(2)}, u32[]{:S(2)}) collective-permute-start(f32[24,6656]{1,0:T(8,128)S(1)} %pad_maximum_fusion.2.refs_0_), channel_id=1, source_target_pairs={{0,4},{4,0},{8,12},{12,8},{16,20},{20,16},{24,28},{28,24},{1,5},{5... | collective-permute-start | bytes 1916936 | tf_op jit(solution)/shard_map/ppermute | solution.py:230
  6.7 37.6 %collective-permute-start.2 = (f32[24,6656]{1,0:T(8,128)S(1)}, f32[24,6656]{1,0:T(8,128)}, u32[]{:S(2)}, u32[]{:S(2)}) collective-permute-start(f32[24,6656]{1,0:T(8,128)S(1)} %pad_maximum_fusion.2.refs_0_), channel_id=1, source_target_pairs={{0,8},{4,12},{8,0},{12,4},{16,24},{20,28},{24,16},{28,20},{1,9},{5... | collective-permute-start | bytes 1916936 | tf_op jit(solution)/shard_map/ppermute | solution.py:230
  6.8 32.0 %collective-permute-start.15 = (f32[24,5120]{1,0:T(8,128)S(1)}, f32[24,5120]{1,0:T(8,128)S(1)}, u32[]{:S(2)}, u32[]{:S(2)}) collective-permute-start(f32[24,5120]{1,0:T(8,128)S(1)} %pad_maximum_fusion.3), channel_id=1, source_target_pairs={{0,4},{4,0},{8,12},{12,8},{16,20},{20,16},{24,28},{28,24},{1,5},{5... | collective-permute-start | bytes 1474568 | tf_op jit(solution)/shard_map/ppermute | solution.py:230
  15.4 36.1 %copy-start.18 = (f32[24,4608]{1,0:T(8,128)}, f32[24,4608]{1,0:T(8,128)S(1)}, u32[]{:S(2)}) copy-start(f32[24,4608]{1,0:T(8,128)S(1)} %collective-permute-done.23.refs_1_) | copy-start | bytes 1327108
  15.4 26.8 %collective-permute-start.9 = (f32[24,4608]{1,0:T(8,128)S(1)}, f32[24,4608]{1,0:T(8,128)S(1)}, u32[]{:S(2)}, u32[]{:S(2)}) collective-permute-start(f32[24,4608]{1,0:T(8,128)S(1)} %pad_maximum_fusion.4.refs_0_), channel_id=1, source_target_pairs={{8,16},{12,20},{16,8},{20,12},{9,17},{13,21},{17,9},{21,13},{10,18... | collective-permute-start | bytes 1327112 | tf_op jit(solution)/shard_map/ppermute | solution.py:230
  38.8 14.3 %collective-permute-start = (f32[24,6656]{1,0:T(8,128)S(1)}, f32[24,6656]{1,0:T(8,128)}, u32[]{:S(2)}, u32[]{:S(2)}) collective-permute-start(f32[24,6656]{1,0:T(8,128)S(1)} %pad_maximum_fusion.2.refs_0_), channel_id=1, source_target_pairs={{8,16},{12,20},{16,8},{20,12},{9,17},{13,21},{17,9},{21,13},{10,18... | collective-permute-start | bytes 1916936 | tf_op jit(solution)/shard_map/ppermute | solution.py:230
  40.4 81.6 %copy-start.19 = (f32[24,4608]{1,0:T(8,128)}, f32[24,4608]{1,0:T(8,128)S(1)}, u32[]{:S(2)}) copy-start(f32[24,4608]{1,0:T(8,128)S(1)} %collective-permute-done.7.refs_2_) | copy-start | bytes 1327108
  40.4 22.7 %collective-permute-start.8 = (f32[24,4608]{1,0:T(8,128)S(1)}, f32[24,4608]{1,0:T(8,128)S(1)}, u32[]{:S(2)}, u32[]{:S(2)}) collective-permute-start(f32[24,4608]{1,0:T(8,128)S(1)} %collective-permute-done.7.refs_2_), channel_id=1, source_target_pairs={{0,4},{4,0},{8,12},{12,8},{16,20},{20,16},{24,28},{28,24},{1,5},{5... | collective-permute-start | bytes 1327112 | tf_op jit(solution)/shard_map/ppermute | solution.py:230
  42.2 79.8 %copy-start.14 = (f32[24,4608]{1,0:T(8,128)}, f32[24,4608]{1,0:T(8,128)S(1)}, u32[]{:S(2)}) copy-start(f32[24,4608]{1,0:T(8,128)S(1)} %collective-permute-done.9.b_ref) | copy-start | bytes 1327108
  42.2 24.0 %collective-permute-start.11 = (f32[24,4608]{1,0:T(8,128)S(1)}, f32[24,4608]{1,0:T(8,128)S(1)}, u32[]{:S(2)}, u32[]{:S(2)}) collective-permute-start(f32[24,4608]{1,0:T(8,128)S(1)} %collective-permute-done.7.refs_2_), channel_id=1, source_target_pairs={{8,16},{12,20},{16,8},{20,12},{9,17},{13,21},{17,9},{21,13},{10,18... | collective-permute-start | bytes 1327112 | tf_op jit(solution)/shard_map/ppermute | solution.py:230
  42.9 21.7 %collective-permute-start.10 = (f32[24,4608]{1,0:T(8,128)S(1)}, f32[24,4608]{1,0:T(8,128)S(1)}, u32[]{:S(2)}, u32[]{:S(2)}) collective-permute-start(f32[24,4608]{1,0:T(8,128)S(1)} %collective-permute-done.9.b_ref), channel_id=1, source_target_pairs={{8,0},{12,4},{16,24},{20,28},{9,1},{13,5},{17,25},{21,29},{10,2},{... | collective-permute-start | bytes 1327112 | tf_op jit(solution)/shard_map/ppermute | solution.py:230
  44.2 23.3 %collective-permute-start.24 = (f32[48,2304]{1,0:T(8,128)S(1)}, f32[48,2304]{1,0:T(8,128)S(1)}, u32[]{:S(2)}, u32[]{:S(2)}) collective-permute-start(f32[48,2304]{1,0:T(8,128)S(1)} %slice.180.refs_1_), channel_id=1, source_target_pairs={{0,8},{4,12},{24,16},{28,20},{1,9},{5,13},{25,17},{29,21},{2,10},{... | collective-permute-start | bytes 1327112 | tf_op jit(solution)/shard_map/ppermute | solution.py:230
  53.0 140.4 %collective-permute-start.26 = (f32[256,2304]{1,0:T(8,128)}, f32[256,2304]{1,0:T(8,128)}, u32[]{:S(2)}, u32[]{:S(2)}) collective-permute-start(f32[256,2304]{1,0:T(8,128)} %pad_maximum_fusion), channel_id=1, source_target_pairs={{0,8},{4,12},{24,16},{28,20},{1,9},{5,13},{25,17},{29,21},{2,10},{... | collective-permute-start | bytes 7077896 | tf_op jit(solution)/shard_map/ppermute | solution.py:230
  63.1 58.9 %copy-start.12 = (f32[24,4608]{1,0:T(8,128)}, f32[24,4608]{1,0:T(8,128)S(1)}, u32[]{:S(2)}) copy-start(f32[24,4608]{1,0:T(8,128)S(1)} %collective-permute-done.8.refs_0_) | copy-start | bytes 1327108
  63.1 8.4 %collective-permute-start.3 = (f32[24,6656]{1,0:T(8,128)}, f32[24,6656]{1,0:T(8,128)}, u32[]{:S(2)}, u32[]{:S(2)}) collective-permute-start(f32[24,6656]{1,0:T(8,128)} %collective-permute-done.2.refs_2_), channel_id=1, source_target_pairs={{8,16},{12,20},{16,8},{20,12},{9,17},{13,21},{17,9},{21,13},{10,18... | collective-permute-start | bytes 1916936 | tf_op jit(solution)/shard_map/ppermute | solution.py:230
  64.7 57.4 %copy-start.16 = (f32[24,4608]{1,0:T(8,128)}, f32[24,4608]{1,0:T(8,128)S(1)}, u32[]{:S(2)}) copy-start(f32[24,4608]{1,0:T(8,128)S(1)} %collective-permute-done.10.a_ref) | copy-start | bytes 1327108
  64.7 59.3 %collective-permute-start.21 = (f32[24,6656]{1,0:T(8,128)}, f32[24,6656]{1,0:T(8,128)}, u32[]{:S(2)}, u32[]{:S(2)}) collective-permute-start(f32[24,6656]{1,0:T(8,128)} %collective-permute-done.2.refs_2_), channel_id=1, source_target_pairs={{0,4},{4,0},{8,12},{12,8},{16,20},{20,16},{24,28},{28,24},{1,5},{5... | collective-permute-start | bytes 1916936 | tf_op jit(solution)/shard_map/ppermute | solution.py:230
  66.2 55.9 %copy-start.15 = (f32[24,4608]{1,0:T(8,128)}, f32[24,4608]{1,0:T(8,128)S(1)}, u32[]{:S(2)}) copy-start(f32[24,4608]{1,0:T(8,128)S(1)} %collective-permute-done.11.b_ref) | copy-start | bytes 1327108
  66.2 58.3 %collective-permute-start.1 = (f32[24,6656]{1,0:T(8,128)}, f32[24,6656]{1,0:T(8,128)}, u32[]{:S(2)}, u32[]{:S(2)}) collective-permute-start(f32[24,6656]{1,0:T(8,128)} %collective-permute-done.b_ref), channel_id=1, source_target_pairs={{8,0},{12,4},{16,24},{20,28},{9,1},{13,5},{17,25},{21,29},{10,2},{... | collective-permute-start | bytes 1916936 | tf_op jit(solution)/shard_map/ppermute | solution.py:230
  67.5 77.0 %copy-start.3 = (f32[48,2816]{1,0:T(8,128)}, f32[48,2816]{1,0:T(8,128)S(1)}, u32[]{:S(2)}) copy-start(f32[48,2816]{1,0:T(8,128)S(1)} %slice.157.refs_0_) | copy-start | bytes 1622020
  67.5 77.0 %copy-start.6 = (f32[48,2304]{1,0:T(8,128)}, f32[48,2304]{1,0:T(8,128)S(1)}, u32[]{:S(2)}) copy-start(f32[48,2304]{1,0:T(8,128)S(1)} %collective-permute-done.24.refs_2_) | copy-start | bytes 1327108
  67.6 53.7 %collective-permute-start.18 = (f32[48,2816]{1,0:T(8,128)S(1)}, f32[48,2816]{1,0:T(8,128)}, u32[]{:S(2)}, u32[]{:S(2)}) collective-permute-start(f32[48,2816]{1,0:T(8,128)S(1)} %slice.157.refs_0_), channel_id=1, source_target_pairs={{0,8},{4,12},{8,0},{12,4},{16,24},{20,28},{24,16},{28,20},{1,9},{5... | collective-permute-start | bytes 1622024 | tf_op jit(solution)/shard_map/ppermute | solution.py:230
  71.5 69.5 %collective-permute-start.5 = (f32[24,6656]{1,0:T(8,128)}, f32[24,6656]{1,0:T(8,128)}, u32[]{:S(2)}, u32[]{:S(2)}) collective-permute-start(f32[24,6656]{1,0:T(8,128)} %collective-permute-done.3.b_ref), channel_id=1, source_target_pairs={{8,0},{12,4},{16,24},{20,28},{9,1},{13,5},{17,25},{21,29},{10,2},{... | collective-permute-start | bytes 1916936 | tf_op jit(solution)/shard_map/ppermute | solution.py:230
  121.3 25.9 %collective-permute-start.16 = (f32[48,5120]{1,0:T(8,128)S(1)}, f32[48,5120]{1,0:T(8,128)S(1)}, u32[]{:S(2)}, u32[]{:S(2)}) collective-permute-start(f32[48,5120]{1,0:T(8,128)S(1)} %pad_maximum_fusion.1), channel_id=1, source_target_pairs={{8,16},{12,20},{16,8},{20,12},{9,17},{13,21},{17,9},{21,13},{10,18... | collective-permute-start | bytes 2949128 | tf_op jit(solution)/shard_map/ppermute | solution.py:230
  124.0 8.6 %collective-permute-start.12 = (f32[24,4608]{1,0:T(8,128)}, f32[24,4608]{1,0:T(8,128)S(1)}, u32[]{:S(2)}, u32[]{:S(2)}) collective-permute-start(f32[24,4608]{1,0:T(8,128)} %shard_map.94.refs_1_), channel_id=1, source_target_pairs={{0,4},{4,0},{8,12},{12,8},{16,20},{20,16},{24,28},{28,24},{1,5},{5... | collective-permute-start | bytes 1327112 | tf_op jit(solution)/shard_map/ppermute | solution.py:230
  124.5 13.1 %collective-permute-start.13 = (f32[24,4608]{1,0:T(8,128)}, f32[24,4608]{1,0:T(8,128)S(1)}, u32[]{:S(2)}, u32[]{:S(2)}) collective-permute-start(f32[24,4608]{1,0:T(8,128)} %copy-done.15), channel_id=1, source_target_pairs={{8,0},{12,4},{16,24},{20,28},{9,1},{13,5},{17,25},{21,29},{10,2},{... | collective-permute-start | bytes 1327112 | tf_op jit(solution)/shard_map/ppermute | solution.py:230
  132.5 16.2 %collective-permute-start.19 = (f32[48,2816]{1,0:T(8,128)}, f32[48,2816]{1,0:T(8,128)}, u32[]{:S(2)}, u32[]{:S(2)}) collective-permute-start(f32[48,2816]{1,0:T(8,128)} %collective-permute-done.18.refs_1_), channel_id=1, source_target_pairs={{8,16},{12,20},{16,8},{20,12},{9,17},{13,21},{17,9},{21,13},{10,18... | collective-permute-start | bytes 1622024 | tf_op jit(solution)/shard_map/ppermute | solution.py:230
  138.4 8.2 %collective-permute-start.25 = (f32[48,2304]{1,0:T(8,128)S(1)}, f32[48,2304]{1,0:T(8,128)S(1)}, u32[]{:S(2)}, u32[]{:S(2)}) collective-permute-start(f32[48,2304]{1,0:T(8,128)S(1)} %collective-permute-done.24.refs_2_), channel_id=1, source_target_pairs={{8,16},{12,20},{16,8},{20,12},{9,17},{13,21},{17,9},{21,13},{10,18... | collective-permute-start | bytes 1327112 | tf_op jit(solution)/shard_map/ppermute | solution.py:230
  141.0 13.4 %collective-permute-start.14 = (f32[24,4608]{1,0:T(8,128)}, f32[24,4608]{1,0:T(8,128)}, u32[]{:S(2)}, u32[]{:S(2)}) collective-permute-start(f32[24,4608]{1,0:T(8,128)} %shard_map.95.refs_3_), channel_id=1, source_target_pairs={{0,4},{4,0},{8,12},{12,8},{16,20},{20,16},{24,28},{28,24},{1,5},{5... | collective-permute-start | bytes 1327112 | tf_op jit(solution)/shard_map/ppermute | solution.py:230
  146.5 53.2 %collective-permute-start.4 = (f32[24,6656]{1,0:T(8,128)}, f32[24,6656]{1,0:T(8,128)}, u32[]{:S(2)}, u32[]{:S(2)}) collective-permute-start(f32[24,6656]{1,0:T(8,128)} %shard_map.91.refs_1_), channel_id=1, source_target_pairs={{0,4},{4,0},{8,12},{12,8},{16,20},{20,16},{24,28},{28,24},{1,5},{5... | collective-permute-start | bytes 1916936 | tf_op jit(solution)/shard_map/ppermute | solution.py:230
  147.3 52.5 %collective-permute-start.6 = (f32[24,6656]{1,0:T(8,128)}, f32[24,6656]{1,0:T(8,128)}, u32[]{:S(2)}, u32[]{:S(2)}) collective-permute-start(f32[24,6656]{1,0:T(8,128)} %shard_map.92.refs_1_), channel_id=1, source_target_pairs={{0,4},{4,0},{8,12},{12,8},{16,20},{20,16},{24,28},{28,24},{1,5},{5... | collective-permute-start | bytes 1916936 | tf_op jit(solution)/shard_map/ppermute | solution.py:230
  148.8 35.3 %collective-permute-start.17 = (f32[48,2816]{1,0:T(8,128)S(1)}, f32[48,2816]{1,0:T(8,128)S(1)}, u32[]{:S(2)}, u32[]{:S(2)}) collective-permute-start(f32[48,2816]{1,0:T(8,128)S(1)} %slice.156.refs_5_), channel_id=1, source_target_pairs={{8,0},{12,4},{16,24},{20,28},{9,1},{13,5},{17,25},{21,29},{10,2},{... | collective-permute-start | bytes 1622024 | tf_op jit(solution)/shard_map/ppermute | solution.py:230
  154.4 34.7 %collective-permute-start.20 = (f32[48,2816]{1,0:T(8,128)}, f32[48,2816]{1,0:T(8,128)S(1)}, u32[]{:S(2)}, u32[]{:S(2)}) collective-permute-start(f32[48,2816]{1,0:T(8,128)} %collective-permute-done.19.refs_3_), channel_id=1, source_target_pairs={{8,0},{12,4},{16,24},{20,28},{9,1},{13,5},{17,25},{21,29},{10,2},{... | collective-permute-start | bytes 1622024 | tf_op jit(solution)/shard_map/ppermute | solution.py:230
  198.3 17.5 %copy-start.33 = (s32[128]{0:T(128)S(1)}, s32[128]{0:T(128)}, u32[]{:S(2)}) copy-start(s32[128]{0:T(128)} %param.14) | copy-start | bytes 1540
  198.3 19.4 %copy-start.27 = (f32[128]{0:T(128)S(1)}, f32[128]{0:T(128)}, u32[]{:S(2)}) copy-start(f32[128]{0:T(128)} %param.13) | copy-start | bytes 1540
  198.3 19.4 %copy-start.28 = (f32[128]{0:T(128)S(1)}, f32[128]{0:T(128)}, u32[]{:S(2)}) copy-start(f32[128]{0:T(128)} %param.12) | copy-start | bytes 1540
  198.3 19.4 %copy-start.29 = (f32[128]{0:T(128)S(1)}, f32[128]{0:T(128)}, u32[]{:S(2)}) copy-start(f32[128]{0:T(128)} %param.11) | copy-start | bytes 1540
  198.3 15.5 %collective-permute-start.27 = (f32[8,12,128]{2,1,0:T(8,128)}, f32[8,12,128]{2,1,0:T(8,128)S(1)}, u32[]{:S(2)}, u32[]{:S(2)}) collective-permute-start(f32[8,12,128]{2,1,0:T(8,128)} %shard_map.102), channel_id=1, source_target_pairs={{8,0},{12,4},{16,24},{20,28},{9,1},{13,5},{17,25},{21,29},{10,2},{... | collective-permute-start | bytes 147464 | tf_op jit(solution)/shard_map/ppermute | solution.py:230
  213.9 3.3 %collective-permute-start.30 = (f32[24,128]{1,0:T(8,128)S(1)}, f32[24,128]{1,0:T(8,128)S(1)}, u32[]{:S(2)}, u32[]{:S(2)}) collective-permute-start(f32[24,128]{1,0:T(8,128)S(1)} %get-tuple-element.34), channel_id=1, source_target_pairs={{0,3},{1,2},{2,1},{3,0},{4,7},{5,6},{6,5},{7,4},{8,11},{9,10},{10,... | collective-permute-start | bytes 36872 | tf_op jit(solution)/shard_map/ppermute | solution.py:345
  214.0 3.8 %collective-permute-start.29 = (f32[24,128]{1,0:T(8,128)S(1)}, f32[24,128]{1,0:T(8,128)S(1)}, u32[]{:S(2)}, u32[]{:S(2)}) collective-permute-start(f32[24,128]{1,0:T(8,128)S(1)} %get-tuple-element.35), channel_id=1, source_target_pairs={{0,2},{1,3},{2,0},{3,1},{4,6},{5,7},{6,4},{7,5},{8,10},{9,11},{10,... | collective-permute-start | bytes 36872 | tf_op jit(solution)/shard_map/ppermute | solution.py:345
  215.5 2.2 collective-permute-start.28
  217.8 3.8 %collective-permute-start.31 = (f32[25,128]{1,0:T(8,128)S(1)}, f32[25,128]{1,0:T(8,128)S(1)}, u32[]{:S(2)}, u32[]{:S(2)}) collective-permute-start(f32[25,128]{1,0:T(8,128)S(1)} %get-tuple-element.36), channel_id=1, source_target_pairs={{0,4},{4,0},{8,12},{12,8},{16,20},{20,16},{24,28},{28,24},{1,5},{5... | collective-permute-start | bytes 38408 | tf_op jit(solution)/shard_map/ppermute | solution.py:230
  221.6 6.5 %collective-permute-start.32 = (f32[25,256]{1,0:T(8,128)S(1)}, f32[25,256]{1,0:T(8,128)S(1)}, u32[]{:S(2)}, u32[]{:S(2)}) collective-permute-start(f32[25,256]{1,0:T(8,128)S(1)} %pad_maximum_fusion.5), channel_id=1, source_target_pairs={{0,8},{4,12},{8,0},{12,4},{16,24},{20,28},{24,16},{28,20},{1,9},{5... | collective-permute-start | bytes 76808 | tf_op jit(solution)/shard_map/ppermute | solution.py:230
  225.6 5.4 %collective-permute-start.33 = (f32[25,256]{1,0:T(8,128)S(1)}, f32[25,256]{1,0:T(8,128)S(1)}, u32[]{:S(2)}, u32[]{:S(2)}) collective-permute-start(f32[25,256]{1,0:T(8,128)S(1)} %pad_maximum_fusion.5), channel_id=1, source_target_pairs={{0,16},{4,20},{8,24},{12,28},{16,0},{20,4},{24,8},{28,12},{1,17},{... | collective-permute-start | bytes 76808 | tf_op jit(solution)/shard_map/ppermute | solution.py:230
  226.7 5.7 %collective-permute-start.34 = (f32[25,256]{1,0:T(8,128)S(1)}, f32[25,256]{1,0:T(8,128)S(1)}, u32[]{:S(2)}, u32[]{:S(2)}) collective-permute-start(f32[25,256]{1,0:T(8,128)S(1)} %pad_maximum_fusion.5), channel_id=1, source_target_pairs={{0,24},{4,28},{8,16},{12,20},{16,8},{20,12},{24,0},{28,4},{1,25},{... | collective-permute-start | bytes 76808 | tf_op jit(solution)/shard_map/ppermute | solution.py:230
  (21 other events, 170.7 us)
